TPU v7x, 256 devices: a whole 4x4x8 slice. The times are simulated.
256 devices in a mesh: dp: 4 (over z_lo, core), ang: 4 (over y), rows: 16 (over z_hi, x).
Axes of the slice: x: 4, y: 4, z: 8 (z_hi: 4, z_lo: 2; z = z_hi * 2 + z_lo), core: 2. Of those that a mesh axis runs over, the one named last changes fastest.
Arguments:
- light_field: bfloat16 [4, 1, 8, 64, 64, 512], P('dp', None, 'ang', 'rows'), may hold values from -6 to 6
- spatial_weight: bfloat16 [3, 3, 64, 64], replicated, may hold values from -0.25 to 0.25
- epi_weight: bfloat16 [3, 3, 64, 64], replicated, may hold values from -0.25 to 0.25
- upsample_weight: bfloat16 [16, 64], replicated, may hold values from -0.75 to 0.75
- image_grad: bfloat16 [4, 1, 8, 256, 2048], P('dp', None, 'ang', 'rows'), may hold values from -0.005859375 to 0.005859375
Outputs:
- upscaled: bfloat16 [4, 1, 8, 256, 2048], P('dp', None, 'ang', 'rows')
- spatial_grad: float32 [3, 3, 64, 64], replicated
- epi_grad: float32 [3, 3, 64, 64], replicated
- upsample_grad: float32 [16, 64], replicated
All inputs are finite; a program needn't handle non-finite values.
Results may differ from a plain program's by a relative error of at most 0.0066.
Values may be sent and summed in bfloat16 or wider, within the bound.
No kernel may reach another device: no remote copies, remote signals or barrier semaphores. Data moves between devices by JAX's collectives and lax.ppermute only.
A program may use at most 64 MiB of HBM per device.

v0:
```python
import jax
import jax.numpy as jnp
from jax import lax
from jax.sharding import PartitionSpec as P

SCALE = 4
SUB = 16


def with_halo(cells, sides, width):
    for axis, dim in sides:
        count = lax.axis_size(axis)
        ends = count - 1
        head = lax.slice_in_dim(cells, 0, width, axis=dim)
        tail = lax.slice_in_dim(cells, cells.shape[dim] - width, cells.shape[dim], axis=dim)
        cells = jnp.concatenate(
            [
                lax.ppermute(tail, axis, [(i, (i + 1) % count) for i in range(ends)]),
                cells,
                lax.ppermute(head, axis, [((i + 1) % count, i) for i in range(ends)]),
            ],
            axis=dim,
        )
    return cells


def silu_slope(values):
    sigmoid_value = jax.nn.sigmoid(values)
    return sigmoid_value * (1.0 + values * (1.0 - sigmoid_value))


def spatial_conv(padded, weight, height, breadth):
    summed = jnp.zeros(padded.shape[:3] + (height, weight.shape[2], breadth), jnp.float32)
    for tap_row in range(3):
        for tap_col in range(3):
            summed = summed + jnp.einsum(
                "oc,buvhcw->buvhow",
                weight[tap_row, tap_col],
                padded[:, :, :, tap_row : tap_row + height, :, tap_col : tap_col + breadth],
                preferred_element_type=jnp.float32,
            )
    return summed


def epi_conv(padded, weight, views_all, breadth):
    summed = jnp.zeros(
        padded.shape[:2] + (views_all, padded.shape[3], weight.shape[2], breadth), jnp.float32
    )
    for tap_row in range(3):
        for tap_col in range(3):
            summed = summed + jnp.einsum(
                "oc,buvhcw->buvhow",
                weight[tap_row, tap_col],
                padded[:, :, tap_row : tap_row + views_all, :, :, tap_col : tap_col + breadth],
                preferred_element_type=jnp.float32,
            )
    return summed


def epi_back(padded, weight, views_all, breadth):
    summed = jnp.zeros(
        padded.shape[:2] + (views_all, padded.shape[3], weight.shape[3], breadth), jnp.float32
    )
    for tap_row in range(3):
        for tap_col in range(3):
            summed = summed + jnp.einsum(
                "oc,buvhow->buvhcw",
                weight[tap_row, tap_col],
                padded[
                    :,
                    :,
                    2 - tap_row : 2 - tap_row + views_all,
                    :,
                    :,
                    2 - tap_col : 2 - tap_col + breadth,
                ],
                preferred_element_type=jnp.float32,
            )
    return summed


def weight_grad(upstream, padded, along_dim, extent, breadth):
    rows_out = []
    for tap_row in range(3):
        row_list = []
        for tap_col in range(3):
            window = lax.slice_in_dim(padded, tap_row, tap_row + extent, axis=along_dim)
            window = lax.slice_in_dim(window, tap_col, tap_col + breadth, axis=5)
            row_list.append(
                jnp.einsum(
                    "buvhow,buvhcw->oc", upstream, window, preferred_element_type=jnp.float32
                )
            )
        rows_out.append(jnp.stack(row_list))
    return jnp.stack(rows_out)


def project_up(weight, features):
    return jnp.einsum(
        "sc,buvhcw->buvhsw", weight, features, preferred_element_type=jnp.float32
    ).astype(jnp.bfloat16)


def on_device(light_field, spatial_weight, epi_weight, upsample_weight, image_grad):
    batch_here, angular_rows, views_here, rows_here, channels, breadth = light_field.shape
    rimmed = with_halo(light_field, (("rows", 3),), 1)
    spatial_in = jnp.pad(rimmed, ((0, 0), (0, 0), (0, 0), (0, 0), (0, 0), (1, 1)))
    spatial_out = spatial_conv(spatial_in, spatial_weight, rows_here, breadth)
    first = (light_field.astype(jnp.float32) + jax.nn.silu(spatial_out)).astype(jnp.bfloat16)
    cotangent = image_grad.reshape(
        batch_here, angular_rows, views_here, rows_here, SCALE, breadth, SCALE
    )
    cotangent = cotangent.transpose(0, 1, 2, 3, 4, 6, 5).reshape(
        batch_here, angular_rows, views_here, rows_here, SUB, breadth
    )
    epi_block = lax.all_to_all(first, "ang", split_axis=3, concat_axis=2, tiled=True)
    views_block = epi_block.shape[2]
    padded_block = jnp.pad(epi_block, ((0, 0), (0, 0), (1, 1), (0, 0), (0, 0), (1, 1)))
    block_out = epi_conv(padded_block, epi_weight, views_block, breadth)
    block_second = (epi_block.astype(jnp.float32) + jax.nn.silu(block_out)).astype(jnp.bfloat16)
    views_all = block_second.shape[2]
    second_views = lax.all_to_all(block_second, "ang", split_axis=2, concat_axis=3, tiled=True)
    lifted_views = project_up(upsample_weight, second_views)
    up_grad = jnp.einsum(
        "buvhsw,buvhcw->sc", cotangent, second_views, preferred_element_type=jnp.float32
    )
    view_grad = jnp.einsum(
        "sc,buvhsw->buvhcw", upsample_weight, cotangent, preferred_element_type=jnp.float32
    ).astype(jnp.bfloat16)
    second_grad = lax.all_to_all(view_grad, "ang", split_axis=3, concat_axis=2, tiled=True)
    epi_slope = (second_grad.astype(jnp.float32) * silu_slope(block_out)).astype(jnp.bfloat16)
    epi_grad = weight_grad(epi_slope, padded_block, 2, views_all, breadth)
    slope_pad = jnp.pad(epi_slope, ((0, 0), (0, 0), (1, 1), (0, 0), (0, 0), (1, 1)))
    first_grad = (
        second_grad.astype(jnp.float32) + epi_back(slope_pad, epi_weight, views_all, breadth)
    ).astype(jnp.bfloat16)
    first_views = lax.all_to_all(first_grad, "ang", split_axis=2, concat_axis=3, tiled=True)
    upscaled = lifted_views.reshape(
        batch_here, angular_rows, views_here, rows_here, SCALE, SCALE, breadth
    )
    upscaled = upscaled.transpose(0, 1, 2, 3, 4, 6, 5).reshape(
        batch_here, angular_rows, views_here, rows_here * SCALE, breadth * SCALE
    )
    spatial_slope = (first_views.astype(jnp.float32) * silu_slope(spatial_out)).astype(jnp.bfloat16)
    spatial_grad = weight_grad(spatial_slope, spatial_in, 3, rows_here, breadth)
    spatial_grad, epi_grad, up_grad = lax.psum(
        (spatial_grad, epi_grad, up_grad), ("dp", "ang", "rows")
    )
    return (upscaled, spatial_grad, epi_grad, up_grad)


def solution(mesh):
    placed = (
        P("dp", None, "ang", "rows", None, None),
        P(),
        P(),
        P(),
        P("dp", None, "ang", "rows", None),
    )
    return jax.shard_map(
        on_device,
        mesh=mesh,
        in_specs=placed,
        out_specs=(P("dp", None, "ang", "rows", None), P(), P(), P()),
        check_vma=False,
    )
```

profile of v0, /device:TPU:64, one launch (start us, length us, event | category | flops | bytes accessed | tf_op | source)
XLA Modules:
  0.0 354.9 jit_solution(12636711815975530539)
XLA Ops:
  7.2 1.0 fusion.177
  8.2 3.4 collective-permute-start
  11.6 5.5 %collective-permute-start.1 = (bf16[1,1,2,1,64,512]{5,4,3,2,1,0:T(8,128)(2,1)S(1)}, bf16[1,1,2,1,64,512]{5,4,3,2,1,0:T(8,128)(2,1)S(1)}, u32[]{:S(2)}, u32[]{:S(2)}) collective-permute-start(bf16[1,1,2,1,64,512]{5,4,3,2,1,0:T(8,128)(2,1)S(1)} %get-tuple-element.17), channel_id=1, source_target_pairs={{1,0},{2,1},{3,2},{4,3},{5,4},{6,5},{7,6},{8,7},{9,8},{10,9},{11,1... | collective-permute-start | bytes 393224 | tf_op jit(solution)/shard_map/ppermute | solution.py:20
  17.0 10.8 %reshape.256 = bf16[1,1,2,4,4,512,4]{6,5,4,3,2,1,0:T(8,128)(2,1)} reshape(bf16[1,1,2,16,2048]{4,3,2,1,0:T(8,128)(2,1)} %param.9) | data formatting | bytes 262144 | tf_op jit(solution)/shard_map/reshape | solution.py:110
  27.8 3.7 %copy.156 = bf16[1,1,2,4,4,4,512]{6,3,5,4,2,1,0:T(4,128)(2,1)S(1)} copy(bf16[1,1,2,4,4,4,512]{5,6,4,3,2,1,0:T(8,128)(2,1)} %bitcast.452) | data formatting | bytes 262144 | tf_op jit(solution)/shard_map/transpose | solution.py:113
  31.5 0.3 fusion.7
  31.9 0.8 copy.158
  32.8 4.5 %all-to-all-start.2 = ((bf16[1,1,2,4,64,512]{5,4,2,1,0,3:T(8,128)(2,1)}), bf16[1,1,2,4,64,512]{5,4,2,1,0,3:T(8,128)(2,1)S(1)}, u32[]{:S(2)}, u32[]{:S(2)}) async-start(bf16[1,1,2,4,64,512]{5,4,2,1,0,3:T(8,128)(2,1)} %copy.158), calls=%async_computation.2 | async-start | bytes 1048576 | tf_op jit(solution)/shard_map/all_to_all | solution.py:130
  37.2 0.5 fusion.15
  38.4 0.4 convolution_add_fusion.13
  39.5 0.4 convolution_add_fusion.10
  40.1 0.4 fusion.112
  40.5 1.5 add_convert_fusion.1
  42.0 0.8 copy.152
  42.8 3.3 all-to-all-done.2
  46.1 0.8 copy-done.4
  46.9 3.6 %all-to-all-start = ((bf16[1,1,2,4,64,512]{5,4,2,1,0,3:T(8,128)(2,1)}), bf16[1,1,2,4,64,512]{5,4,2,1,0,3:T(8,128)(2,1)S(1)}, u32[]{:S(2)}, u32[]{:S(2)}) async-start(bf16[1,1,2,4,64,512]{5,4,2,1,0,3:T(8,128)(2,1)} %copy.152), calls=%async_computation | async-start | bytes 1048576 | tf_op jit(solution)/shard_map/all_to_all | solution.py:116
  50.6 2.3 slice_bitcast_fusion.5
  53.0 5.4 %all-to-all-done = bf16[1,1,2,4,64,512]{5,4,2,1,0,3:T(8,128)(2,1)S(1)} async-done(((bf16[1,1,2,4,64,512]{5,4,2,1,0,3:T(8,128)(2,1)}), bf16[1,1,2,4,64,512]{5,4,2,1,0,3:T(8,128)(2,1)S(1)}, u32[]{:S(2)}, u32[]{:S(2)}) %all-to-all-start) | async-done | bytes 524320 | tf_op jit(solution)/shard_map/all_to_all | solution.py:116
  58.4 0.4 fusion.81
  59.1 0.4 convolution_add_fusion.6
  59.4 0.4 convolution_add_fusion.5
  60.1 0.4 convolution_add_fusion.3
  60.5 0.4 convolution_add_fusion.2
  61.1 1.6 multiply_convert_fusion
  62.7 0.4 convolution_bitcast_fusion.5
  63.1 0.3 convolution_bitcast_fusion.4
  63.4 0.4 convolution_bitcast_fusion.3
  63.7 1.0 convolution_bitcast_fusion.8
  64.7 0.9 convolution_bitcast_fusion.7
  65.6 1.0 convolution_bitcast_fusion.6
  66.6 1.0 convolution_bitcast_fusion.2
  67.6 0.9 convolution_bitcast_fusion.1
  68.5 0.4 fusion.25
  68.9 0.4 convolution_add_fusion.22
  69.2 0.4 convolution_add_fusion.21
  69.6 0.4 convolution_add_fusion.20
  70.1 0.4 convolution_add_fusion.19
  70.5 0.4 convolution_add_fusion.18
  70.9 0.4 convolution_add_fusion.17
  71.3 0.4 convolution_add_fusion.16
  71.7 1.2 fusion.8
  73.0 3.6 %all-to-all-start.3 = ((bf16[1,1,8,1,64,512]{5,4,3,1,0,2:T(8,128)(2,1)}), bf16[1,1,8,1,64,512]{5,4,3,1,0,2:T(8,128)(2,1)S(1)}, u32[]{:S(2)}, u32[]{:S(2)}) async-start(bf16[1,1,8,1,64,512]{5,4,3,1,0,2:T(8,128)(2,1)} %fusion.8), calls=%async_computation.3 | async-start | bytes 1048576 | tf_op jit(solution)/shard_map/all_to_all | solution.py:137
  76.6 0.4 convolution_bitcast_fusion
  77.1 0.7 pad_maximum_fusion.3
  77.8 6.8 %all-to-all-done.3 = bf16[1,1,8,1,64,512]{5,4,3,1,0,2:T(8,128)(2,1)S(1)} async-done(((bf16[1,1,8,1,64,512]{5,4,3,1,0,2:T(8,128)(2,1)}), bf16[1,1,8,1,64,512]{5,4,3,1,0,2:T(8,128)(2,1)S(1)}, u32[]{:S(2)}, u32[]{:S(2)}) %all-to-all-start.3) | async-done | bytes 524320 | tf_op jit(solution)/shard_map/all_to_all | solution.py:137
  84.6 3.5 all-to-all-start.1
  88.4 1.7 fusion.65
  90.1 0.3 convolution_bitcast_fusion.16
  90.4 0.3 convolution_bitcast_fusion.13
  90.7 0.3 convolution_bitcast_fusion.10
  91.1 0.3 convolution_bitcast_fusion.14
  91.5 0.3 convolution_bitcast_fusion.12
  92.2 0.3 convolution_bitcast_fusion.11
  92.6 0.3 convolution_bitcast_fusion.9
  92.9 0.3 convolution_bitcast_fusion.15
  93.2 0.7 pad_maximum_fusion.2
  94.0 2.2 all-to-all-done.1
  96.4 3.3 copy.155
  99.7 9.7 %reshape.255 = bf16[1,1,2,16,2048]{4,3,2,1,0:T(8,128)(2,1)} reshape(bf16[1,1,2,4,4,512,4]{6,5,4,3,2,1,0:T(8,128)(2,1)} %bitcast.451) | data formatting | bytes 262144 | tf_op jit(solution)/shard_map/reshape | solution.py:141
  109.6 74.9 %psum.23 = f32[16,64]{1,0:T(8,128)} all-reduce(f32[16,64]{1,0:T(8,128)S(1)} %convolution_bitcast_fusion.18), channel_id=1, replica_groups=mesh['dp'=4,'ang'=4,'rows'=16] {'dp','ang','rows'}, use_global_device_ids=true, to_apply=%region_2.3 | all-reduce | flops 1024 | bytes 8192 | tf_op jit(solution)/shard_map/psum | solution.py:146
  184.6 160.1 %all-reduce.6.cloned.1.call-done = (f32[3,3,64,64]{3,2,1,0:T(8,128)}, f32[3,3,64,64]{3,2,1,0:T(8,128)}) async-done(((f32[3,3,64,64]{3,2,1,0:T(8,128)}, f32[3,3,64,64]{3,2,1,0:T(8,128)}), (f32[3,3,64,64]{3,2,1,0:T(8,128)}, f32[3,3,64,64]{3,2,1,0:T(8,128)})) %all-reduce.6.cloned.1.call-update) | async-done | bytes 294928 | tf_op jit(solution)/shard_map/psum | solution.py:146
  344.7 1.7 copy.279
  346.4 1.7 copy.280
  (59 shorter events, 4.1 us)
Async XLA Ops:
  7.2 24.4 %copy-start = (bf16[16,64]{1,0:T(8,128)(2,1)S(1)}, bf16[16,64]{1,0:T(8,128)(2,1)}, u32[]{:S(2)}) copy-start(bf16[16,64]{1,0:T(8,128)(2,1)} %param.8) | copy-start | bytes 6148
  8.2 29.0 %collective-permute-start = (bf16[1,1,2,1,64,512]{5,4,3,2,1,0:T(8,128)(2,1)S(1)}, bf16[1,1,2,1,64,512]{5,4,3,2,1,0:T(8,128)(2,1)S(1)}, u32[]{:S(2)}, u32[]{:S(2)}) collective-permute-start(bf16[1,1,2,1,64,512]{5,4,3,2,1,0:T(8,128)(2,1)S(1)} %get-tuple-element.16), channel_id=1, source_target_pairs={{0,1},{1,2},{2,3},{3,4},{4,5},{5,6},{6,7},{7,8},{8,9},{9,10},{10,1... | collective-permute-start | bytes 393224 | tf_op jit(solution)/shard_map/ppermute | solution.py:18
  11.6 25.6 %collective-permute-start.1 = (bf16[1,1,2,1,64,512]{5,4,3,2,1,0:T(8,128)(2,1)S(1)}, bf16[1,1,2,1,64,512]{5,4,3,2,1,0:T(8,128)(2,1)S(1)}, u32[]{:S(2)}, u32[]{:S(2)}) collective-permute-start(bf16[1,1,2,1,64,512]{5,4,3,2,1,0:T(8,128)(2,1)S(1)} %get-tuple-element.17), channel_id=1, source_target_pairs={{1,0},{2,1},{3,2},{4,3},{5,4},{6,5},{7,6},{8,7},{9,8},{10,9},{11,1... | collective-permute-start | bytes 393224 | tf_op jit(solution)/shard_map/ppermute | solution.py:20
  31.5 5.7 %copy-start.1 = (bf16[1,1,2,4,64,512]{5,4,3,2,1,0:T(8,128)(2,1)S(1)}, bf16[1,1,2,4,64,512]{5,4,3,2,1,0:T(8,128)(2,1)}, u32[]{:S(2)}) copy-start(bf16[1,1,2,4,64,512]{5,4,3,2,1,0:T(8,128)(2,1)} %param.5) | copy-start | bytes 1572868
  31.9 5.9 %copy-start.13 = (bf16[3,3,64,64]{3,2,1,0:T(8,128)(2,1)S(1)}, bf16[3,3,64,64]{3,2,1,0:T(8,128)(2,1)}, u32[]{:S(2)}) copy-start(bf16[3,3,64,64]{3,2,1,0:T(8,128)(2,1)} %param.6) | copy-start | bytes 221188
  32.8 13.4 %all-to-all-start.2 = ((bf16[1,1,2,4,64,512]{5,4,2,1,0,3:T(8,128)(2,1)}), bf16[1,1,2,4,64,512]{5,4,2,1,0,3:T(8,128)(2,1)S(1)}, u32[]{:S(2)}, u32[]{:S(2)}) async-start(bf16[1,1,2,4,64,512]{5,4,2,1,0,3:T(8,128)(2,1)} %copy.158), calls=%async_computation.2 | async-start | bytes 1048576 | tf_op jit(solution)/shard_map/all_to_all | solution.py:130
  38.1 0.8 copy-start.2
  46.1 0.8 copy-start.4
  46.9 11.5 %all-to-all-start = ((bf16[1,1,2,4,64,512]{5,4,2,1,0,3:T(8,128)(2,1)}), bf16[1,1,2,4,64,512]{5,4,2,1,0,3:T(8,128)(2,1)S(1)}, u32[]{:S(2)}, u32[]{:S(2)}) async-start(bf16[1,1,2,4,64,512]{5,4,2,1,0,3:T(8,128)(2,1)} %copy.152), calls=%async_computation | async-start | bytes 1048576 | tf_op jit(solution)/shard_map/all_to_all | solution.py:116
  50.6 2.3 copy-start.5
  50.6 7.9 %copy-start.6 = (bf16[3,3,64,64]{3,2,1,0:T(8,128)(2,1)S(1)}, bf16[3,3,64,64]{3,2,1,0:T(8,128)(2,1)}, u32[]{:S(2)}) copy-start(bf16[3,3,64,64]{3,2,1,0:T(8,128)(2,1)} %param.7) | copy-start | bytes 221188
  73.0 4.0 %copy-start.17 = (f32[1,64,64]{2,1,0:T(8,128)S(1)}, f32[1,64,64]{2,1,0:T(8,128)}, u32[]{:S(2)}) copy-start(f32[1,64,64]{2,1,0:T(8,128)} %convolution_bitcast_fusion.2) | copy-start | bytes 49156
  73.0 4.0 %copy-start.18 = (f32[1,64,64]{2,1,0:T(8,128)S(1)}, f32[1,64,64]{2,1,0:T(8,128)}, u32[]{:S(2)}) copy-start(f32[1,64,64]{2,1,0:T(8,128)} %convolution_bitcast_fusion.1) | copy-start | bytes 49156
  73.0 4.1 %copy-start.14 = (f32[1,64,64]{2,1,0:T(8,128)S(1)}, f32[1,64,64]{2,1,0:T(8,128)}, u32[]{:S(2)}) copy-start(f32[1,64,64]{2,1,0:T(8,128)} %convolution_bitcast_fusion.8) | copy-start | bytes 49156
  73.0 4.1 %copy-start.15 = (f32[1,64,64]{2,1,0:T(8,128)S(1)}, f32[1,64,64]{2,1,0:T(8,128)}, u32[]{:S(2)}) copy-start(f32[1,64,64]{2,1,0:T(8,128)} %convolution_bitcast_fusion.7) | copy-start | bytes 49156
  73.0 4.1 %copy-start.16 = (f32[1,64,64]{2,1,0:T(8,128)S(1)}, f32[1,64,64]{2,1,0:T(8,128)}, u32[]{:S(2)}) copy-start(f32[1,64,64]{2,1,0:T(8,128)} %convolution_bitcast_fusion.6) | copy-start | bytes 49156
  73.0 11.7 %all-to-all-start.3 = ((bf16[1,1,8,1,64,512]{5,4,3,1,0,2:T(8,128)(2,1)}), bf16[1,1,8,1,64,512]{5,4,3,1,0,2:T(8,128)(2,1)S(1)}, u32[]{:S(2)}, u32[]{:S(2)}) async-start(bf16[1,1,8,1,64,512]{5,4,3,1,0,2:T(8,128)(2,1)} %fusion.8), calls=%async_computation.3 | async-start | bytes 1048576 | tf_op jit(solution)/shard_map/all_to_all | solution.py:137
  77.1 13.0 %copy-start.3 = (bf16[2,4,64,512]{3,2,1,0:T(8,128)(2,1)S(1)}, bf16[2,4,64,512]{3,2,1,0:T(8,128)(2,1)}, u32[]{:S(2)}) copy-start(bf16[2,4,64,512]{3,2,1,0:T(8,128)(2,1)} %copy-done.2) | copy-start | bytes 1572868
  84.6 11.5 %all-to-all-start.1 = ((bf16[1,1,8,1,64,512]{5,4,3,1,0,2:T(8,128)(2,1)}), bf16[1,1,8,1,64,512]{5,4,3,1,0,2:T(8,128)(2,1)S(1)}, u32[]{:S(2)}, u32[]{:S(2)}) async-start(bf16[1,1,8,1,64,512]{5,4,3,1,0,2:T(8,128)(2,1)} %get-tuple-element.7), calls=%async_computation.1 | async-start | bytes 1048576 | tf_op jit(solution)/shard_map/all_to_all | solution.py:122
  88.1 256.6 %all-reduce.6.cloned.1.call-start = ((), (), s32[]{:S(2)}) async-start(), calls=%async_computation.4 | async-start | bytes 1179648 | tf_op jit(solution)/shard_map/psum | solution.py:146
  90.1 1.0 copy-start.12
  90.4 1.1 copy-start.11
  90.7 1.1 copy-start.10
  91.1 1.1 copy-start.9
  91.5 1.1 copy-start.8
  91.8 1.1 copy-start.7
Sparse Core Ops, SparseCore 0:
  95.1 249.5 all-reduce.5
where the time goes:
time: 359 us; the launch traced here: 355 us
  waiting for transfers between devices  178 us (50%)
  blocking collectives  74.9 us (21%)
  local copies, waits for them, and re-layouts  37.3 us (10%)
  starting transfers between devices  24.3 us (7%)
  matrix products  21.9 us (6%)
  between operations  14.6 us (4%)
  other arithmetic  3.92 us (1%)
    psum x1, waiting for transfers between devices, on_device(): lax.psum((spatial_grad, epi_grad, up_grad), ('dp', 'ang', 'rows'))  160 us
    psum x1, blocking collectives, on_device(): lax.psum((spatial_grad, epi_grad, up_grad), ('dp', 'ang', 'rows'))  74.9 us
    reshape x1, local copies, waits for them, and re-layouts, on_device(): image_grad.reshape(batch_here, angular_rows, views_here, rows_here, SCALE...  10.8 us
    reshape x1, local copies, waits for them, and re-layouts, on_device(): upscaled.transpose(0, 1, 2, 3, 4, 6, 5)  9.74 us
    dot_general x18, matrix products, weight_grad(): jnp.einsum('buvhow,buvhcw->oc', upstream, window, preferred_element_type=...  8.61 us
  transfers between devices with their start and end apart: 7, of which 5 were waited for; matrix products, arithmetic and copies ran while one was open for 12% of the time, Pallas kernels for 0%

commit v1 on v0

--- a/solution.py
+++ b/solution.py
@@ -101,6 +101,67 @@
     ).astype(jnp.bfloat16)
 
 
+def shift_pairs(kind, step):
+    if kind == "x":
+        return "rows", [(g * 4 + i, g * 4 + (i + step) % 4) for g in range(4) for i in range(4)]
+    if kind == "z":
+        return "rows", [(4 * i + g, 4 * ((i + step) % 4) + g) for g in range(4) for i in range(4)]
+    return kind, [(i, (i + step) % 4) for i in range(4)]
+
+
+def place_in(kind):
+    if kind == "x":
+        return lax.axis_index("rows") % 4
+    if kind == "z":
+        return lax.axis_index("rows") // 4
+    return lax.axis_index(kind)
+
+
+def shifted(value, kind, step):
+    axis, pairs = shift_pairs(kind, step)
+    return lax.ppermute(value, axis, pairs)
+
+
+def gather_sum(value, kind):
+    one, two, three = (shifted(value, kind, step) for step in (1, 2, 3))
+    return (value + two) + (one + three)
+
+
+def scatter_sum(value, kind):
+    place = place_in(kind)
+    mine = lax.dynamic_index_in_dim(value, place, 0, keepdims=False)
+    one, two, three = (
+        shifted(lax.dynamic_index_in_dim(value, (place + step) % 4, 0, keepdims=False), kind, step)
+        for step in (1, 2, 3)
+    )
+    return (mine + two) + (one + three)
+
+
+def gather_parts(value, kind):
+    place = place_in(kind)
+    around = jnp.stack([value] + [shifted(value, kind, step) for step in (1, 2, 3)])
+    return jnp.concatenate(
+        [lax.dynamic_index_in_dim(around, (place - part) % 4, 0) for part in range(4)], axis=0
+    )
+
+
+def sum_everywhere(parts):
+    flat = jnp.concatenate([part.reshape(-1, 128) for part in parts], axis=0)
+    rows = flat.shape[0]
+    share = -(-rows // 32) * 8
+    flat = jnp.pad(flat, ((0, 4 * share - rows), (0, 0))).reshape(4, share, 128)
+    mine = scatter_sum(flat, "dp")
+    for kind in ("x", "z", "ang"):
+        mine = gather_sum(mine, kind)
+    flat = gather_parts(mine, "dp").reshape(4 * share, 128)
+    results, start = [], 0
+    for part in parts:
+        count = part.size // 128
+        results.append(flat[start : start + count].reshape(part.shape))
+        start += count
+    return results
+
+
 def on_device(light_field, spatial_weight, epi_weight, upsample_weight, image_grad):
     batch_here, angular_rows, views_here, rows_here, channels, breadth = light_field.shape
     rimmed = with_halo(light_field, (("rows", 3),), 1)
@@ -143,9 +204,7 @@
     )
     spatial_slope = (first_views.astype(jnp.float32) * silu_slope(spatial_out)).astype(jnp.bfloat16)
     spatial_grad = weight_grad(spatial_slope, spatial_in, 3, rows_here, breadth)
-    spatial_grad, epi_grad, up_grad = lax.psum(
-        (spatial_grad, epi_grad, up_grad), ("dp", "ang", "rows")
-    )
+    spatial_grad, epi_grad, up_grad = sum_everywhere((spatial_grad, epi_grad, up_grad))
     return (upscaled, spatial_grad, epi_grad, up_grad)
 
 

time: 359 us -> 145 us (0.40)
  waiting for transfers between devices: 178 us -> 35.1 us
  blocking collectives: 74.9 us -> 0 us
  starting transfers between devices: 24.3 us -> 48.5 us
  between operations: 14.6 us -> 1.33 us
    psum x1 -> x0, waiting for transfers between devices: 160 us -> none  [on_device(): lax.psum((spatial_grad, epi_grad, up_grad), ('dp', 'ang', 'rows'))]
    psum x1 -> x0, blocking collectives: 74.9 us -> none  [on_device(): lax.psum((spatial_grad, epi_grad, up_grad), ('dp', 'ang', 'rows'))]
    ppermute x0 -> x15, starting transfers between devices: none -> 24.6 us  [shifted(): return lax.ppermute(value, axis, pairs)]
    ppermute x0 -> x15, waiting for transfers between devices: none -> 14.6 us  [shifted(): return lax.ppermute(value, axis, pairs)]
  transfers between devices with their start and end apart: 7 -> 21, of which waited for: 5 -> 13; matrix products, arithmetic and copies ran while one was open for 12% -> 28% of each run, Pallas kernels for 0% -> 0%
where the time goes in v1:
time: 145 us; the launch traced here: 142 us
  starting transfers between devices  48.5 us (33%)
  local copies, waits for them, and re-layouts  36.7 us (25%)
  waiting for transfers between devices  35.1 us (24%)
  matrix products  18.9 us (13%)
    ppermute x15, starting transfers between devices, shifted(): return lax.ppermute(value, axis, pairs)  24.6 us
    ppermute x15, waiting for transfers between devices, shifted(): return lax.ppermute(value, axis, pairs)  14.6 us
    reshape x1, local copies, waits for them, and re-layouts, on_device(): image_grad.reshape(batch_here, angular_rows, views_here, rows_here, SCALE...  10.8 us
    reshape x1, local copies, waits for them, and re-layouts, on_device(): upscaled.transpose(0, 1, 2, 3, 4, 6, 5)  9.74 us
    all_to_all x1, waiting for transfers between devices, on_device(): lax.all_to_all(first_grad, 'ang', split_axis=2, concat_axis=3, tiled=True)  7.48 us
    dot_general x18, matrix products, weight_grad(): jnp.einsum('buvhow,buvhcw->oc', upstream, window, preferred_element_type=...  5.47 us
    ppermute x1, starting transfers between devices, with_halo(): lax.ppermute(head, axis, [((i + 1) % count, i) for i in range(ends)])  5.45 us
    all_to_all x1, waiting for transfers between devices, on_device(): lax.all_to_all(first, 'ang', split_axis=3, concat_axis=2, tiled=True)  5.42 us
  transfers between devices with their start and end apart: 21, of which 13 were waited for; matrix products, arithmetic and copies ran while one was open for 28% of the time, Pallas kernels for 0%

profile of v1, /device:TPU:64, one launch (start us, length us, event | category | flops | bytes accessed | tf_op | source)
XLA Modules:
  0.0 141.9 jit_solution(14145591861268365492)
XLA Ops:
  0.6 1.0 fusion.178
  1.6 3.4 %collective-permute-start = (bf16[1,1,2,1,64,512]{5,4,3,2,1,0:T(8,128)(2,1)S(1)}, bf16[1,1,2,1,64,512]{5,4,3,2,1,0:T(8,128)(2,1)S(1)}, u32[]{:S(2)}, u32[]{:S(2)}) collective-permute-start(bf16[1,1,2,1,64,512]{5,4,3,2,1,0:T(8,128)(2,1)S(1)} %get-tuple-element.14), channel_id=1, source_target_pairs={{0,1},{1,2},{2,3},{3,4},{4,5},{5,6},{6,7},{7,8},{8,9},{9,10},{10,1... | collective-permute-start | bytes 393224 | tf_op jit(solution)/shard_map/ppermute | solution.py:18
  5.1 5.5 %collective-permute-start.1 = (bf16[1,1,2,1,64,512]{5,4,3,2,1,0:T(8,128)(2,1)S(1)}, bf16[1,1,2,1,64,512]{5,4,3,2,1,0:T(8,128)(2,1)S(1)}, u32[]{:S(2)}, u32[]{:S(2)}) collective-permute-start(bf16[1,1,2,1,64,512]{5,4,3,2,1,0:T(8,128)(2,1)S(1)} %get-tuple-element.15), channel_id=1, source_target_pairs={{1,0},{2,1},{3,2},{4,3},{5,4},{6,5},{7,6},{8,7},{9,8},{10,9},{11,1... | collective-permute-start | bytes 393224 | tf_op jit(solution)/shard_map/ppermute | solution.py:20
  10.5 10.8 %reshape.280 = bf16[1,1,2,4,4,512,4]{6,5,4,3,2,1,0:T(8,128)(2,1)} reshape(bf16[1,1,2,16,2048]{4,3,2,1,0:T(8,128)(2,1)} %param.9) | data formatting | bytes 262144 | tf_op jit(solution)/shard_map/reshape | solution.py:171
  21.3 3.7 %copy.156 = bf16[1,1,2,4,4,4,512]{6,3,5,4,2,1,0:T(4,128)(2,1)S(1)} copy(bf16[1,1,2,4,4,4,512]{5,6,4,3,2,1,0:T(8,128)(2,1)} %bitcast.472) | data formatting | bytes 262144 | tf_op jit(solution)/shard_map/transpose | solution.py:174
  25.4 0.8 copy.158
  26.2 4.5 %all-to-all-start.2 = ((bf16[1,1,2,4,64,512]{5,4,2,1,0,3:T(8,128)(2,1)}), bf16[1,1,2,4,64,512]{5,4,2,1,0,3:T(8,128)(2,1)S(1)}, u32[]{:S(2)}, u32[]{:S(2)}) async-start(bf16[1,1,2,4,64,512]{5,4,2,1,0,3:T(8,128)(2,1)} %copy.158), calls=%async_computation.2 | async-start | bytes 1048576 | tf_op jit(solution)/shard_map/all_to_all | solution.py:191
  30.7 0.5 fusion.15
  31.9 0.4 convolution_add_fusion.13
  32.9 0.4 convolution_add_fusion.10
  33.6 0.4 fusion.113
  34.0 1.5 %add_convert_fusion.1 = (bf16[1,1,2,4,64,512]{5,4,3,2,1,0:T(8,128)(2,1)S(1)}, f32[1,1,2,4,64,512]{5,4,3,2,1,0:T(8,128)}) fusion(bf16[1,1,2,4,64,512]{5,4,3,2,1,0:T(8,128)(2,1)S(1)} %copy-done.1, f32[2,4,512,64]{2,3,1,0:T(8,128)S(1)} %fusion.113, f32[2,4,512,64]{2,3,1,0:T(8,128)S(1)} %convolution_add_fusion.9, ...), kind=kOutput, calls=%fused_computation.80 | convolution fusion | flops 35913728 | bytes 4734976 | tf_op jit(solution)/shard_map/oc,buvhcw->buvhow/dot_general | solution.py:36
  35.4 0.9 copy.152
  36.3 3.3 %all-to-all-done.2 = bf16[1,1,2,4,64,512]{5,4,2,1,0,3:T(8,128)(2,1)S(1)} async-done(((bf16[1,1,2,4,64,512]{5,4,2,1,0,3:T(8,128)(2,1)}), bf16[1,1,2,4,64,512]{5,4,2,1,0,3:T(8,128)(2,1)S(1)}, u32[]{:S(2)}, u32[]{:S(2)}) %all-to-all-start.2) | async-done | bytes 524320 | tf_op jit(solution)/shard_map/all_to_all | solution.py:191
  39.6 0.8 copy-done.4
  40.4 3.6 %all-to-all-start = ((bf16[1,1,2,4,64,512]{5,4,2,1,0,3:T(8,128)(2,1)}), bf16[1,1,2,4,64,512]{5,4,2,1,0,3:T(8,128)(2,1)S(1)}, u32[]{:S(2)}, u32[]{:S(2)}) async-start(bf16[1,1,2,4,64,512]{5,4,2,1,0,3:T(8,128)(2,1)} %copy.152), calls=%async_computation | async-start | bytes 1048576 | tf_op jit(solution)/shard_map/all_to_all | solution.py:177
  44.1 2.3 %slice_bitcast_fusion.5 = (bf16[2,4,64,512]{3,2,1,0:T(8,128)(2,1)}, bf16[2,4,64,512]{3,2,1,0:T(8,128)(2,1)}, bf16[2,4,64,512]{3,2,1,0:T(8,128)(2,1)}, bf16[2,4,6...) fusion(bf16[1,1,2,6,64,514]{5,4,3,2,1,0:T(8,128)(2,1)S(1)} %fusion.15), kind=kLoop, calls=%fused_computation.110 | loop fusion | bytes 6291456 | tf_op jit(solution)/shard_map/reshape
  46.5 5.4 %all-to-all-done = bf16[1,1,2,4,64,512]{5,4,2,1,0,3:T(8,128)(2,1)S(1)} async-done(((bf16[1,1,2,4,64,512]{5,4,2,1,0,3:T(8,128)(2,1)}), bf16[1,1,2,4,64,512]{5,4,2,1,0,3:T(8,128)(2,1)S(1)}, u32[]{:S(2)}, u32[]{:S(2)}) %all-to-all-start) | async-done | bytes 524320 | tf_op jit(solution)/shard_map/all_to_all | solution.py:177
  51.9 0.4 fusion.81
  52.9 0.4 convolution_add_fusion.5
  53.6 0.4 convolution_add_fusion.3
  53.9 0.4 convolution_add_fusion.2
  54.6 1.6 %multiply_convert_fusion = (bf16[1,1,8,1,64,512]{5,4,2,3,1,0:T(8,128)(2,1)S(1)}, bf16[1,1,8,1,64,512]{5,4,3,1,0,2:T(8,128)(2,1)}) fusion(f32[1,1,8,1,64,512]{5,4,2,3,1,0:T(8,128)S(1)} %bitcast.475, bf16[1,1,8,1,64,512]{5,4,2,3,1,0:T(8,128)(2,1)S(1)} %bitcast.461, f32[8,512,64]{1,2,0:T(8,128)S(1)} %convolution_add_fusion.1, ...), kind=kOutput, calls=%fused_computation.77 | convolution fusion | flops 37224448 | bytes 4210688 | tf_op jit(solution)/shard_map/oc,buvhcw->buvhow/dot_general | solution.py:51
  56.2 0.4 fusion.25
  57.6 0.4 convolution_bitcast_fusion.8
  58.2 0.4 convolution_bitcast_fusion.6
  58.6 0.4 convolution_bitcast_fusion.2
  59.6 0.4 convolution_add_fusion.21
  60.0 0.4 convolution_add_fusion.20
  60.5 0.4 convolution_add_fusion.19
  60.9 0.4 convolution_add_fusion.18
  61.3 0.4 convolution_add_fusion.17
  61.7 0.4 convolution_add_fusion.16
  62.1 1.3 fusion.8
  63.4 3.5 %all-to-all-start.3 = ((bf16[1,1,8,1,64,512]{5,4,3,1,0,2:T(8,128)(2,1)}), bf16[1,1,8,1,64,512]{5,4,3,1,0,2:T(8,128)(2,1)S(1)}, u32[]{:S(2)}, u32[]{:S(2)}) async-start(bf16[1,1,8,1,64,512]{5,4,3,1,0,2:T(8,128)(2,1)} %fusion.8), calls=%async_computation.3 | async-start | bytes 1048576 | tf_op jit(solution)/shard_map/all_to_all | solution.py:198
  66.9 0.4 convolution_bitcast_fusion
  67.4 7.5 %all-to-all-done.3 = bf16[1,1,8,1,64,512]{5,4,3,1,0,2:T(8,128)(2,1)S(1)} async-done(((bf16[1,1,8,1,64,512]{5,4,3,1,0,2:T(8,128)(2,1)}), bf16[1,1,8,1,64,512]{5,4,3,1,0,2:T(8,128)(2,1)S(1)}, u32[]{:S(2)}, u32[]{:S(2)}) %all-to-all-start.3) | async-done | bytes 524320 | tf_op jit(solution)/shard_map/all_to_all | solution.py:198
  74.9 3.5 %all-to-all-start.1 = ((bf16[1,1,8,1,64,512]{5,4,3,1,0,2:T(8,128)(2,1)}), bf16[1,1,8,1,64,512]{5,4,3,1,0,2:T(8,128)(2,1)S(1)}, u32[]{:S(2)}, u32[]{:S(2)}) async-start(bf16[1,1,8,1,64,512]{5,4,3,1,0,2:T(8,128)(2,1)} %get-tuple-element.5), calls=%async_computation.1 | async-start | bytes 1048576 | tf_op jit(solution)/shard_map/all_to_all | solution.py:183
  78.4 0.4 fusion.65
  82.1 4.3 %all-to-all-done.1 = bf16[1,1,8,1,64,512]{5,4,3,1,0,2:T(8,128)(2,1)S(1)} async-done(((bf16[1,1,8,1,64,512]{5,4,3,1,0,2:T(8,128)(2,1)}), bf16[1,1,8,1,64,512]{5,4,3,1,0,2:T(8,128)(2,1)S(1)}, u32[]{:S(2)}, u32[]{:S(2)}) %all-to-all-start.1) | async-done | bytes 524320 | tf_op jit(solution)/shard_map/all_to_all | solution.py:183
  86.8 2.0 %collective-permute-start.2 = (f32[152,128]{1,0:T(8,128)S(1)}, f32[152,128]{1,0:T(8,128)S(1)}, u32[]{:S(2)}, u32[]{:S(2)}) collective-permute-start(f32[152,128]{1,0:T(8,128)S(1)} %get-tuple-element.24), channel_id=1, source_target_pairs={{0,128},{64,192},{128,0},{192,64},{1,129},{65,193},{129,1},{193,65... | collective-permute-start | bytes 233480 | tf_op jit(solution)/shard_map/ppermute | solution.py:122
  88.8 1.7 %collective-permute-start.4 = (f32[152,128]{1,0:T(8,128)S(1)}, f32[152,128]{1,0:T(8,128)S(1)}, u32[]{:S(2)}, u32[]{:S(2)}) collective-permute-start(f32[152,128]{1,0:T(8,128)S(1)} %get-tuple-element.22), channel_id=1, source_target_pairs={{0,192},{64,0},{128,64},{192,128},{1,193},{65,1},{129,65},{193,129... | collective-permute-start | bytes 233480 | tf_op jit(solution)/shard_map/ppermute | solution.py:122
  90.6 0.7 collective-permute-done.2
  91.3 1.6 %collective-permute-done.3 = f32[152,128]{1,0:T(8,128)S(1)} collective-permute-done((f32[152,128]{1,0:T(8,128)S(1)}, f32[152,128]{1,0:T(8,128)S(1)}, u32[]{:S(2)}, u32[]{:S(2)}) %collective-permute-start.3) | collective-permute-done | bytes 77856 | tf_op jit(solution)/shard_map/ppermute | solution.py:122
  93.1 2.5 %collective-permute-start.6 = (f32[152,128]{1,0:T(8,128)S(1)}, f32[152,128]{1,0:T(8,128)S(1)}, u32[]{:S(2)}, u32[]{:S(2)}) collective-permute-start(f32[152,128]{1,0:T(8,128)S(1)} %fusion.85), channel_id=1, source_target_pairs={{0,1},{1,2},{2,3},{3,0},{4,5},{5,6},{6,7},{7,4},{8,9},{9,10},{10,1... | collective-permute-start | bytes 233480 | tf_op jit(solution)/shard_map/ppermute | solution.py:122
  95.5 0.9 collective-permute-start.7
  96.4 3.4 %collective-permute-done.5 = f32[152,128]{1,0:T(8,128)S(1)} collective-permute-done((f32[152,128]{1,0:T(8,128)S(1)}, f32[152,128]{1,0:T(8,128)S(1)}, u32[]{:S(2)}, u32[]{:S(2)}) %collective-permute-start.5) | collective-permute-done | bytes 77856 | tf_op jit(solution)/shard_map/ppermute | solution.py:122
  99.8 0.9 collective-permute-done.6
  100.8 7.6 %collective-permute-start.8 = (f32[152,128]{1,0:T(8,128)S(1)}, f32[152,128]{1,0:T(8,128)S(1)}, u32[]{:S(2)}, u32[]{:S(2)}) collective-permute-start(f32[152,128]{1,0:T(8,128)S(1)} %add_add_fusion.2), channel_id=1, source_target_pairs={{0,8},{4,12},{8,0},{12,4},{1,9},{5,13},{9,1},{13,5},{2,10},{6,14},... | collective-permute-start | bytes 233480 | tf_op jit(solution)/shard_map/ppermute | solution.py:122
  108.4 1.5 %collective-permute-start.9 = (f32[152,128]{1,0:T(8,128)S(1)}, f32[152,128]{1,0:T(8,128)S(1)}, u32[]{:S(2)}, u32[]{:S(2)}) collective-permute-start(f32[152,128]{1,0:T(8,128)S(1)} %add_add_fusion.2), channel_id=1, source_target_pairs={{0,4},{4,8},{8,12},{12,0},{1,5},{5,9},{9,13},{13,1},{2,6},{6,10},{... | collective-permute-start | bytes 233480 | tf_op jit(solution)/shard_map/ppermute | solution.py:122
  110.1 2.3 %collective-permute-done.8 = f32[152,128]{1,0:T(8,128)S(1)} collective-permute-done((f32[152,128]{1,0:T(8,128)S(1)}, f32[152,128]{1,0:T(8,128)S(1)}, u32[]{:S(2)}, u32[]{:S(2)}) %collective-permute-start.8) | collective-permute-done | bytes 77856 | tf_op jit(solution)/shard_map/ppermute | solution.py:122
  112.5 2.4 %collective-permute-done.9 = f32[152,128]{1,0:T(8,128)S(1)} collective-permute-done((f32[152,128]{1,0:T(8,128)S(1)}, f32[152,128]{1,0:T(8,128)S(1)}, u32[]{:S(2)}, u32[]{:S(2)}) %collective-permute-start.9) | collective-permute-done | bytes 77856 | tf_op jit(solution)/shard_map/ppermute | solution.py:122
  114.9 0.6 collective-permute-start.11
  115.6 1.5 %collective-permute-start.12 = (f32[152,128]{1,0:T(8,128)S(1)}, f32[152,128]{1,0:T(8,128)S(1)}, u32[]{:S(2)}, u32[]{:S(2)}) collective-permute-start(f32[152,128]{1,0:T(8,128)S(1)} %add_add_fusion.1), channel_id=1, source_target_pairs={{0,16},{16,32},{32,48},{48,0},{1,17},{17,33},{33,49},{49,1},{2,18}... | collective-permute-start | bytes 233480 | tf_op jit(solution)/shard_map/ppermute | solution.py:122
  117.0 1.8 %collective-permute-start.13 = (f32[152,128]{1,0:T(8,128)S(1)}, f32[152,128]{1,0:T(8,128)S(1)}, u32[]{:S(2)}, u32[]{:S(2)}) collective-permute-start(f32[152,128]{1,0:T(8,128)S(1)} %add_add_fusion.1), channel_id=1, source_target_pairs={{0,48},{16,0},{32,16},{48,32},{1,49},{17,1},{33,17},{49,33},{2,50}... | collective-permute-start | bytes 233480 | tf_op jit(solution)/shard_map/ppermute | solution.py:122
  118.8 2.2 %collective-permute-done.11 = f32[152,128]{1,0:T(8,128)S(1)} collective-permute-done((f32[152,128]{1,0:T(8,128)S(1)}, f32[152,128]{1,0:T(8,128)S(1)}, u32[]{:S(2)}, u32[]{:S(2)}) %collective-permute-start.11) | collective-permute-done | bytes 77856 | tf_op jit(solution)/shard_map/ppermute | solution.py:122
  121.0 0.8 collective-permute-done.12
  121.9 2.9 %collective-permute-start.15 = (f32[152,128]{1,0:T(8,128)S(1)}, f32[152,128]{1,0:T(8,128)S(1)}, u32[]{:S(2)}, u32[]{:S(2)}) collective-permute-start(f32[152,128]{1,0:T(8,128)S(1)} %add_add_fusion), channel_id=1, source_target_pairs={{0,128},{64,192},{128,0},{192,64},{1,129},{65,193},{129,1},{193,65... | collective-permute-start | bytes 233480 | tf_op jit(solution)/shard_map/ppermute | solution.py:122
  124.8 1.4 collective-permute-start.16
  126.4 3.3 %copy.155 = bf16[1,1,2,4,4,4,512]{5,6,4,3,2,1,0:T(8,128)(2,1)} copy(bf16[1,1,2,4,4,4,512]{6,5,4,3,2,1,0:T(4,128)(2,1)S(1)} %reshape.278) | data formatting | bytes 262144 | tf_op jit(solution)/shard_map/reshape | solution.py:199
  129.7 9.7 %reshape.279 = bf16[1,1,2,16,2048]{4,3,2,1,0:T(8,128)(2,1)} reshape(bf16[1,1,2,4,4,512,4]{6,5,4,3,2,1,0:T(8,128)(2,1)} %bitcast.471) | data formatting | bytes 262144 | tf_op jit(solution)/shard_map/reshape | solution.py:202
  139.6 0.8 reshape.297
  140.4 0.8 reshape.298
  141.2 0.7 reshape.299
  (96 shorter events, 9.8 us)
Async XLA Ops:
  0.6 24.4 %copy-start = (bf16[16,64]{1,0:T(8,128)(2,1)S(1)}, bf16[16,64]{1,0:T(8,128)(2,1)}, u32[]{:S(2)}) copy-start(bf16[16,64]{1,0:T(8,128)(2,1)} %param.8) | copy-start | bytes 6148
  1.6 29.0 %collective-permute-start = (bf16[1,1,2,1,64,512]{5,4,3,2,1,0:T(8,128)(2,1)S(1)}, bf16[1,1,2,1,64,512]{5,4,3,2,1,0:T(8,128)(2,1)S(1)}, u32[]{:S(2)}, u32[]{:S(2)}) collective-permute-start(bf16[1,1,2,1,64,512]{5,4,3,2,1,0:T(8,128)(2,1)S(1)} %get-tuple-element.14), channel_id=1, source_target_pairs={{0,1},{1,2},{2,3},{3,4},{4,5},{5,6},{6,7},{7,8},{8,9},{9,10},{10,1... | collective-permute-start | bytes 393224 | tf_op jit(solution)/shard_map/ppermute | solution.py:18
  5.1 25.6 %collective-permute-start.1 = (bf16[1,1,2,1,64,512]{5,4,3,2,1,0:T(8,128)(2,1)S(1)}, bf16[1,1,2,1,64,512]{5,4,3,2,1,0:T(8,128)(2,1)S(1)}, u32[]{:S(2)}, u32[]{:S(2)}) collective-permute-start(bf16[1,1,2,1,64,512]{5,4,3,2,1,0:T(8,128)(2,1)S(1)} %get-tuple-element.15), channel_id=1, source_target_pairs={{1,0},{2,1},{3,2},{4,3},{5,4},{6,5},{7,6},{8,7},{9,8},{10,9},{11,1... | collective-permute-start | bytes 393224 | tf_op jit(solution)/shard_map/ppermute | solution.py:20
  25.0 5.7 %copy-start.1 = (bf16[1,1,2,4,64,512]{5,4,3,2,1,0:T(8,128)(2,1)S(1)}, bf16[1,1,2,4,64,512]{5,4,3,2,1,0:T(8,128)(2,1)}, u32[]{:S(2)}) copy-start(bf16[1,1,2,4,64,512]{5,4,3,2,1,0:T(8,128)(2,1)} %param.5) | copy-start | bytes 1572868
  25.4 5.9 %copy-start.16 = (bf16[3,3,64,64]{3,2,1,0:T(8,128)(2,1)S(1)}, bf16[3,3,64,64]{3,2,1,0:T(8,128)(2,1)}, u32[]{:S(2)}) copy-start(bf16[3,3,64,64]{3,2,1,0:T(8,128)(2,1)} %param.6) | copy-start | bytes 221188
  26.2 13.4 %all-to-all-start.2 = ((bf16[1,1,2,4,64,512]{5,4,2,1,0,3:T(8,128)(2,1)}), bf16[1,1,2,4,64,512]{5,4,2,1,0,3:T(8,128)(2,1)S(1)}, u32[]{:S(2)}, u32[]{:S(2)}) async-start(bf16[1,1,2,4,64,512]{5,4,2,1,0,3:T(8,128)(2,1)} %copy.158), calls=%async_computation.2 | async-start | bytes 1048576 | tf_op jit(solution)/shard_map/all_to_all | solution.py:191
  31.6 0.8 copy-start.2
  31.6 2.4 %copy-start.8 = (bf16[2,4,64,512]{3,2,1,0:T(8,128)(2,1)}, bf16[2,4,64,512]{3,2,1,0:T(8,128)(2,1)S(1)}, u32[]{:S(2)}) copy-start(bf16[2,4,64,512]{3,2,1,0:T(8,128)(2,1)S(1)} %get-tuple-element.12) | copy-start | bytes 1572868
  39.6 0.8 copy-start.4
  40.4 11.5 %all-to-all-start = ((bf16[1,1,2,4,64,512]{5,4,2,1,0,3:T(8,128)(2,1)}), bf16[1,1,2,4,64,512]{5,4,2,1,0,3:T(8,128)(2,1)S(1)}, u32[]{:S(2)}, u32[]{:S(2)}) async-start(bf16[1,1,2,4,64,512]{5,4,2,1,0,3:T(8,128)(2,1)} %copy.152), calls=%async_computation | async-start | bytes 1048576 | tf_op jit(solution)/shard_map/all_to_all | solution.py:177
  44.0 2.3 %copy-start.5 = (bf16[1,1,2,4,64,512]{5,4,2,1,0,3:T(8,128)(2,1)S(1)}, bf16[1,1,2,4,64,512]{5,4,2,1,0,3:T(8,128)(2,1)}, u32[]{:S(2)}) copy-start(bf16[1,1,2,4,64,512]{5,4,2,1,0,3:T(8,128)(2,1)} %copy-done.4) | copy-start | bytes 1572868
  44.0 7.9 %copy-start.7 = (bf16[3,3,64,64]{3,2,1,0:T(8,128)(2,1)S(1)}, bf16[3,3,64,64]{3,2,1,0:T(8,128)(2,1)}, u32[]{:S(2)}) copy-start(bf16[3,3,64,64]{3,2,1,0:T(8,128)(2,1)} %param.7) | copy-start | bytes 221188
  63.4 11.5 %all-to-all-start.3 = ((bf16[1,1,8,1,64,512]{5,4,3,1,0,2:T(8,128)(2,1)}), bf16[1,1,8,1,64,512]{5,4,3,1,0,2:T(8,128)(2,1)S(1)}, u32[]{:S(2)}, u32[]{:S(2)}) async-start(bf16[1,1,8,1,64,512]{5,4,3,1,0,2:T(8,128)(2,1)} %fusion.8), calls=%async_computation.3 | async-start | bytes 1048576 | tf_op jit(solution)/shard_map/all_to_all | solution.py:198
  67.2 11.2 %copy-start.6 = (f32[1,1,2,4,64,512]{5,4,3,2,1,0:T(8,128)S(1)}, f32[1,1,2,4,64,512]{5,4,3,2,1,0:T(8,128)}, u32[]{:S(2)}) copy-start(f32[1,1,2,4,64,512]{5,4,3,2,1,0:T(8,128)} %get-tuple-element.26) | copy-start | bytes 3145732
  67.3 11.5 %copy-start.3 = (bf16[2,4,64,512]{3,2,1,0:T(8,128)(2,1)S(1)}, bf16[2,4,64,512]{3,2,1,0:T(8,128)(2,1)}, u32[]{:S(2)}) copy-start(bf16[2,4,64,512]{3,2,1,0:T(8,128)(2,1)} %copy-done.2) | copy-start | bytes 1572868
  74.9 11.5 %all-to-all-start.1 = ((bf16[1,1,8,1,64,512]{5,4,3,1,0,2:T(8,128)(2,1)}), bf16[1,1,8,1,64,512]{5,4,3,1,0,2:T(8,128)(2,1)S(1)}, u32[]{:S(2)}, u32[]{:S(2)}) async-start(bf16[1,1,8,1,64,512]{5,4,3,1,0,2:T(8,128)(2,1)} %get-tuple-element.5), calls=%async_computation.1 | async-start | bytes 1048576 | tf_op jit(solution)/shard_map/all_to_all | solution.py:183
  78.4 1.0 copy-start.9
  78.8 1.1 copy-start.15
  79.1 1.1 copy-start.14
  79.4 1.1 copy-start.13
  79.9 1.1 copy-start.12
  80.2 1.1 copy-start.11
  80.6 1.1 copy-start.10
  86.8 4.5 %collective-permute-start.2 = (f32[152,128]{1,0:T(8,128)S(1)}, f32[152,128]{1,0:T(8,128)S(1)}, u32[]{:S(2)}, u32[]{:S(2)}) collective-permute-start(f32[152,128]{1,0:T(8,128)S(1)} %get-tuple-element.24), channel_id=1, source_target_pairs={{0,128},{64,192},{128,0},{192,64},{1,129},{65,193},{129,1},{193,65... | collective-permute-start | bytes 233480 | tf_op jit(solution)/shard_map/ppermute | solution.py:122
  88.8 4.1 %collective-permute-start.3 = (f32[152,128]{1,0:T(8,128)S(1)}, f32[152,128]{1,0:T(8,128)S(1)}, u32[]{:S(2)}, u32[]{:S(2)}) collective-permute-start(f32[152,128]{1,0:T(8,128)S(1)} %get-tuple-element.23), channel_id=1, source_target_pairs={{0,64},{64,128},{128,192},{192,0},{1,65},{65,129},{129,193},{193,1... | collective-permute-start | bytes 233480 | tf_op jit(solution)/shard_map/ppermute | solution.py:122
  88.8 4.1 %collective-permute-start.4 = (f32[152,128]{1,0:T(8,128)S(1)}, f32[152,128]{1,0:T(8,128)S(1)}, u32[]{:S(2)}, u32[]{:S(2)}) collective-permute-start(f32[152,128]{1,0:T(8,128)S(1)} %get-tuple-element.22), channel_id=1, source_target_pairs={{0,192},{64,0},{128,64},{192,128},{1,193},{65,1},{129,65},{193,129... | collective-permute-start | bytes 233480 | tf_op jit(solution)/shard_map/ppermute | solution.py:122
  92.9 6.8 %collective-permute-start.5 = (f32[152,128]{1,0:T(8,128)S(1)}, f32[152,128]{1,0:T(8,128)S(1)}, u32[]{:S(2)}, u32[]{:S(2)}) collective-permute-start(f32[152,128]{1,0:T(8,128)S(1)} %fusion.85), channel_id=1, source_target_pairs={{0,2},{1,3},{2,0},{3,1},{4,6},{5,7},{6,4},{7,5},{8,10},{9,11},{10,... | collective-permute-start | bytes 233480 | tf_op jit(solution)/shard_map/ppermute | solution.py:122
  93.1 7.6 %collective-permute-start.6 = (f32[152,128]{1,0:T(8,128)S(1)}, f32[152,128]{1,0:T(8,128)S(1)}, u32[]{:S(2)}, u32[]{:S(2)}) collective-permute-start(f32[152,128]{1,0:T(8,128)S(1)} %fusion.85), channel_id=1, source_target_pairs={{0,1},{1,2},{2,3},{3,0},{4,5},{5,6},{6,7},{7,4},{8,9},{9,10},{10,1... | collective-permute-start | bytes 233480 | tf_op jit(solution)/shard_map/ppermute | solution.py:122
  95.5 5.1 %collective-permute-start.7 = (f32[152,128]{1,0:T(8,128)S(1)}, f32[152,128]{1,0:T(8,128)S(1)}, u32[]{:S(2)}, u32[]{:S(2)}) collective-permute-start(f32[152,128]{1,0:T(8,128)S(1)} %fusion.85), channel_id=1, source_target_pairs={{0,3},{1,0},{2,1},{3,2},{4,7},{5,4},{6,5},{7,6},{8,11},{9,8},{10,9... | collective-permute-start | bytes 233480 | tf_op jit(solution)/shard_map/ppermute | solution.py:122
  100.7 9.5 %collective-permute-start.10 = (f32[152,128]{1,0:T(8,128)S(1)}, f32[152,128]{1,0:T(8,128)S(1)}, u32[]{:S(2)}, u32[]{:S(2)}) collective-permute-start(f32[152,128]{1,0:T(8,128)S(1)} %add_add_fusion.2), channel_id=1, source_target_pairs={{0,12},{4,0},{8,4},{12,8},{1,13},{5,1},{9,5},{13,9},{2,14},{6,2},{... | collective-permute-start | bytes 233480 | tf_op jit(solution)/shard_map/ppermute | solution.py:122
  100.8 11.7 %collective-permute-start.8 = (f32[152,128]{1,0:T(8,128)S(1)}, f32[152,128]{1,0:T(8,128)S(1)}, u32[]{:S(2)}, u32[]{:S(2)}) collective-permute-start(f32[152,128]{1,0:T(8,128)S(1)} %add_add_fusion.2), channel_id=1, source_target_pairs={{0,8},{4,12},{8,0},{12,4},{1,9},{5,13},{9,1},{13,5},{2,10},{6,14},... | collective-permute-start | bytes 233480 | tf_op jit(solution)/shard_map/ppermute | solution.py:122
  108.4 6.5 %collective-permute-start.9 = (f32[152,128]{1,0:T(8,128)S(1)}, f32[152,128]{1,0:T(8,128)S(1)}, u32[]{:S(2)}, u32[]{:S(2)}) collective-permute-start(f32[152,128]{1,0:T(8,128)S(1)} %add_add_fusion.2), channel_id=1, source_target_pairs={{0,4},{4,8},{8,12},{12,0},{1,5},{5,9},{9,13},{13,1},{2,6},{6,10},{... | collective-permute-start | bytes 233480 | tf_op jit(solution)/shard_map/ppermute | solution.py:122
  114.9 6.0 %collective-permute-start.11 = (f32[152,128]{1,0:T(8,128)S(1)}, f32[152,128]{1,0:T(8,128)S(1)}, u32[]{:S(2)}, u32[]{:S(2)}) collective-permute-start(f32[152,128]{1,0:T(8,128)S(1)} %add_add_fusion.1), channel_id=1, source_target_pairs={{0,32},{16,48},{32,0},{48,16},{1,33},{17,49},{33,1},{49,17},{2,34}... | collective-permute-start | bytes 233480 | tf_op jit(solution)/shard_map/ppermute | solution.py:122
  115.6 6.2 %collective-permute-start.12 = (f32[152,128]{1,0:T(8,128)S(1)}, f32[152,128]{1,0:T(8,128)S(1)}, u32[]{:S(2)}, u32[]{:S(2)}) collective-permute-start(f32[152,128]{1,0:T(8,128)S(1)} %add_add_fusion.1), channel_id=1, source_target_pairs={{0,16},{16,32},{32,48},{48,0},{1,17},{17,33},{33,49},{49,1},{2,18}... | collective-permute-start | bytes 233480 | tf_op jit(solution)/shard_map/ppermute | solution.py:122
  117.0 4.7 %collective-permute-start.13 = (f32[152,128]{1,0:T(8,128)S(1)}, f32[152,128]{1,0:T(8,128)S(1)}, u32[]{:S(2)}, u32[]{:S(2)}) collective-permute-start(f32[152,128]{1,0:T(8,128)S(1)} %add_add_fusion.1), channel_id=1, source_target_pairs={{0,48},{16,0},{32,16},{48,32},{1,49},{17,1},{33,17},{49,33},{2,50}... | collective-permute-start | bytes 233480 | tf_op jit(solution)/shard_map/ppermute | solution.py:122
  121.8 17.6 %collective-permute-start.14 = (f32[152,128]{1,0:T(8,128)S(1)}, f32[152,128]{1,0:T(8,128)S(1)}, u32[]{:S(2)}, u32[]{:S(2)}) collective-permute-start(f32[152,128]{1,0:T(8,128)S(1)} %add_add_fusion), channel_id=1, source_target_pairs={{0,64},{64,128},{128,192},{192,0},{1,65},{65,129},{129,193},{193,1... | collective-permute-start | bytes 233480 | tf_op jit(solution)/shard_map/ppermute | solution.py:122
  121.9 17.6 %collective-permute-start.15 = (f32[152,128]{1,0:T(8,128)S(1)}, f32[152,128]{1,0:T(8,128)S(1)}, u32[]{:S(2)}, u32[]{:S(2)}) collective-permute-start(f32[152,128]{1,0:T(8,128)S(1)} %add_add_fusion), channel_id=1, source_target_pairs={{0,128},{64,192},{128,0},{192,64},{1,129},{65,193},{129,1},{193,65... | collective-permute-start | bytes 233480 | tf_op jit(solution)/shard_map/ppermute | solution.py:122
  124.8 14.6 %collective-permute-start.16 = (f32[152,128]{1,0:T(8,128)S(1)}, f32[152,128]{1,0:T(8,128)S(1)}, u32[]{:S(2)}, u32[]{:S(2)}) collective-permute-start(f32[152,128]{1,0:T(8,128)S(1)} %add_add_fusion), channel_id=1, source_target_pairs={{0,192},{64,0},{128,64},{192,128},{1,193},{65,1},{129,65},{193,129... | collective-permute-start | bytes 233480 | tf_op jit(solution)/shard_map/ppermute | solution.py:122

commit v2 on v1

v2 whole, which is shorter than its diff:
```python
import jax
import jax.numpy as jnp
from jax import lax
from jax.experimental import pallas as pl
from jax.experimental.pallas import tpu as pltpu
from jax.sharding import PartitionSpec as P

F32 = jnp.float32
BF16 = jnp.bfloat16
VMEM_LIMIT = 56 * 1024 * 1024


def mesh_pairs(kind, step):
    if kind == "x":
        return "rows", [(g * 4 + i, g * 4 + (i + step) % 4) for g in range(4) for i in range(4)]
    if kind == "z":
        return "rows", [(4 * i + g, 4 * ((i + step) % 4) + g) for g in range(4) for i in range(4)]
    return kind, [(i, (i + step) % 4) for i in range(4)]


def shifted(value, kind, step):
    axis, pairs = mesh_pairs(kind, step)
    return lax.ppermute(value, axis, pairs)


def gather_sum(value, kind):
    one, two, three = (shifted(value, kind, step) for step in (1, 2, 3))
    return (value + two) + (one + three)


def scatter_sum(value, kind):
    place = lax.axis_index(kind)
    mine = lax.dynamic_index_in_dim(value, place, 0, keepdims=False)
    one, two, three = (
        shifted(lax.dynamic_index_in_dim(value, (place + step) % 4, 0, keepdims=False), kind, step)
        for step in (1, 2, 3)
    )
    return (mine + two) + (one + three)


def gather_parts(value, kind):
    place = lax.axis_index(kind)
    around = jnp.stack([value] + [shifted(value, kind, step) for step in (1, 2, 3)])
    return jnp.concatenate(
        [lax.dynamic_index_in_dim(around, (place - part) % 4, 0) for part in range(4)], axis=0
    )


def sum_everywhere(flat):
    rows = flat.shape[0]
    mine = scatter_sum(flat.reshape(4, rows // 4, 128), "dp")
    for kind in ("x", "z", "ang"):
        mine = gather_sum(mine, kind)
    return gather_parts(mine, "dp").reshape(rows, 128)


def from_both(head, tail, axis):
    ends = lax.axis_size(axis) - 1
    before = lax.ppermute(tail, axis, [(i, i + 1) for i in range(ends)])
    after = lax.ppermute(head, axis, [(i + 1, i) for i in range(ends)])
    return before, after


def column(shape):
    return lax.broadcasted_iota(jnp.int32, shape, len(shape) - 1)


def from_left(values):
    return jnp.where(column(values.shape) == 0, 0.0, pltpu.roll(values, 1, axis=1))


def from_right(values):
    width = values.shape[1]
    return jnp.where(column(values.shape) == width - 1, 0.0, pltpu.roll(values, width - 1, axis=1))


def product(left, right):
    return jnp.dot(left, right, preferred_element_type=F32)


def product_nt(left, right):
    return lax.dot_general(left, right, (((1,), (1,)), ((), ())), preferred_element_type=F32)


def silu_slope(values, gate):
    return gate * (1.0 + values * (1.0 - gate))


def taps_of(slope):
    return jnp.concatenate(
        [from_right(slope).astype(BF16), slope.astype(BF16), from_left(slope).astype(BF16)], axis=0
    )


def deal_kernel(own_ref, before_ref, after_ref, dealt_ref, deal_ref):
    size = deal_ref.shape[0]
    source = lax.broadcasted_iota(jnp.int32, (size, size), 0)
    target = lax.broadcasted_iota(jnp.int32, (size, size), 1)
    lanes = size // 4
    wanted = 4 * (target % lanes) + target // lanes
    deal = jnp.where(source == wanted, 1.0, 0.0).astype(BF16)
    deal_ref[...] = deal
    views = [before_ref[...], own_ref[0], own_ref[1], after_ref[...]]
    for block in range(own_ref.shape[2] // size):
        stacked = jnp.concatenate([v[:, block * size : (block + 1) * size] for v in views], axis=0)
        moved = product(stacked, deal).astype(BF16)
        for view in range(4):
            for q in range(4):
                dealt_ref[view, q * 16 : (q + 1) * 16, block * lanes : (block + 1) * lanes] = moved[
                    view * 16 : (view + 1) * 16, q * lanes : (q + 1) * lanes
                ]


def spatial_kernel(light_ref, above_ref, below_ref, weight_ref, first_ref, out_ref):
    rows = light_ref.shape[1]
    lines = [above_ref[0, 0]] + [light_ref[0, h] for h in range(rows)] + [below_ref[0, 0]]
    chans = lines[0].shape[0]
    for h in range(rows):
        stacked = jnp.concatenate(lines[h : h + 3], axis=0)
        taps = product(weight_ref[...], stacked)
        total = (
            taps[chans : 2 * chans]
            + from_left(taps[:chans])
            + from_right(taps[2 * chans :])
        )
        out_ref[0, h] = total
        first_ref[0, h] = (lines[h + 1].astype(F32) + total * jax.nn.sigmoid(total)).astype(BF16)


def main_kernel(
    own_ref,
    before_ref,
    after_ref,
    dealt_ref,
    deal_ref,
    light_ref,
    above_ref,
    below_ref,
    out_ref,
    epi_ref,
    back_ref,
    lift_ref,
    drop_ref,
    up_ref,
    pay_ref,
    lines,
    epi_acc,
    spatial_acc,
    up_acc,
    lift_acc,
):
    step = pl.program_id(0)
    rows = light_ref.shape[1]
    chans = light_ref.shape[2]

    @pl.when(step == 0)
    def _():
        for v in range(2):
            lines[v, :chans] = above_ref[v, 0]
            for h in range(rows):
                lines[v, (h + 1) * chans : (h + 2) * chans] = light_ref[v, h]
            lines[v, (rows + 1) * chans :] = below_ref[v, 0]
        epi_acc[...] = jnp.zeros_like(epi_acc)
        spatial_acc[...] = jnp.zeros_like(spatial_acc)
        up_acc[...] = jnp.zeros_like(up_acc)
        lift_acc[...] = jnp.zeros_like(lift_acc)

    firsts = jnp.concatenate(
        [ref[v, 0] for ref in (before_ref, own_ref, after_ref) for v in range(2)], axis=0
    )
    here = (lax.broadcasted_iota(jnp.int32, (4 * 16, chans), 0) % 16) // 4 == step
    grads, slopes, slopes_f = [], [], []
    for v in range(4):
        window = firsts[v * chans : (v + 3) * chans]
        taps = product(epi_ref[...], window)
        total = (
            taps[chans : 2 * chans]
            + from_left(taps[:chans])
            + from_right(taps[2 * chans :])
        )
        gate = jax.nn.sigmoid(total)
        grad = product(drop_ref[0], dealt_ref[v]).astype(BF16).astype(F32)
        slope = grad * silu_slope(total, gate)
        slopes.append(slope.astype(BF16))
        if v in (1, 2):
            grads.append(grad)
            second = (own_ref[v - 1, 0].astype(F32) + total * gate).astype(BF16)
            lift_acc[v - 1] += product(lift_ref[0], second)
            up_acc[...] += jnp.where(here, product_nt(dealt_ref[v], second), 0.0)
            epi_acc[...] += product_nt(taps_of(slope), window)
    slopes = jnp.concatenate(slopes, axis=0)
    for v in range(2):
        taps = product(back_ref[...], slopes[v * chans : (v + 3) * chans])
        first_grad = grads[v] + (
            taps[chans : 2 * chans]
            + from_right(taps[:chans])
            + from_left(taps[2 * chans :])
        )
        first_grad = first_grad.astype(BF16).astype(F32)
        total = out_ref[v, 0]
        slope = first_grad * silu_slope(total, jax.nn.sigmoid(total))
        near = lines[v, pl.ds(pl.multiple_of(step * chans, chans), 3 * chans)]
        spatial_acc[...] += product_nt(taps_of(slope), near)

    @pl.when(step == pl.num_programs(0) - 1)
    def _():
        size = deal_ref.shape[0]
        lanes = size // 4
        lifted = [lift_acc[v].astype(BF16) for v in range(2)]
        for block in range(up_ref.shape[2] // size):
            spread = jnp.concatenate(
                [
                    jnp.concatenate(
                        [
                            lifted[v][q * 16 : (q + 1) * 16, block * lanes : (block + 1) * lanes]
                            for q in range(4)
                        ],
                        axis=1,
                    )
                    for v in range(2)
                ],
                axis=0,
            )
            woven = product_nt(spread, deal_ref[...]).astype(BF16)
            for v in range(2):
                up_ref[v, :, block * size : (block + 1) * size] = woven[v * 16 : (v + 1) * 16]
        three = 3 * chans
        pay_ref[:three] = spatial_acc[:, :128]
        pay_ref[three : 2 * three] = epi_acc[:, :128]
        pay_ref[2 * three : 3 * three] = jnp.concatenate(
            [spatial_acc[:, 128:], epi_acc[:, 128:]], axis=1
        )
        pay_ref[3 * three :] = jnp.concatenate([up_acc[...], jnp.zeros_like(up_acc)], axis=1)


def unpack_kernel(pay_ref, spatial_ref, epi_ref, up_ref):
    chans = spatial_ref.shape[2]
    three = 3 * chans
    for which, ref in enumerate((spatial_ref, epi_ref)):
        for j in range(3):
            both = pay_ref[which * three + j * chans : which * three + (j + 1) * chans, :]
            ref[0, j] = both[:, :chans]
            ref[1, j] = both[:, chans:]
            last = pay_ref[2 * three + j * chans : 2 * three + (j + 1) * chans, :]
            ref[2, j] = last[:, which * chans : (which + 1) * chans]
    for p in range(4):
        for q in range(4):
            base = 3 * three + q * 16 + p
            total = pay_ref[base : base + 1, :chans]
            for h in range(1, 4):
                total = total + pay_ref[base + 4 * h : base + 4 * h + 1, :chans]
            up_ref[4 * p + q : 4 * p + q + 1, :] = total


def whole(shape):
    return pl.BlockSpec(shape, lambda *_: (0,) * len(shape))


def on_device(light_field, spatial_weight, epi_weight, upsample_weight, image_grad):
    _, _, views, rows, chans, breadth = light_field.shape
    light = light_field.reshape(views, rows, chans, breadth)
    image = image_grad.reshape(views, image_grad.shape[3], image_grad.shape[4])
    params = pltpu.CompilerParams(vmem_limit_bytes=VMEM_LIMIT)

    above, below = from_both(light[:, :1], light[:, rows - 1 :], "rows")
    image_before, image_after = from_both(image[0], image[views - 1], "ang")

    three = 3 * chans
    spatial_taps = spatial_weight.transpose(1, 2, 0, 3).reshape(three, three)
    epi_taps = epi_weight.transpose(1, 2, 0, 3).reshape(three, three)
    back_taps = epi_weight[::-1].transpose(1, 3, 0, 2).reshape(three, three)
    by_q = upsample_weight.reshape(4, 4, chans).transpose(1, 0, 2)
    same = jnp.eye(rows, dtype=BF16)
    lift = (same[:, None, :, None, None] * by_q[None, :, None, :, :]).reshape(rows, 64, chans)
    drop = lift.transpose(0, 2, 1)

    dealt, deal = pl.pallas_call(
        deal_kernel,
        out_shape=(
            jax.ShapeDtypeStruct((4, 64, breadth), BF16),
            jax.ShapeDtypeStruct((512, 512), BF16),
        ),
        compiler_params=params,
        name="deal",
    )(image, image_before, image_after)

    by_view = pl.BlockSpec((1, rows, chans, breadth), lambda v: (v, 0, 0, 0))
    edge = pl.BlockSpec((1, 1, chans, breadth), lambda v: (v, 0, 0, 0))
    first, spatial_out = pl.pallas_call(
        spatial_kernel,
        grid=(views,),
        in_specs=[by_view, edge, edge, whole((three, three))],
        out_specs=(by_view, by_view),
        out_shape=(
            jax.ShapeDtypeStruct(light.shape, BF16),
            jax.ShapeDtypeStruct(light.shape, F32),
        ),
        compiler_params=params,
        name="spatial",
    )(light, above, below, spatial_taps)

    before, after = from_both(first, first, "ang")

    by_row = pl.BlockSpec((views, 1, chans, breadth), lambda h: (0, h, 0, 0))
    up, pay = pl.pallas_call(
        main_kernel,
        grid=(rows,),
        in_specs=[
            by_row,
            by_row,
            by_row,
            whole(dealt.shape),
            whole(deal.shape),
            whole(light.shape),
            whole(above.shape),
            whole(below.shape),
            by_row,
            whole((three, three)),
            whole((three, three)),
            pl.BlockSpec((1, 64, chans), lambda h: (h, 0, 0)),
            pl.BlockSpec((1, chans, 64), lambda h: (h, 0, 0)),
        ],
        out_specs=(whole(image.shape), whole((640, 128))),
        out_shape=(
            jax.ShapeDtypeStruct(image.shape, BF16),
            jax.ShapeDtypeStruct((640, 128), F32),
        ),
        scratch_shapes=[
            pltpu.VMEM((views, (rows + 2) * chans, breadth), BF16),
            pltpu.VMEM((three, three), F32),
            pltpu.VMEM((three, three), F32),
            pltpu.VMEM((64, chans), F32),
            pltpu.VMEM((views, 64, breadth), F32),
        ],
        compiler_params=params,
        name="main",
    )(
        first,
        before,
        after,
        dealt,
        deal,
        light,
        above,
        below,
        spatial_out,
        epi_taps,
        back_taps,
        lift,
        drop,
    )

    total = sum_everywhere(pay)
    spatial_grad, epi_grad, up_grad = pl.pallas_call(
        unpack_kernel,
        out_shape=(
            jax.ShapeDtypeStruct(spatial_weight.shape, F32),
            jax.ShapeDtypeStruct(epi_weight.shape, F32),
            jax.ShapeDtypeStruct(upsample_weight.shape, F32),
        ),
        compiler_params=params,
        name="unpack",
    )(total)
    return (up.reshape(image_grad.shape), spatial_grad, epi_grad, up_grad)


def solution(mesh):
    placed = (
        P("dp", None, "ang", "rows", None, None),
        P(),
        P(),
        P(),
        P("dp", None, "ang", "rows", None),
    )
    return jax.shard_map(
        on_device,
        mesh=mesh,
        in_specs=placed,
        out_specs=(P("dp", None, "ang", "rows", None), P(), P(), P()),
        check_vma=False,
    )
```

time: 145 us -> 108 us (0.74); the launches traced: 142 us -> 107 us
  local copies, waits for them, and re-layouts: 36.7 us -> 7.43 us
  matrix products: 18.9 us -> 0 us
  Pallas kernels: 0 us -> 17.8 us
  starting transfers between devices: 48.5 us -> 45.5 us
  waiting for transfers between devices: 35.1 us -> 33.2 us
    reshape x11 -> x3, local copies, waits for them, and re-layouts: 28.7 us -> 2.4 us  [the longest x1 0.81 us: on_device(): spatial_taps = spatial_weight.transpose(1, 2, 0, 3).reshape(three, three)]
    all_to_all x4 -> x0, waiting for transfers between devices: 20.5 us -> none  [the longest x1 7.48 us: on_device(): lax.all_to_all(first_grad, 'ang', split_axis=2, concat_axis=3, tiled=True)]
    dot_general x48 -> x0, matrix products: 18.9 us -> none  [the longest x18 5.47 us: weight_grad(): jnp.einsum('buvhow,buvhcw->oc', upstream, window, preferred_element_type=...]
    pallas_call x0 -> x4, Pallas kernels: none -> 17.8 us  [the longest x1 10.7 us: on_device(): pl.pallas_call(main_kernel, grid=(rows,), in_specs=[by_row, by_row, by_ro...]
    all_to_all x4 -> x0, starting transfers between devices: 15.1 us -> none  [the longest x1 4.46 us: on_device(): lax.all_to_all(view_grad, 'ang', split_axis=3, concat_axis=2, tiled=True)]
    ppermute x15, waiting for transfers between devices: 14.6 us -> 26.1 us  [shifted(): return lax.ppermute(value, axis, pairs)]
    ppermute x2 -> x6, starting transfers between devices: 8.85 us -> 19.6 us  [the longest x3 11.6 us: from_both(): before = lax.ppermute(tail, axis, [(i, i + 1) for i in range(ends)])]
    ppermute x2 -> x6, waiting for transfers between devices: 0.01 us -> 7.11 us  [the longest x3 6.69 us: from_both(): after = lax.ppermute(head, axis, [(i + 1, i) for i in range(ends)])]
  transfers between devices with their start and end apart: 21 -> 21, of which waited for: 13 -> 14; matrix products, arithmetic and copies ran while one was open for 28% -> 4% of each run, Pallas kernels for 0% -> 2%
where the time goes in v2:
time: 108 us; the launch traced here: 107 us
  starting transfers between devices  45.5 us (42%)
  waiting for transfers between devices  33.2 us (31%)
  Pallas kernels  17.8 us (16%)
  local copies, waits for them, and re-layouts  7.43 us (7%)
  other arithmetic  2.47 us (2%)
    ppermute x15, waiting for transfers between devices, shifted(): return lax.ppermute(value, axis, pairs)  26.1 us
    ppermute x15, starting transfers between devices, shifted(): return lax.ppermute(value, axis, pairs)  25.9 us
    ppermute x3, starting transfers between devices, from_both(): before = lax.ppermute(tail, axis, [(i, i + 1) for i in range(ends)])  11.6 us
    pallas_call x1, Pallas kernels, on_device(): pl.pallas_call(main_kernel, grid=(rows,), in_specs=[by_row, by_row, by_ro...  10.7 us
    ppermute x3, starting transfers between devices, from_both(): after = lax.ppermute(head, axis, [(i + 1, i) for i in range(ends)])  8.04 us
    ppermute x3, waiting for transfers between devices, from_both(): after = lax.ppermute(head, axis, [(i + 1, i) for i in range(ends)])  6.69 us
    pallas_call x1, Pallas kernels, on_device(): pl.pallas_call(spatial_kernel, grid=(views,), in_specs=[by_view, edge, ed...  3.06 us
    unnamed x20, local copies, waits for them, and re-layouts  2.26 us
  transfers between devices with their start and end apart: 21, of which 14 were waited for; matrix products, arithmetic and copies ran while one was open for 4% of the time, Pallas kernels for 2%

profile of v2, /device:TPU:64, one launch (start us, length us, event | category | flops | bytes accessed | tf_op | source)
XLA Modules:
  0.0 107.3 jit_solution(14561412860831255834)
XLA Ops:
  0.6 1.0 fusion.2
  1.7 3.4 %collective-permute-start = (bf16[2,1,64,512]{3,2,1,0:T(8,128)(2,1)S(1)}, bf16[2,1,64,512]{3,2,1,0:T(8,128)(2,1)S(1)}, u32[]{:S(2)}, u32[]{:S(2)}) collective-permute-start(bf16[2,1,64,512]{3,2,1,0:T(8,128)(2,1)S(1)} %get-tuple-element.23), channel_id=1, source_target_pairs={{0,1},{1,2},{2,3},{3,4},{4,5},{5,6},{6,7},{7,8},{8,9},{9,10},{10,1... | collective-permute-start | bytes 393224 | tf_op jit(solution)/shard_map/ppermute | solution.py:59
  5.1 5.5 %collective-permute-start.1 = (bf16[2,1,64,512]{3,2,1,0:T(8,128)(2,1)S(1)}, bf16[2,1,64,512]{3,2,1,0:T(8,128)(2,1)S(1)}, u32[]{:S(2)}, u32[]{:S(2)}) collective-permute-start(bf16[2,1,64,512]{3,2,1,0:T(8,128)(2,1)S(1)} %get-tuple-element.22), channel_id=1, source_target_pairs={{1,0},{2,1},{3,2},{4,3},{5,4},{6,5},{7,6},{8,7},{9,8},{10,9},{11,1... | collective-permute-start | bytes 393224 | tf_op jit(solution)/shard_map/ppermute | solution.py:60
  10.5 0.1 copy.14
  10.7 0.8 reshape.52.weight_ref
  11.5 0.4 collective-permute-done.above_ref
  11.9 3.9 %collective-permute-done.1.below_ref = bf16[2,1,64,512]{3,2,1,0:T(8,128)(2,1)S(1)} collective-permute-done((bf16[2,1,64,512]{3,2,1,0:T(8,128)(2,1)S(1)}, bf16[2,1,64,512]{3,2,1,0:T(8,128)(2,1)S(1)}, u32[]{:S(2)}, u32[]{:S(2)}) %collective-permute-start.1) | collective-permute-done | bytes 131104 | tf_op jit(solution)/shard_map/ppermute | solution.py:60
  15.8 0.7 copy-done.4
  16.5 3.1 %spatial.1 = (bf16[2,4,64,512]{3,2,1,0:T(8,128)(2,1)}, f32[2,4,64,512]{3,2,1,0:T(8,128)}) custom-call(bf16[2,4,64,512]{3,2,1,0:T(8,128)(2,1)} %bitcast.34, bf16[2,1,64,512]{3,2,1,0:T(8,128)(2,1)} %copy-done.3, bf16[2,1,64,512]{3,2,1,0:T(8,128)(2,1)} %copy-done.4, bf16[192,192]{1,0:T(8,128)(2,1)} %reshape.52.weight_ref), custom_call_target="tpu_custom_call" | custom-call | tf_op jit(solution)/shard_map/spatial/pallas_call | solution.py:289
  19.5 3.6 %collective-permute-start.2 = (bf16[2,4,64,512]{3,2,1,0:T(8,128)(2,1)}, bf16[2,4,64,512]{3,2,1,0:T(8,128)(2,1)S(1)}, u32[]{:S(2)}, u32[]{:S(2)}) collective-permute-start(bf16[2,4,64,512]{3,2,1,0:T(8,128)(2,1)} %get-tuple-element.13.own_ref), channel_id=1, source_target_pairs={{0,16},{16,32},{32,48},{1,17},{17,33},{33,49},{2,18},{18,34},{34,5... | collective-permute-start | bytes 1572872 | tf_op jit(solution)/shard_map/ppermute | solution.py:59
  23.1 1.3 %collective-permute-start.3 = (bf16[2,4,64,512]{3,2,1,0:T(8,128)(2,1)}, bf16[2,4,64,512]{3,2,1,0:T(8,128)(2,1)S(1)}, u32[]{:S(2)}, u32[]{:S(2)}) collective-permute-start(bf16[2,4,64,512]{3,2,1,0:T(8,128)(2,1)} %get-tuple-element.13.own_ref), channel_id=1, source_target_pairs={{16,0},{32,16},{48,32},{17,1},{33,17},{49,33},{18,2},{34,18},{50,3... | collective-permute-start | bytes 1572872 | tf_op jit(solution)/shard_map/ppermute | solution.py:60
  24.5 4.5 %collective-permute-start.4 = (bf16[16,2048]{1,0:T(8,128)(2,1)S(1)}, bf16[16,2048]{1,0:T(8,128)(2,1)S(1)}, u32[]{:S(2)}, u32[]{:S(2)}) collective-permute-start(bf16[16,2048]{1,0:T(8,128)(2,1)S(1)} %get-tuple-element.32), channel_id=1, source_target_pairs={{0,16},{16,32},{32,48},{1,17},{17,33},{33,49},{2,18},{18,34},{34,5... | collective-permute-start | bytes 196616 | tf_op jit(solution)/shard_map/ppermute | solution.py:59
  29.0 1.3 %collective-permute-start.5 = (bf16[16,2048]{1,0:T(8,128)(2,1)S(1)}, bf16[16,2048]{1,0:T(8,128)(2,1)S(1)}, u32[]{:S(2)}, u32[]{:S(2)}) collective-permute-start(bf16[16,2048]{1,0:T(8,128)(2,1)S(1)} %get-tuple-element.31), channel_id=1, source_target_pairs={{16,0},{32,16},{48,32},{17,1},{33,17},{49,33},{18,2},{34,18},{50,3... | collective-permute-start | bytes 196616 | tf_op jit(solution)/shard_map/ppermute | solution.py:60
  30.4 0.1 copy.15
  30.5 0.0 copy-start.9
  30.5 0.8 reshape.54.epi_ref
  31.3 0.1 copy.18
  31.5 0.1 mul.35
  31.5 0.1 mul.36
  31.6 0.7 broadcast_multiply_fusion
  32.4 0.2 copy.16
  32.6 0.8 reshape.55.back_ref
  33.3 0.0 collective-permute-done.4.before_ref
  33.4 2.8 %collective-permute-done.5.after_ref = bf16[16,2048]{1,0:T(8,128)(2,1)S(1)} collective-permute-done((bf16[16,2048]{1,0:T(8,128)(2,1)S(1)}, bf16[16,2048]{1,0:T(8,128)(2,1)S(1)}, u32[]{:S(2)}, u32[]{:S(2)}) %collective-permute-start.5) | collective-permute-done | bytes 65568 | tf_op jit(solution)/shard_map/ppermute | solution.py:60
  36.2 0.6 copy-done.8
  36.8 2.2 %deal.1 = (bf16[4,64,512]{2,1,0:T(8,128)(2,1)}, bf16[512,512]{1,0:T(8,128)(2,1)}) custom-call(bf16[2,16,2048]{2,1,0:T(8,128)(2,1)} %bitcast.38, bf16[16,2048]{1,0:T(8,128)(2,1)} %copy-done.7, bf16[16,2048]{1,0:T(8,128)(2,1)} %copy-done.8), custom_call_target="tpu_custom_call" | custom-call | tf_op jit(solution)/shard_map/deal/pallas_call | solution.py:277
  39.0 0.0 collective-permute-done.2.before_ref
  39.0 0.0 collective-permute-done.3.after_ref
  39.0 0.8 copy-done.1
  39.8 0.2 copy-done.2
  40.0 10.7 %main.1 = (bf16[2,16,2048]{2,1,0:T(8,128)(2,1)}, f32[640,128]{1,0:T(8,128)}) custom-call(bf16[2,4,64,512]{3,2,1,0:T(8,128)(2,1)} %get-tuple-element.13.own_ref, bf16[2,4,64,512]{3,2,1,0:T(8,128)(2,1)} %copy-done.1, bf16[2,4,64,512]{3,2,1,0:T(8,128)(2,1)} %copy-done.2, bf16[4,64,512]{2,1,0:T(8,128)(2,1)} %get-tuple-element.14.dealt_ref, ...), custom_call_target="tpu_custom_call" | custom-call | tf_op jit(solution)/shard_map/main/pallas_call | solution.py:305
  50.7 1.0 dynamic-slice_bitcast_fusion
  51.6 5.1 %collective-permute-start.6 = (f32[160,128]{1,0:T(8,128)S(1)}, f32[160,128]{1,0:T(8,128)S(1)}, u32[]{:S(2)}, u32[]{:S(2)}) collective-permute-start(f32[160,128]{1,0:T(8,128)S(1)} %get-tuple-element.30), channel_id=1, source_target_pairs={{0,128},{64,192},{128,0},{192,64},{1,129},{65,193},{129,1},{193,65... | collective-permute-start | bytes 245768 | tf_op jit(solution)/shard_map/ppermute | solution.py:23
  56.8 0.0 collective-permute-start.7
  56.8 1.7 %collective-permute-start.8 = (f32[160,128]{1,0:T(8,128)S(1)}, f32[160,128]{1,0:T(8,128)S(1)}, u32[]{:S(2)}, u32[]{:S(2)}) collective-permute-start(f32[160,128]{1,0:T(8,128)S(1)} %get-tuple-element.28), channel_id=1, source_target_pairs={{0,192},{64,0},{128,64},{192,128},{1,193},{65,1},{129,65},{193,129... | collective-permute-start | bytes 245768 | tf_op jit(solution)/shard_map/ppermute | solution.py:23
  58.5 0.7 collective-permute-done.6
  59.2 2.0 %collective-permute-done.7 = f32[160,128]{1,0:T(8,128)S(1)} collective-permute-done((f32[160,128]{1,0:T(8,128)S(1)}, f32[160,128]{1,0:T(8,128)S(1)}, u32[]{:S(2)}, u32[]{:S(2)}) %collective-permute-start.7) | collective-permute-done | bytes 81952 | tf_op jit(solution)/shard_map/ppermute | solution.py:23
  61.2 0.0 collective-permute-done.8
  61.2 0.9 fusion
  62.1 0.1 collective-permute-start.10
  62.2 7.7 %collective-permute-start.11 = (f32[160,128]{1,0:T(8,128)S(1)}, f32[160,128]{1,0:T(8,128)S(1)}, u32[]{:S(2)}, u32[]{:S(2)}) collective-permute-start(f32[160,128]{1,0:T(8,128)S(1)} %fusion), channel_id=1, source_target_pairs={{0,3},{1,0},{2,1},{3,2},{4,7},{5,4},{6,5},{7,6},{8,11},{9,8},{10,9... | collective-permute-start | bytes 245768 | tf_op jit(solution)/shard_map/ppermute | solution.py:23
  69.9 1.4 %collective-permute-start.9 = (f32[160,128]{1,0:T(8,128)S(1)}, f32[160,128]{1,0:T(8,128)S(1)}, u32[]{:S(2)}, u32[]{:S(2)}) collective-permute-start(f32[160,128]{1,0:T(8,128)S(1)} %fusion), channel_id=1, source_target_pairs={{0,2},{1,3},{2,0},{3,1},{4,6},{5,7},{6,4},{7,5},{8,10},{9,11},{10,... | collective-permute-start | bytes 245768 | tf_op jit(solution)/shard_map/ppermute | solution.py:23
  71.3 1.4 %collective-permute-done.10 = f32[160,128]{1,0:T(8,128)S(1)} collective-permute-done((f32[160,128]{1,0:T(8,128)S(1)}, f32[160,128]{1,0:T(8,128)S(1)}, u32[]{:S(2)}, u32[]{:S(2)}) %collective-permute-start.10) | collective-permute-done | bytes 81952 | tf_op jit(solution)/shard_map/ppermute | solution.py:23
  72.7 0.0 collective-permute-done.11
  72.7 3.9 %collective-permute-done.9 = f32[160,128]{1,0:T(8,128)S(1)} collective-permute-done((f32[160,128]{1,0:T(8,128)S(1)}, f32[160,128]{1,0:T(8,128)S(1)}, u32[]{:S(2)}, u32[]{:S(2)}) %collective-permute-start.9) | collective-permute-done | bytes 81952 | tf_op jit(solution)/shard_map/ppermute | solution.py:23
  76.7 0.5 collective-permute-start.13
  77.2 2.5 %collective-permute-start.14 = (f32[160,128]{1,0:T(8,128)S(1)}, f32[160,128]{1,0:T(8,128)S(1)}, u32[]{:S(2)}, u32[]{:S(2)}) collective-permute-start(f32[160,128]{1,0:T(8,128)S(1)} %add_add_fusion.2), channel_id=1, source_target_pairs={{0,12},{4,0},{8,4},{12,8},{1,13},{5,1},{9,5},{13,9},{2,14},{6,2},{... | collective-permute-start | bytes 245768 | tf_op jit(solution)/shard_map/ppermute | solution.py:23
  79.7 0.0 collective-permute-start.12
  79.7 2.4 %collective-permute-done.13 = f32[160,128]{1,0:T(8,128)S(1)} collective-permute-done((f32[160,128]{1,0:T(8,128)S(1)}, f32[160,128]{1,0:T(8,128)S(1)}, u32[]{:S(2)}, u32[]{:S(2)}) %collective-permute-start.13) | collective-permute-done | bytes 81952 | tf_op jit(solution)/shard_map/ppermute | solution.py:23
  82.1 6.0 %collective-permute-done.14 = f32[160,128]{1,0:T(8,128)S(1)} collective-permute-done((f32[160,128]{1,0:T(8,128)S(1)}, f32[160,128]{1,0:T(8,128)S(1)}, u32[]{:S(2)}, u32[]{:S(2)}) %collective-permute-start.14) | collective-permute-done | bytes 81952 | tf_op jit(solution)/shard_map/ppermute | solution.py:23
  88.1 0.5 collective-permute-done.12
  88.6 1.6 %collective-permute-start.16 = (f32[160,128]{1,0:T(8,128)S(1)}, f32[160,128]{1,0:T(8,128)S(1)}, u32[]{:S(2)}, u32[]{:S(2)}) collective-permute-start(f32[160,128]{1,0:T(8,128)S(1)} %add_add_fusion.1), channel_id=1, source_target_pairs={{0,16},{16,32},{32,48},{48,0},{1,17},{17,33},{33,49},{49,1},{2,18}... | collective-permute-start | bytes 245768 | tf_op jit(solution)/shard_map/ppermute | solution.py:23
  90.2 1.7 %collective-permute-start.17 = (f32[160,128]{1,0:T(8,128)S(1)}, f32[160,128]{1,0:T(8,128)S(1)}, u32[]{:S(2)}, u32[]{:S(2)}) collective-permute-start(f32[160,128]{1,0:T(8,128)S(1)} %add_add_fusion.1), channel_id=1, source_target_pairs={{0,48},{16,0},{32,16},{48,32},{1,49},{17,1},{33,17},{49,33},{2,50}... | collective-permute-start | bytes 245768 | tf_op jit(solution)/shard_map/ppermute | solution.py:23
  91.9 1.7 %collective-permute-start.15 = (f32[160,128]{1,0:T(8,128)S(1)}, f32[160,128]{1,0:T(8,128)S(1)}, u32[]{:S(2)}, u32[]{:S(2)}) collective-permute-start(f32[160,128]{1,0:T(8,128)S(1)} %add_add_fusion.1), channel_id=1, source_target_pairs={{0,32},{16,48},{32,0},{48,16},{1,33},{17,49},{33,1},{49,17},{2,34}... | collective-permute-start | bytes 245768 | tf_op jit(solution)/shard_map/ppermute | solution.py:23
  93.6 1.6 %collective-permute-done.16 = f32[160,128]{1,0:T(8,128)S(1)} collective-permute-done((f32[160,128]{1,0:T(8,128)S(1)}, f32[160,128]{1,0:T(8,128)S(1)}, u32[]{:S(2)}, u32[]{:S(2)}) %collective-permute-start.16) | collective-permute-done | bytes 81952 | tf_op jit(solution)/shard_map/ppermute | solution.py:23
  95.2 2.6 %collective-permute-done.15 = f32[160,128]{1,0:T(8,128)S(1)} collective-permute-done((f32[160,128]{1,0:T(8,128)S(1)}, f32[160,128]{1,0:T(8,128)S(1)}, u32[]{:S(2)}, u32[]{:S(2)}) %collective-permute-start.15) | collective-permute-done | bytes 81952 | tf_op jit(solution)/shard_map/ppermute | solution.py:23
  97.9 0.1 collective-permute-start.20
  98.0 1.6 %collective-permute-start.19 = (f32[160,128]{1,0:T(8,128)S(1)}, f32[160,128]{1,0:T(8,128)S(1)}, u32[]{:S(2)}, u32[]{:S(2)}) collective-permute-start(f32[160,128]{1,0:T(8,128)S(1)} %add_add_fusion), channel_id=1, source_target_pairs={{0,128},{64,192},{128,0},{192,64},{1,129},{65,193},{129,1},{193,65... | collective-permute-start | bytes 245768 | tf_op jit(solution)/shard_map/ppermute | solution.py:23
  99.6 0.1 collective-permute-start.18
  99.8 0.3 collective-permute-done.20
  100.0 4.5 %collective-permute-done.19 = f32[160,128]{1,0:T(8,128)S(1)} collective-permute-done((f32[160,128]{1,0:T(8,128)S(1)}, f32[160,128]{1,0:T(8,128)S(1)}, u32[]{:S(2)}, u32[]{:S(2)}) %collective-permute-start.19) | collective-permute-done | bytes 81952 | tf_op jit(solution)/shard_map/ppermute | solution.py:23
  104.6 0.0 collective-permute-done.18
  104.7 0.8 pad_maximum_fusion.1
  105.4 1.9 %unpack.1 = (f32[3,3,64,64]{3,2,1,0:T(8,128)}, f32[3,3,64,64]{3,2,1,0:T(8,128)}, f32[16,64]{1,0:T(8,128)}) custom-call(f32[640,128]{1,0:T(8,128)} %bitcast.36), custom_call_target="tpu_custom_call" | custom-call | tf_op jit(solution)/shard_map/unpack/pallas_call | solution.py:354
  (26 shorter events, 0.2 us)
Async XLA Ops:
  0.6 9.9 %copy-start.6 = (bf16[3,3,64,64]{3,2,1,0:T(8,128)(2,1)S(1)}, bf16[3,3,64,64]{3,2,1,0:T(8,128)(2,1)}, u32[]{:S(2)}) copy-start(bf16[3,3,64,64]{3,2,1,0:T(8,128)(2,1)} %param.6) | copy-start | bytes 221188
  1.7 10.2 %collective-permute-start = (bf16[2,1,64,512]{3,2,1,0:T(8,128)(2,1)S(1)}, bf16[2,1,64,512]{3,2,1,0:T(8,128)(2,1)S(1)}, u32[]{:S(2)}, u32[]{:S(2)}) collective-permute-start(bf16[2,1,64,512]{3,2,1,0:T(8,128)(2,1)S(1)} %get-tuple-element.23), channel_id=1, source_target_pairs={{0,1},{1,2},{2,3},{3,4},{4,5},{5,6},{6,7},{7,8},{8,9},{9,10},{10,1... | collective-permute-start | bytes 393224 | tf_op jit(solution)/shard_map/ppermute | solution.py:59
  5.1 10.7 %collective-permute-start.1 = (bf16[2,1,64,512]{3,2,1,0:T(8,128)(2,1)S(1)}, bf16[2,1,64,512]{3,2,1,0:T(8,128)(2,1)S(1)}, u32[]{:S(2)}, u32[]{:S(2)}) collective-permute-start(bf16[2,1,64,512]{3,2,1,0:T(8,128)(2,1)S(1)} %get-tuple-element.22), channel_id=1, source_target_pairs={{1,0},{2,1},{3,2},{4,3},{5,4},{6,5},{7,6},{8,7},{9,8},{10,9},{11,1... | collective-permute-start | bytes 393224 | tf_op jit(solution)/shard_map/ppermute | solution.py:60
  11.5 13.0 %copy-start.5 = (bf16[1,1,2,16,2048]{4,3,2,1,0:T(8,128)(2,1)S(1)}, bf16[1,1,2,16,2048]{4,3,2,1,0:T(8,128)(2,1)}, u32[]{:S(2)}) copy-start(bf16[1,1,2,16,2048]{4,3,2,1,0:T(8,128)(2,1)} %param.9) | copy-start | bytes 393220
  11.9 3.9 %copy-start.3 = (bf16[2,1,64,512]{3,2,1,0:T(8,128)(2,1)}, bf16[2,1,64,512]{3,2,1,0:T(8,128)(2,1)S(1)}, u32[]{:S(2)}) copy-start(bf16[2,1,64,512]{3,2,1,0:T(8,128)(2,1)S(1)} %collective-permute-done.above_ref) | copy-start | bytes 393220
  15.8 0.7 copy-start.4
  19.5 10.9 %copy-start = (bf16[3,3,64,64]{3,2,1,0:T(8,128)(2,1)S(1)}, bf16[3,3,64,64]{3,2,1,0:T(8,128)(2,1)}, u32[]{:S(2)}) copy-start(bf16[3,3,64,64]{3,2,1,0:T(8,128)(2,1)} %param.7) | copy-start | bytes 221188
  19.5 19.5 %collective-permute-start.2 = (bf16[2,4,64,512]{3,2,1,0:T(8,128)(2,1)}, bf16[2,4,64,512]{3,2,1,0:T(8,128)(2,1)S(1)}, u32[]{:S(2)}, u32[]{:S(2)}) collective-permute-start(bf16[2,4,64,512]{3,2,1,0:T(8,128)(2,1)} %get-tuple-element.13.own_ref), channel_id=1, source_target_pairs={{0,16},{16,32},{32,48},{1,17},{17,33},{33,49},{2,18},{18,34},{34,5... | collective-permute-start | bytes 1572872 | tf_op jit(solution)/shard_map/ppermute | solution.py:59
  23.1 15.8 %collective-permute-start.3 = (bf16[2,4,64,512]{3,2,1,0:T(8,128)(2,1)}, bf16[2,4,64,512]{3,2,1,0:T(8,128)(2,1)S(1)}, u32[]{:S(2)}, u32[]{:S(2)}) collective-permute-start(bf16[2,4,64,512]{3,2,1,0:T(8,128)(2,1)} %get-tuple-element.13.own_ref), channel_id=1, source_target_pairs={{16,0},{32,16},{48,32},{17,1},{33,17},{49,33},{18,2},{34,18},{50,3... | collective-permute-start | bytes 1572872 | tf_op jit(solution)/shard_map/ppermute | solution.py:60
  24.5 8.9 %collective-permute-start.4 = (bf16[16,2048]{1,0:T(8,128)(2,1)S(1)}, bf16[16,2048]{1,0:T(8,128)(2,1)S(1)}, u32[]{:S(2)}, u32[]{:S(2)}) collective-permute-start(bf16[16,2048]{1,0:T(8,128)(2,1)S(1)} %get-tuple-element.32), channel_id=1, source_target_pairs={{0,16},{16,32},{32,48},{1,17},{17,33},{33,49},{2,18},{18,34},{34,5... | collective-permute-start | bytes 196616 | tf_op jit(solution)/shard_map/ppermute | solution.py:59
  29.0 7.1 %collective-permute-start.5 = (bf16[16,2048]{1,0:T(8,128)(2,1)S(1)}, bf16[16,2048]{1,0:T(8,128)(2,1)S(1)}, u32[]{:S(2)}, u32[]{:S(2)}) collective-permute-start(bf16[16,2048]{1,0:T(8,128)(2,1)S(1)} %get-tuple-element.31), channel_id=1, source_target_pairs={{16,0},{32,16},{48,32},{17,1},{33,17},{49,33},{18,2},{34,18},{50,3... | collective-permute-start | bytes 196616 | tf_op jit(solution)/shard_map/ppermute | solution.py:60
  30.5 0.8 copy-start.9
  33.4 2.8 %copy-start.7 = (bf16[16,2048]{1,0:T(8,128)(2,1)}, bf16[16,2048]{1,0:T(8,128)(2,1)S(1)}, u32[]{:S(2)}) copy-start(bf16[16,2048]{1,0:T(8,128)(2,1)S(1)} %collective-permute-done.4.before_ref) | copy-start | bytes 196612
  36.2 0.6 copy-start.8
  39.0 0.8 copy-start.1
  39.0 1.0 copy-start.2
  51.6 7.6 %collective-permute-start.6 = (f32[160,128]{1,0:T(8,128)S(1)}, f32[160,128]{1,0:T(8,128)S(1)}, u32[]{:S(2)}, u32[]{:S(2)}) collective-permute-start(f32[160,128]{1,0:T(8,128)S(1)} %get-tuple-element.30), channel_id=1, source_target_pairs={{0,128},{64,192},{128,0},{192,64},{1,129},{65,193},{129,1},{193,65... | collective-permute-start | bytes 245768 | tf_op jit(solution)/shard_map/ppermute | solution.py:23
  56.8 4.4 %collective-permute-start.7 = (f32[160,128]{1,0:T(8,128)S(1)}, f32[160,128]{1,0:T(8,128)S(1)}, u32[]{:S(2)}, u32[]{:S(2)}) collective-permute-start(f32[160,128]{1,0:T(8,128)S(1)} %get-tuple-element.29), channel_id=1, source_target_pairs={{0,64},{64,128},{128,192},{192,0},{1,65},{65,129},{129,193},{193,1... | collective-permute-start | bytes 245768 | tf_op jit(solution)/shard_map/ppermute | solution.py:23
  56.8 4.4 %collective-permute-start.8 = (f32[160,128]{1,0:T(8,128)S(1)}, f32[160,128]{1,0:T(8,128)S(1)}, u32[]{:S(2)}, u32[]{:S(2)}) collective-permute-start(f32[160,128]{1,0:T(8,128)S(1)} %get-tuple-element.28), channel_id=1, source_target_pairs={{0,192},{64,0},{128,64},{192,128},{1,193},{65,1},{129,65},{193,129... | collective-permute-start | bytes 245768 | tf_op jit(solution)/shard_map/ppermute | solution.py:23
  62.1 10.6 %collective-permute-start.10 = (f32[160,128]{1,0:T(8,128)S(1)}, f32[160,128]{1,0:T(8,128)S(1)}, u32[]{:S(2)}, u32[]{:S(2)}) collective-permute-start(f32[160,128]{1,0:T(8,128)S(1)} %fusion), channel_id=1, source_target_pairs={{0,1},{1,2},{2,3},{3,0},{4,5},{5,6},{6,7},{7,4},{8,9},{9,10},{10,1... | collective-permute-start | bytes 245768 | tf_op jit(solution)/shard_map/ppermute | solution.py:23
  62.2 10.5 %collective-permute-start.11 = (f32[160,128]{1,0:T(8,128)S(1)}, f32[160,128]{1,0:T(8,128)S(1)}, u32[]{:S(2)}, u32[]{:S(2)}) collective-permute-start(f32[160,128]{1,0:T(8,128)S(1)} %fusion), channel_id=1, source_target_pairs={{0,3},{1,0},{2,1},{3,2},{4,7},{5,4},{6,5},{7,6},{8,11},{9,8},{10,9... | collective-permute-start | bytes 245768 | tf_op jit(solution)/shard_map/ppermute | solution.py:23
  69.9 6.7 %collective-permute-start.9 = (f32[160,128]{1,0:T(8,128)S(1)}, f32[160,128]{1,0:T(8,128)S(1)}, u32[]{:S(2)}, u32[]{:S(2)}) collective-permute-start(f32[160,128]{1,0:T(8,128)S(1)} %fusion), channel_id=1, source_target_pairs={{0,2},{1,3},{2,0},{3,1},{4,6},{5,7},{6,4},{7,5},{8,10},{9,11},{10,... | collective-permute-start | bytes 245768 | tf_op jit(solution)/shard_map/ppermute | solution.py:23
  76.7 5.5 %collective-permute-start.13 = (f32[160,128]{1,0:T(8,128)S(1)}, f32[160,128]{1,0:T(8,128)S(1)}, u32[]{:S(2)}, u32[]{:S(2)}) collective-permute-start(f32[160,128]{1,0:T(8,128)S(1)} %add_add_fusion.2), channel_id=1, source_target_pairs={{0,4},{4,8},{8,12},{12,0},{1,5},{5,9},{9,13},{13,1},{2,6},{6,10},{... | collective-permute-start | bytes 245768 | tf_op jit(solution)/shard_map/ppermute | solution.py:23
  77.2 10.9 %collective-permute-start.14 = (f32[160,128]{1,0:T(8,128)S(1)}, f32[160,128]{1,0:T(8,128)S(1)}, u32[]{:S(2)}, u32[]{:S(2)}) collective-permute-start(f32[160,128]{1,0:T(8,128)S(1)} %add_add_fusion.2), channel_id=1, source_target_pairs={{0,12},{4,0},{8,4},{12,8},{1,13},{5,1},{9,5},{13,9},{2,14},{6,2},{... | collective-permute-start | bytes 245768 | tf_op jit(solution)/shard_map/ppermute | solution.py:23
  79.7 8.9 %collective-permute-start.12 = (f32[160,128]{1,0:T(8,128)S(1)}, f32[160,128]{1,0:T(8,128)S(1)}, u32[]{:S(2)}, u32[]{:S(2)}) collective-permute-start(f32[160,128]{1,0:T(8,128)S(1)} %add_add_fusion.2), channel_id=1, source_target_pairs={{0,8},{4,12},{8,0},{12,4},{1,9},{5,13},{9,1},{13,5},{2,10},{6,14},... | collective-permute-start | bytes 245768 | tf_op jit(solution)/shard_map/ppermute | solution.py:23
  88.6 6.6 %collective-permute-start.16 = (f32[160,128]{1,0:T(8,128)S(1)}, f32[160,128]{1,0:T(8,128)S(1)}, u32[]{:S(2)}, u32[]{:S(2)}) collective-permute-start(f32[160,128]{1,0:T(8,128)S(1)} %add_add_fusion.1), channel_id=1, source_target_pairs={{0,16},{16,32},{32,48},{48,0},{1,17},{17,33},{33,49},{49,1},{2,18}... | collective-permute-start | bytes 245768 | tf_op jit(solution)/shard_map/ppermute | solution.py:23
  90.2 5.0 %collective-permute-start.17 = (f32[160,128]{1,0:T(8,128)S(1)}, f32[160,128]{1,0:T(8,128)S(1)}, u32[]{:S(2)}, u32[]{:S(2)}) collective-permute-start(f32[160,128]{1,0:T(8,128)S(1)} %add_add_fusion.1), channel_id=1, source_target_pairs={{0,48},{16,0},{32,16},{48,32},{1,49},{17,1},{33,17},{49,33},{2,50}... | collective-permute-start | bytes 245768 | tf_op jit(solution)/shard_map/ppermute | solution.py:23
  91.9 5.9 %collective-permute-start.15 = (f32[160,128]{1,0:T(8,128)S(1)}, f32[160,128]{1,0:T(8,128)S(1)}, u32[]{:S(2)}, u32[]{:S(2)}) collective-permute-start(f32[160,128]{1,0:T(8,128)S(1)} %add_add_fusion.1), channel_id=1, source_target_pairs={{0,32},{16,48},{32,0},{48,16},{1,33},{17,49},{33,1},{49,17},{2,34}... | collective-permute-start | bytes 245768 | tf_op jit(solution)/shard_map/ppermute | solution.py:23
  97.9 2.1 %collective-permute-start.20 = (f32[160,128]{1,0:T(8,128)S(1)}, f32[160,128]{1,0:T(8,128)S(1)}, u32[]{:S(2)}, u32[]{:S(2)}) collective-permute-start(f32[160,128]{1,0:T(8,128)S(1)} %add_add_fusion), channel_id=1, source_target_pairs={{0,192},{64,0},{128,64},{192,128},{1,193},{65,1},{129,65},{193,129... | collective-permute-start | bytes 245768 | tf_op jit(solution)/shard_map/ppermute | solution.py:23
  98.0 6.6 %collective-permute-start.19 = (f32[160,128]{1,0:T(8,128)S(1)}, f32[160,128]{1,0:T(8,128)S(1)}, u32[]{:S(2)}, u32[]{:S(2)}) collective-permute-start(f32[160,128]{1,0:T(8,128)S(1)} %add_add_fusion), channel_id=1, source_target_pairs={{0,128},{64,192},{128,0},{192,64},{1,129},{65,193},{129,1},{193,65... | collective-permute-start | bytes 245768 | tf_op jit(solution)/shard_map/ppermute | solution.py:23
  99.6 5.0 %collective-permute-start.18 = (f32[160,128]{1,0:T(8,128)S(1)}, f32[160,128]{1,0:T(8,128)S(1)}, u32[]{:S(2)}, u32[]{:S(2)}) collective-permute-start(f32[160,128]{1,0:T(8,128)S(1)} %add_add_fusion), channel_id=1, source_target_pairs={{0,64},{64,128},{128,192},{192,0},{1,65},{65,129},{129,193},{193,1... | collective-permute-start | bytes 245768 | tf_op jit(solution)/shard_map/ppermute | solution.py:23

commit v3 on v0

v3 whole, which is shorter than its diff:
```python
import jax
import jax.numpy as jnp
from jax import lax
from jax.experimental import pallas as pl
from jax.experimental.pallas import tpu as pltpu
from jax.sharding import Mesh
from jax.sharding import PartitionSpec as P

F32 = jnp.float32
BF16 = jnp.bfloat16
DP = ("pair", "core")
ROWS = ("quad", "x")
VMEM_LIMIT = 40 * 1024 * 1024


def swapped(value, axis, step):
    count = lax.axis_size(axis)
    return lax.ppermute(value, axis, [(i, (i + step) % count) for i in range(count)])


def sum_everywhere(pay):
    plane = ("ang", "x")
    rows = pay.shape[0]
    mine = lax.all_to_all(
        pay.reshape(16, rows // 16, 128), plane, split_axis=0, concat_axis=0, tiled=True
    ).sum(0)
    for axis in ("core", "pair"):
        mine = mine + swapped(mine, axis, 1)
    one, two, three = (swapped(mine, "quad", step) for step in (1, 2, 3))
    mine = (mine + two) + (one + three)
    spread = jnp.broadcast_to(mine[None], (16,) + mine.shape)
    return lax.all_to_all(spread, plane, split_axis=0, concat_axis=0, tiled=True).reshape(rows, 128)


def from_both(head, tail, axis):
    count = lax.axis_size(axis)
    before = lax.ppermute(tail, axis, [(i, (i + 1) % count) for i in range(count)])
    after = lax.ppermute(head, axis, [((i + 1) % count, i) for i in range(count)])
    return before, after


def has_neighbours(axis, count):
    place = lax.axis_index(axis)
    return place > 0, place < count - 1


def kept(flag, values):
    return jnp.where(flag, values, jnp.zeros_like(values))


def column(shape):
    return lax.broadcasted_iota(jnp.int32, shape, len(shape) - 1)


def from_left(values):
    return jnp.where(column(values.shape) == 0, 0.0, pltpu.roll(values, 1, axis=1))


def from_right(values):
    width = values.shape[1]
    return jnp.where(column(values.shape) == width - 1, 0.0, pltpu.roll(values, width - 1, axis=1))


def product(left, right):
    return jnp.dot(left, right, preferred_element_type=F32)


def product_nt(left, right):
    return lax.dot_general(left, right, (((1,), (1,)), ((), ())), preferred_element_type=F32)


def gate_of(values):
    return 0.5 * jnp.tanh(0.5 * values) + 0.5


def silu_slope(values, gate):
    return gate * (1.0 + values * (1.0 - gate))


def taps_of(slope):
    return jnp.concatenate(
        [from_right(slope).astype(BF16), slope.astype(BF16), from_left(slope).astype(BF16)], axis=0
    )


def conv_taps(weights, stacked, forward):
    taps = product(weights, stacked)
    chans = weights.shape[0] // 3
    left, right = (from_left, from_right) if forward else (from_right, from_left)
    return taps[chans : 2 * chans] + left(taps[:chans]) + right(taps[2 * chans :])


def unit(size):
    return jnp.where(
        lax.broadcasted_iota(jnp.int32, (size, size), 0)
        == lax.broadcasted_iota(jnp.int32, (size, size), 1),
        1.0,
        0.0,
    ).astype(BF16)


def forward_taps(ref, taps_ref):
    chans = ref.shape[2]
    for j in range(3):
        taps_ref[j * chans : (j + 1) * chans] = jnp.concatenate([ref[i, j] for i in range(3)], axis=1)


def prepare_weights(spatial_ref, epi_ref, up_ref, taps_ref, epi_taps_ref, back_ref, lift_ref, drop_ref):
    chans = spatial_ref.shape[2]
    forward_taps(spatial_ref, taps_ref)
    forward_taps(epi_ref, epi_taps_ref)
    stacked = jnp.concatenate(
        [jnp.concatenate([epi_ref[2 - s, j] for j in range(3)], axis=1) for s in range(3)], axis=0
    )
    back_ref[...] = product_nt(unit(3 * chans), stacked).astype(BF16)
    turned = product_nt(unit(chans), up_ref[...]).astype(BF16)
    line = lax.broadcasted_iota(jnp.int32, (64, 16), 0)
    sub = lax.broadcasted_iota(jnp.int32, (64, 16), 1)
    match = sub == 4 * (line % 4) + line // 16
    for h in range(4):
        pick = jnp.where(match & ((line % 16) // 4 == h), 1.0, 0.0).astype(BF16)
        lift_ref[h] = product(pick, up_ref[...]).astype(BF16)
        drop_ref[h] = product_nt(turned, pick).astype(BF16)


def inner_kernel(
    image_ref,
    light_ref,
    spatial_ref,
    epi_ref,
    up_ref,
    mixed_ref,
    out_ref,
    deal_ref,
    weight_ref,
    epi_taps_ref,
    back_ref,
    lift_ref,
    drop_ref,
):
    prepare_weights(
        spatial_ref, epi_ref, up_ref, weight_ref, epi_taps_ref, back_ref, lift_ref, drop_ref
    )
    size = deal_ref.shape[0]
    source = lax.broadcasted_iota(jnp.int32, (size, size), 0)
    target = lax.broadcasted_iota(jnp.int32, (size, size), 1)
    lanes = size // 4
    wanted = 4 * (target % lanes) + target // lanes
    deal = jnp.where(source == wanted, 1.0, 0.0).astype(BF16)
    deal_ref[...] = deal
    chans = light_ref.shape[2]
    for block in range(image_ref.shape[2] // size):
        cut = slice(block * size, (block + 1) * size)
        stacked = jnp.concatenate([image_ref[0, :, cut], image_ref[1, :, cut]], axis=0)
        moved = product(stacked, deal).astype(BF16)
        for view in range(2):
            for q in range(4):
                mixed_ref[
                    view,
                    2 * chans + q * 16 : 2 * chans + (q + 1) * 16,
                    block * lanes : (block + 1) * lanes,
                ] = moved[view * 16 : (view + 1) * 16, q * lanes : (q + 1) * lanes]
    for view in range(2):
        for slot, h in enumerate((1, 2)):
            stacked = jnp.concatenate([light_ref[view, h + k] for k in (-1, 0, 1)], axis=0)
            total = conv_taps(weight_ref[...], stacked, True)
            out_ref[view, slot] = total
            first = light_ref[view, h].astype(F32) + total * gate_of(total)
            mixed_ref[view, slot * chans : (slot + 1) * chans] = first.astype(BF16)


def edge_kernel(light_ref, above_ref, below_ref, weight_ref, first_ref, out_ref):
    chans = light_ref.shape[2]
    has_above, has_below = has_neighbours(ROWS, 16)
    for view in range(2):
        for slot, h in enumerate((0, 3)):
            if slot == 0:
                stacked = [kept(has_above, above_ref[view, 0]), light_ref[view, 0], light_ref[view, 1]]
            else:
                stacked = [light_ref[view, 2], light_ref[view, 3], kept(has_below, below_ref[view, 0])]
            total = conv_taps(weight_ref[...], jnp.concatenate(stacked, axis=0), True)
            out_ref[view, slot] = total
            first = light_ref[view, h].astype(F32) + total * gate_of(total)
            first_ref[view, slot * chans : (slot + 1) * chans] = first.astype(BF16)


def main_rows(rows, firsts, dealt, near, out_ref, epi_ref, back_ref, lift_ref, drop_ref, pay_ref, lift_out):
    chans = drop_ref.shape[1]
    three = 3 * chans
    lifted = [None, None]
    up_total = None
    epi_left, epi_right, spatial_left, spatial_right = [], [], [], []
    has_before, has_after = has_neighbours("ang", 4)
    for slot, h in enumerate(rows):
        cut = slice(slot * chans, (slot + 1) * chans)
        stack = jnp.concatenate(
            [kept(has_before, firsts[0][v, cut]) for v in range(2)]
            + [firsts[1][v, cut] for v in range(2)]
            + [kept(has_after, firsts[2][v, cut]) for v in range(2)],
            axis=0,
        )
        here = (lax.broadcasted_iota(jnp.int32, (64, chans), 0) % 16) // 4 == h
        grads, slopes = [], []
        for v in range(4):
            window = stack[v * chans : (v + 3) * chans]
            total = conv_taps(epi_ref[...], window, True)
            gate = gate_of(total)
            grad = product(drop_ref[h], dealt[v]).astype(BF16).astype(F32)
            slope = grad * silu_slope(total, gate)
            slopes.append(slope.astype(BF16))
            if v in (1, 2):
                grads.append(grad)
                own = stack[(v + 1) * chans : (v + 2) * chans]
                second = (own.astype(F32) + total * gate).astype(BF16)
                part = product(lift_ref[h], second)
                lifted[v - 1] = part if slot == 0 else lifted[v - 1] + part
                part = jnp.where(here, product_nt(dealt[v], second), 0.0)
                up_total = part if up_total is None else up_total + part
                epi_left.append(taps_of(slope))
                epi_right.append(window)
        slopes = jnp.concatenate(slopes, axis=0)
        for v in range(2):
            moved = conv_taps(back_ref[...], slopes[v * chans : (v + 3) * chans], False)
            first_grad = (grads[v] + moved).astype(BF16).astype(F32)
            total = out_ref[v, slot]
            slope = first_grad * silu_slope(total, gate_of(total))
            spatial_left.append(taps_of(slope))
            spatial_right.append(jnp.concatenate(near(v, h), axis=0))
    for v in range(2):
        lift_out[v] = lifted[v].astype(BF16)
    epi = product_nt(jnp.concatenate(epi_left, axis=1), jnp.concatenate(epi_right, axis=1))
    spatial = product_nt(
        jnp.concatenate(spatial_left, axis=1), jnp.concatenate(spatial_right, axis=1)
    )
    pieces = (
        spatial[:, :128],
        epi[:, :128],
        jnp.concatenate([spatial[:, 128:], epi[:, 128:]], axis=1),
        jnp.concatenate([up_total, jnp.zeros_like(up_total)], axis=1),
    )
    start = 0
    for piece in pieces:
        end = start + piece.shape[0]
        pay_ref[start:end] = piece
        start = end


def dealt_views(own_ref, before_ref, after_ref, chans):
    has_before, has_after = has_neighbours("ang", 4)
    return [
        kept(has_before, before_ref[1, 2 * chans :]),
        own_ref[0, 2 * chans :],
        own_ref[1, 2 * chans :],
        kept(has_after, after_ref[0, 2 * chans :]),
    ]


def main_inner_kernel(
    own_ref, before_ref, after_ref, light_ref, out_ref, epi_ref, back_ref, lift_ref, drop_ref, pay_ref, lift_out
):
    def near(v, h):
        return [light_ref[v, h + k] for k in (-1, 0, 1)]

    main_rows(
        (1, 2),
        (before_ref, own_ref, after_ref),
        dealt_views(own_ref, before_ref, after_ref, light_ref.shape[2]),
        near,
        out_ref,
        epi_ref,
        back_ref,
        lift_ref,
        drop_ref,
        pay_ref,
        lift_out,
    )


def main_edge_kernel(
    first_ref,
    first_before_ref,
    first_after_ref,
    own_ref,
    before_ref,
    after_ref,
    light_ref,
    above_ref,
    below_ref,
    out_ref,
    epi_ref,
    back_ref,
    lift_ref,
    drop_ref,
    inner_pay_ref,
    pay_ref,
    lift_out,
):
    has_above, has_below = has_neighbours(ROWS, 16)

    def near(v, h):
        if h == 0:
            return [kept(has_above, above_ref[v, 0]), light_ref[v, 0], light_ref[v, 1]]
        return [light_ref[v, 2], light_ref[v, 3], kept(has_below, below_ref[v, 0])]

    main_rows(
        (0, 3),
        (first_before_ref, first_ref, first_after_ref),
        dealt_views(own_ref, before_ref, after_ref, light_ref.shape[2]),
        near,
        out_ref,
        epi_ref,
        back_ref,
        lift_ref,
        drop_ref,
        pay_ref,
        lift_out,
    )
    pay_ref[...] += inner_pay_ref[...]


def weave_kernel(inner_ref, edge_ref, deal_ref, up_ref):
    size = deal_ref.shape[0]
    lanes = size // 4
    lifted = [inner_ref[v] + edge_ref[v] for v in range(2)]
    for block in range(up_ref.shape[2] // size):
        spread = [
            jnp.concatenate(
                [
                    lifted[v][q * 16 : (q + 1) * 16, block * lanes : (block + 1) * lanes]
                    for q in range(4)
                ],
                axis=1,
            )
            for v in range(2)
        ]
        woven = product_nt(jnp.concatenate(spread, axis=0), deal_ref[...]).astype(BF16)
        for v in range(2):
            up_ref[v, :, block * size : (block + 1) * size] = woven[v * 16 : (v + 1) * 16]


def unpack_kernel(pay_ref, spatial_ref, epi_ref, up_ref):
    chans = spatial_ref.shape[2]
    three = 3 * chans
    for which, ref in enumerate((spatial_ref, epi_ref)):
        for j in range(3):
            both = pay_ref[which * three + j * chans : which * three + (j + 1) * chans, :]
            ref[0, j] = both[:, :chans]
            ref[1, j] = both[:, chans:]
            last = pay_ref[2 * three + j * chans : 2 * three + (j + 1) * chans, :]
            ref[2, j] = last[:, which * chans : (which + 1) * chans]
    for p in range(4):
        for q in range(4):
            base = 3 * three + q * 16 + p
            total = pay_ref[base : base + 1, :chans]
            for h in range(1, 4):
                total = total + pay_ref[base + 4 * h : base + 4 * h + 1, :chans]
            up_ref[4 * p + q : 4 * p + q + 1, :] = total


def local_call(kernel, shapes, name, *operands, micros=3):
    return pl.pallas_call(
        kernel,
        out_shape=shapes,
        cost_estimate=pl.CostEstimate(
            flops=micros * 1_000_000_000, bytes_accessed=micros * 3_000_000, transcendentals=0
        ),
        compiler_params=pltpu.CompilerParams(vmem_limit_bytes=VMEM_LIMIT),
        name=name,
    )(*(pltpu.with_memory_space_constraint(operand, pltpu.VMEM) for operand in operands))


def on_device(light_field, spatial_weight, epi_weight, upsample_weight, image_grad):
    _, _, views, rows, chans, breadth = light_field.shape
    light = light_field.reshape(views, rows, chans, breadth)
    image = image_grad.reshape(views, image_grad.shape[3], image_grad.shape[4])

    above, below = from_both(light[:, :1], light[:, rows - 1 :], ROWS)

    three = 3 * chans
    like = pltpu.VMEM
    plain = jax.ShapeDtypeStruct
    half_out = like((views, 2, chans, breadth), F32)
    taps = like((three, three), BF16)
    mixed, inner_out, deal, spatial_taps, epi_taps, back_taps, lift, drop = local_call(
        inner_kernel,
        (
            like((views, 2 * chans + 64, breadth), BF16),
            half_out,
            like((512, 512), BF16),
            taps,
            taps,
            taps,
            like((rows, 64, chans), BF16),
            like((rows, chans, 64), BF16),
        ),
        "inner",
        image,
        light,
        spatial_weight,
        epi_weight,
        upsample_weight,
    )
    mixed_before, mixed_after = from_both(mixed, mixed, "ang")
    first, edge_out = local_call(
        edge_kernel,
        (like((views, 2 * chans, breadth), BF16), half_out),
        "edge",
        light,
        above,
        below,
        spatial_taps,
    )
    first_before, first_after = from_both(first, first, "ang")

    weights = (epi_taps, back_taps, lift, drop)
    lift_half = like((views, 64, breadth), BF16)
    whole_pay = like((640, 128), F32)
    inner_pay, inner_lift = local_call(
        main_inner_kernel,
        (whole_pay, lift_half),
        "main_inner",
        mixed,
        mixed_before,
        mixed_after,
        light,
        inner_out,
        *weights,
    )
    pay, edge_lift = local_call(
        main_edge_kernel,
        (whole_pay, lift_half),
        "main_edge",
        first,
        first_before,
        first_after,
        mixed,
        mixed_before,
        mixed_after,
        light,
        above,
        below,
        edge_out,
        *weights,
        inner_pay,
    )
    up = local_call(
        weave_kernel, plain(image.shape, BF16), "weave", inner_lift, edge_lift, deal
    )
    spatial_grad, epi_grad, up_grad = local_call(
        unpack_kernel,
        (
            plain(spatial_weight.shape, F32),
            plain(epi_weight.shape, F32),
            plain(upsample_weight.shape, F32),
        ),
        "unpack",
        sum_everywhere(pay),
    )
    return (up.reshape(image_grad.shape), spatial_grad, epi_grad, up_grad)


def solution(mesh):
    split = Mesh(mesh.devices.reshape(2, 2, 4, 4, 4), ("pair", "core", "ang", "quad", "x"))
    image_spec = P(DP, None, "ang", ROWS, None)
    return jax.shard_map(
        on_device,
        mesh=split,
        in_specs=(P(DP, None, "ang", ROWS, None, None), P(), P(), P(), image_spec),
        out_specs=(image_spec, P(), P(), P()),
        check_vma=False,
    )
```

time: 359 us -> 80.7 us (0.22)
  waiting for transfers between devices: 178 us -> 23.2 us
  blocking collectives: 74.9 us -> 17.1 us
  local copies, waits for them, and re-layouts: 37.3 us -> 4.54 us
  matrix products: 21.9 us -> 0 us
  between operations: 14.6 us -> 0.72 us
  Pallas kernels: 0 us -> 9.99 us
  other arithmetic: 3.92 us -> 0.04 us
    psum x1 -> x0, waiting for transfers between devices: 160 us -> none  [on_device(): lax.psum((spatial_grad, epi_grad, up_grad), ('dp', 'ang', 'rows'))]
    psum x1 -> x0, blocking collectives: 74.9 us -> none  [on_device(): lax.psum((spatial_grad, epi_grad, up_grad), ('dp', 'ang', 'rows'))]
    reshape x5 -> x0, local copies, waits for them, and re-layouts: 26.1 us -> none  [the longest x1 10.8 us: on_device(): image_grad.reshape(batch_here, angular_rows, views_here, rows_here, SCALE...]
    dot_general x48 -> x0, matrix products: 21.9 us -> none  [the longest x18 8.61 us: weight_grad(): jnp.einsum('buvhow,buvhcw->oc', upstream, window, preferred_element_type=...]
    all_to_all x0 -> x1, blocking collectives: none -> 17.1 us  [sum_everywhere(): lax.all_to_all(pay.reshape(16, rows // 16, 128), plane, split_axis=0, con...]
    ppermute x2 -> x11, waiting for transfers between devices: 0.01 us -> 15.6 us  [the longest x5 5.35 us: swapped(): lax.ppermute(value, axis, [(i, (i + step) % count) for i in range(count)])]
    all_to_all x4 -> x1, starting transfers between devices: 15.2 us -> 3.54 us  [sum_everywhere(): lax.all_to_all(spread, plane, split_axis=0, concat_axis=0, tiled=True)]
    ppermute x2 -> x11, starting transfers between devices: 8.85 us -> 20 us  [the longest x5 11.7 us: swapped(): lax.ppermute(value, axis, [(i, (i + step) % count) for i in range(count)])]
  transfers between devices with their start and end apart: 7 -> 12, of which waited for: 5 -> 8; matrix products, arithmetic and copies ran while one was open for 12% -> 0% of each run, Pallas kernels for 0% -> 8%
where the time goes in v3:
time: 80.7 us; the launch traced here: 79.1 us
  starting transfers between devices  23.5 us (29%)
  waiting for transfers between devices  23.2 us (29%)
  blocking collectives  17.1 us (21%)
  Pallas kernels  9.99 us (12%)
  local copies, waits for them, and re-layouts  4.54 us (6%)
    all_to_all x1, blocking collectives, sum_everywhere(): lax.all_to_all(pay.reshape(16, rows // 16, 128), plane, split_axis=0, con...  17.1 us
    ppermute x5, starting transfers between devices, swapped(): lax.ppermute(value, axis, [(i, (i + step) % count) for i in range(count)])  11.7 us
    pallas_call x6, Pallas kernels, local_call(): pl.pallas_call(kernel, out_shape=shapes, cost_estimate=pl.CostEstimate(fl...  9.99 us
    ppermute x3, starting transfers between devices, from_both(): lax.ppermute(head, axis, [((i + 1) % count, i) for i in range(count)])  8.1 us
    all_to_all x1, waiting for transfers between devices, sum_everywhere(): lax.all_to_all(spread, plane, split_axis=0, concat_axis=0, tiled=True)  7.64 us
    ppermute x5, waiting for transfers between devices, swapped(): lax.ppermute(value, axis, [(i, (i + step) % count) for i in range(count)])  5.35 us
    ppermute x3, waiting for transfers between devices, from_both(): lax.ppermute(tail, axis, [(i, (i + 1) % count) for i in range(count)])  5.28 us
    ppermute x3, waiting for transfers between devices, from_both(): lax.ppermute(head, axis, [((i + 1) % count, i) for i in range(count)])  4.94 us
  transfers between devices with their start and end apart: 12, of which 8 were waited for; matrix products, arithmetic and copies ran while one was open for 0% of the time, Pallas kernels for 8%

profile of v3, /device:TPU:64, one launch (start us, length us, event | category | flops | bytes accessed | tf_op | source)
XLA Modules:
  0.0 79.1 jit_solution(1195514598020054407)
XLA Ops:
  0.6 0.0 copy-start
  0.6 1.0 %fusion = (bf16[2,1,64,512]{3,2,1,0:T(8,128)(2,1)S(1)}, bf16[2,1,64,512]{3,2,1,0:T(8,128)(2,1)S(1)}) fusion(bf16[2,4,64,512]{3,2,1,0:T(8,128)(2,1)} %bitcast.7), kind=kLoop, calls=%fused_computation.1 | loop fusion | bytes 524288 | tf_op jit(solution)/shard_map/slice | solution.py:377
  1.7 0.0 copy-start.4
  1.7 1.9 %collective-permute-start.3 = (bf16[2,1,64,512]{3,2,1,0:T(8,128)(2,1)S(1)}, bf16[2,1,64,512]{3,2,1,0:T(8,128)(2,1)S(1)}, u32[]{:S(2)}, u32[]{:S(2)}) collective-permute-start(bf16[2,1,64,512]{3,2,1,0:T(8,128)(2,1)S(1)} %get-tuple-element.38), channel_id=1, source_target_pairs={{1,0},{2,1},{3,2},{4,3},{5,4},{6,5},{7,6},{8,7},{9,8},{10,9},{11,1... | collective-permute-start | bytes 393224 | tf_op jit(solution)/shard_map/ppermute | solution.py:38
  3.6 0.2 collective-permute-start.2
  3.8 0.0 copy-done
  3.8 0.0 copy-done.4
  3.8 0.0 copy-start.1
  3.8 0.9 %copy-done.1 = bf16[3,3,64,64]{3,2,1,0:T(8,128)(2,1)S(1)} copy-done((bf16[3,3,64,64]{3,2,1,0:T(8,128)(2,1)S(1)}, bf16[3,3,64,64]{3,2,1,0:T(8,128)(2,1)}, u32[]{:S(2)}) %copy-start.1) | copy-done | bytes 73752
  4.7 0.0 copy-start.2
  4.7 0.9 %copy-done.2 = bf16[3,3,64,64]{3,2,1,0:T(8,128)(2,1)S(1)} copy-done((bf16[3,3,64,64]{3,2,1,0:T(8,128)(2,1)S(1)}, bf16[3,3,64,64]{3,2,1,0:T(8,128)(2,1)}, u32[]{:S(2)}) %copy-start.2) | copy-done | bytes 73752
  5.6 0.0 copy-start.3
  5.6 0.9 %copy-done.3 = bf16[1,1,2,16,2048]{4,3,2,1,0:T(8,128)(2,1)S(1)} copy-done((bf16[1,1,2,16,2048]{4,3,2,1,0:T(8,128)(2,1)S(1)}, bf16[1,1,2,16,2048]{4,3,2,1,0:T(8,128)(2,1)}, u32[]{:S(2)}) %copy-start.3) | copy-done | bytes 131096
  6.5 1.1 %inner.1 = (bf16[2,192,512]{2,1,0:T(8,128)(2,1)S(1)}, f32[2,2,64,512]{3,2,1,0:T(8,128)S(1)}, bf16[512,512]{1,0:T(8,128)(2,1)S(1)}, bf16[192,192]{1,0:T(8,128)(2,...) custom-call(bf16[2,16,2048]{2,1,0:T(8,128)(2,1)S(1)} %bitcast.12, ...), custom_call_target="tpu_custom_call" | custom-call | flops 3000000000 | bytes 9000000 | tf_op jit(solution)/shard_map/inner/pallas_call | solution.py:361
  7.6 3.1 %collective-permute-start.1 = (bf16[2,192,512]{2,1,0:T(8,128)(2,1)S(1)}, bf16[2,192,512]{2,1,0:T(8,128)(2,1)S(1)}, u32[]{:S(2)}, u32[]{:S(2)}) collective-permute-start(bf16[2,192,512]{2,1,0:T(8,128)(2,1)S(1)} %get-tuple-element.21.own_ref), channel_id=1, source_target_pairs={{16,0},{32,16},{48,32},{0,48},{17,1},{33,17},{49,33},{1,49},{18,2}... | collective-permute-start | bytes 1179656 | tf_op jit(solution)/shard_map/ppermute | solution.py:38
  10.7 0.0 collective-permute-start
  10.7 0.0 collective-permute-done.3.below_ref
  10.7 1.0 %collective-permute-done.2.above_ref = bf16[2,1,64,512]{3,2,1,0:T(8,128)(2,1)S(1)} collective-permute-done((bf16[2,1,64,512]{3,2,1,0:T(8,128)(2,1)S(1)}, bf16[2,1,64,512]{3,2,1,0:T(8,128)(2,1)S(1)}, u32[]{:S(2)}, u32[]{:S(2)}) %collective-permute-start.2) | collective-permute-done | bytes 131104 | tf_op jit(solution)/shard_map/ppermute | solution.py:37
  11.7 0.5 edge.1
  12.2 3.1 %collective-permute-start.5 = (bf16[2,128,512]{2,1,0:T(8,128)(2,1)S(1)}, bf16[2,128,512]{2,1,0:T(8,128)(2,1)S(1)}, u32[]{:S(2)}, u32[]{:S(2)}) collective-permute-start(bf16[2,128,512]{2,1,0:T(8,128)(2,1)S(1)} %get-tuple-element.29.first_ref), channel_id=1, source_target_pairs={{16,0},{32,16},{48,32},{0,48},{17,1},{33,17},{49,33},{1,49},{18,2}... | collective-permute-start | bytes 786440 | tf_op jit(solution)/shard_map/ppermute | solution.py:38
  15.3 0.0 collective-permute-start.4
  15.3 4.9 %collective-permute-done.1.after_ref = bf16[2,192,512]{2,1,0:T(8,128)(2,1)S(1)} collective-permute-done((bf16[2,192,512]{2,1,0:T(8,128)(2,1)S(1)}, bf16[2,192,512]{2,1,0:T(8,128)(2,1)S(1)}, u32[]{:S(2)}, u32[]{:S(2)}) %collective-permute-start.1) | collective-permute-done | bytes 393248 | tf_op jit(solution)/shard_map/ppermute | solution.py:38
  20.3 3.7 %collective-permute-done.before_ref = bf16[2,192,512]{2,1,0:T(8,128)(2,1)S(1)} collective-permute-done((bf16[2,192,512]{2,1,0:T(8,128)(2,1)S(1)}, bf16[2,192,512]{2,1,0:T(8,128)(2,1)S(1)}, u32[]{:S(2)}, u32[]{:S(2)}) %collective-permute-start) | collective-permute-done | bytes 393248 | tf_op jit(solution)/shard_map/ppermute | solution.py:37
  24.0 3.1 %main_inner.1 = (f32[640,128]{1,0:T(8,128)S(1)}, bf16[2,64,512]{2,1,0:T(8,128)(2,1)S(1)}) custom-call(bf16[2,192,512]{2,1,0:T(8,128)(2,1)S(1)} %get-tuple-element.21.own_ref, bf16[2,192,512]{2,1,0:T(8,128)(2,1)S(1)} %collective-permute-done.before_ref, bf16[2,192,512]{2,1,0:T(8,128)(2,1)S(1)} %collective-permute-done.1.after_ref, ...), custom_call_target="tpu_custom_call" | custom-call | flops 3000000000 | bytes 9000000 | tf_op jit(solution)/shard_map/main_inner/pallas_call | solution.py:361
  27.0 0.0 collective-permute-done.5.first_after_ref
  27.0 0.6 collective-permute-done.4.first_before_ref
  27.6 3.1 %main_edge.1 = (f32[640,128]{1,0:T(8,128)S(1)}, bf16[2,64,512]{2,1,0:T(8,128)(2,1)S(1)}) custom-call(bf16[2,128,512]{2,1,0:T(8,128)(2,1)S(1)} %get-tuple-element.29.first_ref, bf16[2,128,512]{2,1,0:T(8,128)(2,1)S(1)} %collective-permute-done.4.first_before_ref, bf16[2,128,512]{2,1,0:T(8,128)(2,1)S(1)} %collective-permute-done.5.first_after_ref, ...), custom_call_target="tpu_custom_call" | custom-call | flops 3000000000 | bytes 9000000 | tf_op jit(solution)/shard_map/main_edge/pallas_call | solution.py:361
  30.7 17.1 %all_to_all.10 = f32[16,40,128]{2,1,0:T(8,128)S(1)} all-to-all(f32[16,40,128]{2,1,0:T(8,128)S(1)} %bitcast.6), channel_id=1, replica_groups=mesh['pair'=2,'core'=2,'ang'=4,'quad'=4,'x'=4] {'ang','x'}, dimensions={0} | all-to-all | bytes 655360 | tf_op jit(solution)/shard_map/all_to_all | solution.py:24
  47.8 0.3 collective-permute-start.6
  48.1 1.2 %collective-permute-done.6 = f32[40,128]{1,0:T(8,128)S(1)} collective-permute-done((f32[40,128]{1,0:T(8,128)S(1)}, f32[40,128]{1,0:T(8,128)S(1)}, u32[]{:S(2)}, u32[]{:S(2)}) %collective-permute-start.6) | collective-permute-done | bytes 20512 | tf_op jit(solution)/shard_map/ppermute | solution.py:18
  49.3 1.9 %collective-permute-start.7 = (f32[40,128]{1,0:T(8,128)S(1)}, f32[40,128]{1,0:T(8,128)S(1)}, u32[]{:S(2)}, u32[]{:S(2)}) collective-permute-start(f32[40,128]{1,0:T(8,128)S(1)} %add.15), channel_id=1, source_target_pairs={{0,128},{128,0},{1,129},{129,1},{2,130},{130,2},{3,131},{131,3},{4... | collective-permute-start | bytes 61448 | tf_op jit(solution)/shard_map/ppermute | solution.py:18
  51.2 1.9 %collective-permute-done.7 = f32[40,128]{1,0:T(8,128)S(1)} collective-permute-done((f32[40,128]{1,0:T(8,128)S(1)}, f32[40,128]{1,0:T(8,128)S(1)}, u32[]{:S(2)}, u32[]{:S(2)}) %collective-permute-start.7) | collective-permute-done | bytes 20512 | tf_op jit(solution)/shard_map/ppermute | solution.py:18
  53.1 0.8 %collective-permute-start.10 = (f32[40,128]{1,0:T(8,128)S(1)}, f32[40,128]{1,0:T(8,128)S(1)}, u32[]{:S(2)}, u32[]{:S(2)}) collective-permute-start(f32[40,128]{1,0:T(8,128)S(1)} %add.16), channel_id=1, source_target_pairs={{0,12},{4,0},{8,4},{12,8},{1,13},{5,1},{9,5},{13,9},{2,14},{6,2},{... | collective-permute-start | bytes 61448 | tf_op jit(solution)/shard_map/ppermute | solution.py:18
  53.9 3.3 %collective-permute-start.9 = (f32[40,128]{1,0:T(8,128)S(1)}, f32[40,128]{1,0:T(8,128)S(1)}, u32[]{:S(2)}, u32[]{:S(2)}) collective-permute-start(f32[40,128]{1,0:T(8,128)S(1)} %add.16), channel_id=1, source_target_pairs={{0,4},{4,8},{8,12},{12,0},{1,5},{5,9},{9,13},{13,1},{2,6},{6,10},{... | collective-permute-start | bytes 61448 | tf_op jit(solution)/shard_map/ppermute | solution.py:18
  57.2 5.4 %collective-permute-start.8 = (f32[40,128]{1,0:T(8,128)S(1)}, f32[40,128]{1,0:T(8,128)S(1)}, u32[]{:S(2)}, u32[]{:S(2)}) collective-permute-start(f32[40,128]{1,0:T(8,128)S(1)} %add.16), channel_id=1, source_target_pairs={{0,8},{4,12},{8,0},{12,4},{1,9},{5,13},{9,1},{13,5},{2,10},{6,14},... | collective-permute-start | bytes 61448 | tf_op jit(solution)/shard_map/ppermute | solution.py:18
  62.6 0.0 collective-permute-done.10
  62.6 0.0 collective-permute-done.9
  62.6 2.3 %collective-permute-done.8 = f32[40,128]{1,0:T(8,128)S(1)} collective-permute-done((f32[40,128]{1,0:T(8,128)S(1)}, f32[40,128]{1,0:T(8,128)S(1)}, u32[]{:S(2)}, u32[]{:S(2)}) %collective-permute-start.8) | collective-permute-done | bytes 20512 | tf_op jit(solution)/shard_map/ppermute | solution.py:18
  64.9 0.8 broadcast_in_dim.2
  65.7 3.5 %all-to-all-start.1 = ((f32[16,40,128]{2,1,0:T(8,128)}), f32[16,40,128]{2,1,0:T(8,128)S(1)}, u32[]{:S(2)}, u32[]{:S(2)}) async-start(f32[16,40,128]{2,1,0:T(8,128)} %broadcast_in_dim.2), calls=%async_computation.1 | async-start | bytes 655360 | tf_op jit(solution)/shard_map/all_to_all | solution.py:32
  69.2 1.4 %weave.1 = bf16[2,16,2048]{2,1,0:T(8,128)(2,1)} custom-call(bf16[2,64,512]{2,1,0:T(8,128)(2,1)S(1)} %get-tuple-element.27.inner_ref, bf16[2,64,512]{2,1,0:T(8,128)(2,1)S(1)} %get-tuple-element.32.edge_ref, bf16[512,512]{1,0:T(8,128)(2,1)S(1)} %get-tuple-element.33.deal_ref), custom_call_target="tpu_custom_call" | custom-call | flops 3000000000 | bytes 9000000 | tf_op jit(solution)/shard_map/weave/pallas_call | solution.py:361
  70.6 7.6 %all-to-all-done.1 = f32[16,40,128]{2,1,0:T(8,128)S(1)} async-done(((f32[16,40,128]{2,1,0:T(8,128)}), f32[16,40,128]{2,1,0:T(8,128)S(1)}, u32[]{:S(2)}, u32[]{:S(2)}) %all-to-all-start.1) | async-done | bytes 327712 | tf_op jit(solution)/shard_map/all_to_all | solution.py:32
  78.2 0.9 %unpack.1 = (f32[3,3,64,64]{3,2,1,0:T(8,128)}, f32[3,3,64,64]{3,2,1,0:T(8,128)}, f32[16,64]{1,0:T(8,128)}) custom-call(f32[640,128]{1,0:T(8,128)S(1)} %bitcast.5), custom_call_target="tpu_custom_call" | custom-call | flops 3000000000 | bytes 9000000 | tf_op jit(solution)/shard_map/unpack/pallas_call | solution.py:361
  (4 shorter events, 0.0 us)
Async XLA Ops:
  0.6 3.2 %copy-start = (bf16[1,1,2,4,64,512]{5,4,3,2,1,0:T(8,128)(2,1)S(1)}, bf16[1,1,2,4,64,512]{5,4,3,2,1,0:T(8,128)(2,1)}, u32[]{:S(2)}) copy-start(bf16[1,1,2,4,64,512]{5,4,3,2,1,0:T(8,128)(2,1)} %param.5) | copy-start | bytes 1572868
  1.7 2.1 %copy-start.4 = (bf16[16,64]{1,0:T(8,128)(2,1)S(1)}, bf16[16,64]{1,0:T(8,128)(2,1)}, u32[]{:S(2)}) copy-start(bf16[16,64]{1,0:T(8,128)(2,1)} %up_ref.1) | copy-start | bytes 6148
  1.7 9.0 %collective-permute-start.3 = (bf16[2,1,64,512]{3,2,1,0:T(8,128)(2,1)S(1)}, bf16[2,1,64,512]{3,2,1,0:T(8,128)(2,1)S(1)}, u32[]{:S(2)}, u32[]{:S(2)}) collective-permute-start(bf16[2,1,64,512]{3,2,1,0:T(8,128)(2,1)S(1)} %get-tuple-element.38), channel_id=1, source_target_pairs={{1,0},{2,1},{3,2},{4,3},{5,4},{6,5},{7,6},{8,7},{9,8},{10,9},{11,1... | collective-permute-start | bytes 393224 | tf_op jit(solution)/shard_map/ppermute | solution.py:38
  3.6 8.1 %collective-permute-start.2 = (bf16[2,1,64,512]{3,2,1,0:T(8,128)(2,1)S(1)}, bf16[2,1,64,512]{3,2,1,0:T(8,128)(2,1)S(1)}, u32[]{:S(2)}, u32[]{:S(2)}) collective-permute-start(bf16[2,1,64,512]{3,2,1,0:T(8,128)(2,1)S(1)} %get-tuple-element.39), channel_id=1, source_target_pairs={{0,1},{1,2},{2,3},{3,4},{4,5},{5,6},{6,7},{7,8},{8,9},{9,10},{10,1... | collective-permute-start | bytes 393224 | tf_op jit(solution)/shard_map/ppermute | solution.py:37
  3.8 0.9 %copy-start.1 = (bf16[3,3,64,64]{3,2,1,0:T(8,128)(2,1)S(1)}, bf16[3,3,64,64]{3,2,1,0:T(8,128)(2,1)}, u32[]{:S(2)}) copy-start(bf16[3,3,64,64]{3,2,1,0:T(8,128)(2,1)} %spatial_ref.1) | copy-start | bytes 221188
  4.7 0.9 %copy-start.2 = (bf16[3,3,64,64]{3,2,1,0:T(8,128)(2,1)S(1)}, bf16[3,3,64,64]{3,2,1,0:T(8,128)(2,1)}, u32[]{:S(2)}) copy-start(bf16[3,3,64,64]{3,2,1,0:T(8,128)(2,1)} %epi_ref.1) | copy-start | bytes 221188
  5.6 0.9 %copy-start.3 = (bf16[1,1,2,16,2048]{4,3,2,1,0:T(8,128)(2,1)S(1)}, bf16[1,1,2,16,2048]{4,3,2,1,0:T(8,128)(2,1)}, u32[]{:S(2)}) copy-start(bf16[1,1,2,16,2048]{4,3,2,1,0:T(8,128)(2,1)} %param.9) | copy-start | bytes 393220
  7.6 12.7 %collective-permute-start.1 = (bf16[2,192,512]{2,1,0:T(8,128)(2,1)S(1)}, bf16[2,192,512]{2,1,0:T(8,128)(2,1)S(1)}, u32[]{:S(2)}, u32[]{:S(2)}) collective-permute-start(bf16[2,192,512]{2,1,0:T(8,128)(2,1)S(1)} %get-tuple-element.21.own_ref), channel_id=1, source_target_pairs={{16,0},{32,16},{48,32},{0,48},{17,1},{33,17},{49,33},{1,49},{18,2}... | collective-permute-start | bytes 1179656 | tf_op jit(solution)/shard_map/ppermute | solution.py:38
  10.7 13.3 %collective-permute-start = (bf16[2,192,512]{2,1,0:T(8,128)(2,1)S(1)}, bf16[2,192,512]{2,1,0:T(8,128)(2,1)S(1)}, u32[]{:S(2)}, u32[]{:S(2)}) collective-permute-start(bf16[2,192,512]{2,1,0:T(8,128)(2,1)S(1)} %get-tuple-element.21.own_ref), channel_id=1, source_target_pairs={{0,16},{16,32},{32,48},{48,0},{1,17},{17,33},{33,49},{49,1},{2,18}... | collective-permute-start | bytes 1179656 | tf_op jit(solution)/shard_map/ppermute | solution.py:37
  12.2 14.8 %collective-permute-start.5 = (bf16[2,128,512]{2,1,0:T(8,128)(2,1)S(1)}, bf16[2,128,512]{2,1,0:T(8,128)(2,1)S(1)}, u32[]{:S(2)}, u32[]{:S(2)}) collective-permute-start(bf16[2,128,512]{2,1,0:T(8,128)(2,1)S(1)} %get-tuple-element.29.first_ref), channel_id=1, source_target_pairs={{16,0},{32,16},{48,32},{0,48},{17,1},{33,17},{49,33},{1,49},{18,2}... | collective-permute-start | bytes 786440 | tf_op jit(solution)/shard_map/ppermute | solution.py:38
  15.3 12.3 %collective-permute-start.4 = (bf16[2,128,512]{2,1,0:T(8,128)(2,1)S(1)}, bf16[2,128,512]{2,1,0:T(8,128)(2,1)S(1)}, u32[]{:S(2)}, u32[]{:S(2)}) collective-permute-start(bf16[2,128,512]{2,1,0:T(8,128)(2,1)S(1)} %get-tuple-element.29.first_ref), channel_id=1, source_target_pairs={{0,16},{16,32},{32,48},{48,0},{1,17},{17,33},{33,49},{49,1},{2,18}... | collective-permute-start | bytes 786440 | tf_op jit(solution)/shard_map/ppermute | solution.py:37
  47.8 1.5 %collective-permute-start.6 = (f32[40,128]{1,0:T(8,128)S(1)}, f32[40,128]{1,0:T(8,128)S(1)}, u32[]{:S(2)}, u32[]{:S(2)}) collective-permute-start(f32[40,128]{1,0:T(8,128)S(1)} %reduce_sum.9), channel_id=1, source_target_pairs={{0,64},{64,0},{1,65},{65,1},{2,66},{66,2},{3,67},{67,3},{4,68},{68... | collective-permute-start | bytes 61448 | tf_op jit(solution)/shard_map/ppermute | solution.py:18
  49.3 3.8 %collective-permute-start.7 = (f32[40,128]{1,0:T(8,128)S(1)}, f32[40,128]{1,0:T(8,128)S(1)}, u32[]{:S(2)}, u32[]{:S(2)}) collective-permute-start(f32[40,128]{1,0:T(8,128)S(1)} %add.15), channel_id=1, source_target_pairs={{0,128},{128,0},{1,129},{129,1},{2,130},{130,2},{3,131},{131,3},{4... | collective-permute-start | bytes 61448 | tf_op jit(solution)/shard_map/ppermute | solution.py:18
  53.1 9.5 %collective-permute-start.10 = (f32[40,128]{1,0:T(8,128)S(1)}, f32[40,128]{1,0:T(8,128)S(1)}, u32[]{:S(2)}, u32[]{:S(2)}) collective-permute-start(f32[40,128]{1,0:T(8,128)S(1)} %add.16), channel_id=1, source_target_pairs={{0,12},{4,0},{8,4},{12,8},{1,13},{5,1},{9,5},{13,9},{2,14},{6,2},{... | collective-permute-start | bytes 61448 | tf_op jit(solution)/shard_map/ppermute | solution.py:18
  53.9 8.7 %collective-permute-start.9 = (f32[40,128]{1,0:T(8,128)S(1)}, f32[40,128]{1,0:T(8,128)S(1)}, u32[]{:S(2)}, u32[]{:S(2)}) collective-permute-start(f32[40,128]{1,0:T(8,128)S(1)} %add.16), channel_id=1, source_target_pairs={{0,4},{4,8},{8,12},{12,0},{1,5},{5,9},{9,13},{13,1},{2,6},{6,10},{... | collective-permute-start | bytes 61448 | tf_op jit(solution)/shard_map/ppermute | solution.py:18
  57.2 7.7 %collective-permute-start.8 = (f32[40,128]{1,0:T(8,128)S(1)}, f32[40,128]{1,0:T(8,128)S(1)}, u32[]{:S(2)}, u32[]{:S(2)}) collective-permute-start(f32[40,128]{1,0:T(8,128)S(1)} %add.16), channel_id=1, source_target_pairs={{0,8},{4,12},{8,0},{12,4},{1,9},{5,13},{9,1},{13,5},{2,10},{6,14},... | collective-permute-start | bytes 61448 | tf_op jit(solution)/shard_map/ppermute | solution.py:18
  65.7 12.6 %all-to-all-start.1 = ((f32[16,40,128]{2,1,0:T(8,128)}), f32[16,40,128]{2,1,0:T(8,128)S(1)}, u32[]{:S(2)}, u32[]{:S(2)}) async-start(f32[16,40,128]{2,1,0:T(8,128)} %broadcast_in_dim.2), calls=%async_computation.1 | async-start | bytes 655360 | tf_op jit(solution)/shard_map/all_to_all | solution.py:32

commit v4 on v3

--- a/solution.py
+++ b/solution.py
@@ -26,17 +26,22 @@
     ).sum(0)
     for axis in ("core", "pair"):
         mine = mine + swapped(mine, axis, 1)
-    one, two, three = (swapped(mine, "quad", step) for step in (1, 2, 3))
-    mine = (mine + two) + (one + three)
-    spread = jnp.broadcast_to(mine[None], (16,) + mine.shape)
+    for flip in (1, 3):
+        mine = mine + lax.ppermute(mine, "quad", [(i, i ^ flip) for i in range(4)])
+    spread = jnp.broadcast_to(mine.astype(BF16)[None], (16,) + mine.shape)
     return lax.all_to_all(spread, plane, split_axis=0, concat_axis=0, tiled=True).reshape(rows, 128)
 
 
-def from_both(head, tail, axis):
+def is_even(axis):
+    return lax.axis_index(axis) % 2 == 0
+
+
+def with_next_and_before(first_send, second_send, axis):
     count = lax.axis_size(axis)
-    before = lax.ppermute(tail, axis, [(i, (i + 1) % count) for i in range(count)])
-    after = lax.ppermute(head, axis, [((i + 1) % count, i) for i in range(count)])
-    return before, after
+    odd = [(i, (i + 1) % count) for i in range(1, count, 2)]
+    two = lax.ppermute(second_send, axis, odd + [(j, i) for i, j in odd])
+    one = lax.ppermute(first_send, axis, [(i, i ^ 1) for i in range(count)])
+    return one, two
 
 
 def has_neighbours(axis, count):
@@ -44,8 +49,16 @@
     return place > 0, place < count - 1
 
 
-def kept(flag, values):
-    return jnp.where(flag, values, jnp.zeros_like(values))
+def chosen(flags, one, two):
+    even, present = flags
+    values = jnp.where(even, one, two)
+    return jnp.where(present, values, jnp.zeros_like(values))
+
+
+def sides(axis, count):
+    even = is_even(axis)
+    before, after = has_neighbours(axis, count)
+    return (jnp.logical_not(even), before), (even, after)
 
 
 def column(shape):
@@ -124,11 +137,11 @@
 
 
 def inner_kernel(
-    image_ref,
-    light_ref,
-    spatial_ref,
-    epi_ref,
-    up_ref,
+    image_hbm,
+    light_hbm,
+    spatial_hbm,
+    epi_hbm,
+    up_hbm,
     mixed_ref,
     out_ref,
     deal_ref,
@@ -137,10 +150,28 @@
     back_ref,
     lift_ref,
     drop_ref,
+    light_ref,
+    one_ref,
+    two_ref,
+    image_ref,
+    spatial_ref,
+    epi_ref,
+    up_ref,
+    sems,
 ):
-    prepare_weights(
-        spatial_ref, epi_ref, up_ref, weight_ref, epi_taps_ref, back_ref, lift_ref, drop_ref
-    )
+    pairs = (
+        (spatial_hbm, spatial_ref),
+        (image_hbm, image_ref),
+        (light_hbm, light_ref),
+        (epi_hbm, epi_ref),
+        (up_hbm, up_ref),
+    )
+    copies = [
+        pltpu.make_async_copy(source, target, sems.at[place])
+        for place, (source, target) in enumerate(pairs)
+    ]
+    for copy in copies:
+        copy.start()
     size = deal_ref.shape[0]
     source = lax.broadcasted_iota(jnp.int32, (size, size), 0)
     target = lax.broadcasted_iota(jnp.int32, (size, size), 1)
@@ -149,6 +180,16 @@
     deal = jnp.where(source == wanted, 1.0, 0.0).astype(BF16)
     deal_ref[...] = deal
     chans = light_ref.shape[2]
+    for copy in copies:
+        copy.wait()
+    even = is_even(ROWS)
+    last = light_ref.shape[1] - 1
+    for view in range(2):
+        one_ref[view, 0] = jnp.where(even, light_ref[view, last], light_ref[view, 0])
+        two_ref[view, 0] = jnp.where(even, light_ref[view, 0], light_ref[view, last])
+    prepare_weights(
+        spatial_ref, epi_ref, up_ref, weight_ref, epi_taps_ref, back_ref, lift_ref, drop_ref
+    )
     for block in range(image_ref.shape[2] // size):
         cut = slice(block * size, (block + 1) * size)
         stacked = jnp.concatenate([image_ref[0, :, cut], image_ref[1, :, cut]], axis=0)
@@ -169,15 +210,15 @@
             mixed_ref[view, slot * chans : (slot + 1) * chans] = first.astype(BF16)
 
 
-def edge_kernel(light_ref, above_ref, below_ref, weight_ref, first_ref, out_ref):
+def edge_kernel(light_ref, one_ref, two_ref, weight_ref, first_ref, out_ref):
     chans = light_ref.shape[2]
-    has_above, has_below = has_neighbours(ROWS, 16)
+    above, below = sides(ROWS, 16)
     for view in range(2):
         for slot, h in enumerate((0, 3)):
             if slot == 0:
-                stacked = [kept(has_above, above_ref[view, 0]), light_ref[view, 0], light_ref[view, 1]]
+                stacked = [chosen(above, one_ref[view, 0], two_ref[view, 0]), light_ref[view, 0], light_ref[view, 1]]
             else:
-                stacked = [light_ref[view, 2], light_ref[view, 3], kept(has_below, below_ref[view, 0])]
+                stacked = [light_ref[view, 2], light_ref[view, 3], chosen(below, one_ref[view, 0], two_ref[view, 0])]
             total = conv_taps(weight_ref[...], jnp.concatenate(stacked, axis=0), True)
             out_ref[view, slot] = total
             first = light_ref[view, h].astype(F32) + total * gate_of(total)
@@ -190,13 +231,13 @@
     lifted = [None, None]
     up_total = None
     epi_left, epi_right, spatial_left, spatial_right = [], [], [], []
-    has_before, has_after = has_neighbours("ang", 4)
+    before, after = sides("ang", 4)
     for slot, h in enumerate(rows):
         cut = slice(slot * chans, (slot + 1) * chans)
         stack = jnp.concatenate(
-            [kept(has_before, firsts[0][v, cut]) for v in range(2)]
-            + [firsts[1][v, cut] for v in range(2)]
-            + [kept(has_after, firsts[2][v, cut]) for v in range(2)],
+            [chosen(before, firsts[1][v, cut], firsts[2][v, cut]) for v in range(2)]
+            + [firsts[0][v, cut] for v in range(2)]
+            + [chosen(after, firsts[1][v, cut], firsts[2][v, cut]) for v in range(2)],
             axis=0,
         )
         here = (lax.broadcasted_iota(jnp.int32, (64, chans), 0) % 16) // 4 == h
@@ -245,26 +286,26 @@
         start = end
 
 
-def dealt_views(own_ref, before_ref, after_ref, chans):
-    has_before, has_after = has_neighbours("ang", 4)
+def dealt_views(own_ref, one_ref, two_ref, chans):
+    before, after = sides("ang", 4)
     return [
-        kept(has_before, before_ref[1, 2 * chans :]),
+        chosen(before, one_ref[1, 2 * chans :], two_ref[1, 2 * chans :]),
         own_ref[0, 2 * chans :],
         own_ref[1, 2 * chans :],
-        kept(has_after, after_ref[0, 2 * chans :]),
+        chosen(after, one_ref[0, 2 * chans :], two_ref[0, 2 * chans :]),
     ]
 
 
 def main_inner_kernel(
-    own_ref, before_ref, after_ref, light_ref, out_ref, epi_ref, back_ref, lift_ref, drop_ref, pay_ref, lift_out
+    own_ref, mixed_one_ref, mixed_two_ref, light_ref, out_ref, epi_ref, back_ref, lift_ref, drop_ref, pay_ref, lift_out
 ):
     def near(v, h):
         return [light_ref[v, h + k] for k in (-1, 0, 1)]
 
     main_rows(
         (1, 2),
-        (before_ref, own_ref, after_ref),
-        dealt_views(own_ref, before_ref, after_ref, light_ref.shape[2]),
+        (own_ref, mixed_one_ref, mixed_two_ref),
+        dealt_views(own_ref, mixed_one_ref, mixed_two_ref, light_ref.shape[2]),
         near,
         out_ref,
         epi_ref,
@@ -278,14 +319,14 @@
 
 def main_edge_kernel(
     first_ref,
-    first_before_ref,
-    first_after_ref,
+    first_one_ref,
+    first_two_ref,
     own_ref,
-    before_ref,
-    after_ref,
+    mixed_one_ref,
+    mixed_two_ref,
     light_ref,
-    above_ref,
-    below_ref,
+    one_ref,
+    two_ref,
     out_ref,
     epi_ref,
     back_ref,
@@ -295,17 +336,17 @@
     pay_ref,
     lift_out,
 ):
-    has_above, has_below = has_neighbours(ROWS, 16)
+    above, below = sides(ROWS, 16)
 
     def near(v, h):
         if h == 0:
-            return [kept(has_above, above_ref[v, 0]), light_ref[v, 0], light_ref[v, 1]]
-        return [light_ref[v, 2], light_ref[v, 3], kept(has_below, below_ref[v, 0])]
+            return [chosen(above, one_ref[v, 0], two_ref[v, 0]), light_ref[v, 0], light_ref[v, 1]]
+        return [light_ref[v, 2], light_ref[v, 3], chosen(below, one_ref[v, 0], two_ref[v, 0])]
 
     main_rows(
         (0, 3),
-        (first_before_ref, first_ref, first_after_ref),
-        dealt_views(own_ref, before_ref, after_ref, light_ref.shape[2]),
+        (first_ref, first_one_ref, first_two_ref),
+        dealt_views(own_ref, mixed_one_ref, mixed_two_ref, light_ref.shape[2]),
         near,
         out_ref,
         epi_ref,
@@ -338,7 +379,8 @@
             up_ref[v, :, block * size : (block + 1) * size] = woven[v * 16 : (v + 1) * 16]
 
 
-def unpack_kernel(pay_ref, spatial_ref, epi_ref, up_ref):
+def unpack_kernel(sent_ref, spatial_ref, epi_ref, up_ref, pay_ref):
+    pay_ref[...] = sent_ref[...].astype(F32)
     chans = spatial_ref.shape[2]
     three = 3 * chans
     for which, ref in enumerate((spatial_ref, epi_ref)):
@@ -357,31 +399,51 @@
             up_ref[4 * p + q : 4 * p + q + 1, :] = total
 
 
-def local_call(kernel, shapes, name, *operands, micros=3):
+def local_call(kernel, shapes, name, *operands, micros=3, loose=(), scratch=()):
+    operands = [
+        pltpu.with_memory_space_constraint(operand, pltpu.HBM if place in loose else pltpu.VMEM)
+        for place, operand in enumerate(operands)
+    ]
     return pl.pallas_call(
         kernel,
         out_shape=shapes,
+        scratch_shapes=scratch,
+        in_specs=[
+            pl.BlockSpec(memory_space=pltpu.HBM if place in loose else pltpu.VMEM)
+            for place in range(len(operands))
+        ],
         cost_estimate=pl.CostEstimate(
             flops=micros * 1_000_000_000, bytes_accessed=micros * 3_000_000, transcendentals=0
         ),
         compiler_params=pltpu.CompilerParams(vmem_limit_bytes=VMEM_LIMIT),
         name=name,
-    )(*(pltpu.with_memory_space_constraint(operand, pltpu.VMEM) for operand in operands))
+    )(*operands)
 
 
 def on_device(light_field, spatial_weight, epi_weight, upsample_weight, image_grad):
     _, _, views, rows, chans, breadth = light_field.shape
     light = light_field.reshape(views, rows, chans, breadth)
     image = image_grad.reshape(views, image_grad.shape[3], image_grad.shape[4])
-
-    above, below = from_both(light[:, :1], light[:, rows - 1 :], ROWS)
 
     three = 3 * chans
     like = pltpu.VMEM
     plain = jax.ShapeDtypeStruct
     half_out = like((views, 2, chans, breadth), F32)
     taps = like((three, three), BF16)
-    mixed, inner_out, deal, spatial_taps, epi_taps, back_taps, lift, drop = local_call(
+    edge_line = like((views, 1, chans, breadth), BF16)
+    (
+        mixed,
+        inner_out,
+        deal,
+        spatial_taps,
+        epi_taps,
+        back_taps,
+        lift,
+        drop,
+        light_here,
+        send_one,
+        send_two,
+    ) = local_call(
         inner_kernel,
         (
             like((views, 2 * chans + 64, breadth), BF16),
@@ -392,6 +454,9 @@
             taps,
             like((rows, 64, chans), BF16),
             like((rows, chans, 64), BF16),
+            like(light.shape, BF16),
+            edge_line,
+            edge_line,
         ),
         "inner",
         image,
@@ -399,18 +464,28 @@
         spatial_weight,
         epi_weight,
         upsample_weight,
-    )
-    mixed_before, mixed_after = from_both(mixed, mixed, "ang")
+        loose=(0, 1, 2, 3, 4),
+        scratch=[
+            pltpu.VMEM(image.shape, BF16),
+            pltpu.VMEM(spatial_weight.shape, BF16),
+            pltpu.VMEM(epi_weight.shape, BF16),
+            pltpu.VMEM(upsample_weight.shape, BF16),
+            pltpu.SemaphoreType.DMA((5,)),
+        ],
+    )
+    light = light_here
+    line_one, line_two = with_next_and_before(send_one, send_two, ROWS)
+    mixed_one, mixed_two = with_next_and_before(mixed, mixed, "ang")
     first, edge_out = local_call(
         edge_kernel,
         (like((views, 2 * chans, breadth), BF16), half_out),
         "edge",
         light,
-        above,
-        below,
+        line_one,
+        line_two,
         spatial_taps,
     )
-    first_before, first_after = from_both(first, first, "ang")
+    first_one, first_two = with_next_and_before(first, first, "ang")
 
     weights = (epi_taps, back_taps, lift, drop)
     lift_half = like((views, 64, breadth), BF16)
@@ -420,8 +495,8 @@
         (whole_pay, lift_half),
         "main_inner",
         mixed,
-        mixed_before,
-        mixed_after,
+        mixed_one,
+        mixed_two,
         light,
         inner_out,
         *weights,
@@ -431,14 +506,14 @@
         (whole_pay, lift_half),
         "main_edge",
         first,
-        first_before,
-        first_after,
+        first_one,
+        first_two,
         mixed,
-        mixed_before,
-        mixed_after,
+        mixed_one,
+        mixed_two,
         light,
-        above,
-        below,
+        line_one,
+        line_two,
         edge_out,
         *weights,
         inner_pay,
@@ -455,6 +530,7 @@
         ),
         "unpack",
         sum_everywhere(pay),
+        scratch=[pltpu.VMEM((640, 128), F32)],
     )
     return (up.reshape(image_grad.shape), spatial_grad, epi_grad, up_grad)
 

time: 80.7 us -> 74 us (0.917); the launches traced: 79.1 us -> 73.4 us
  starting transfers between devices: 23.5 us -> 17.3 us
  local copies, waits for them, and re-layouts: 4.54 us -> 0.69 us
  waiting for transfers between devices: 23.2 us -> 26.4 us
  Pallas kernels: 9.99 us -> 11.2 us
    ppermute x5 -> x2, starting transfers between devices: 11.7 us -> 1.11 us  [swapped(): lax.ppermute(value, axis, [(i, (i + step) % count) for i in range(count)])]
    ppermute x6 -> x8, waiting for transfers between devices: 10.2 us -> 15.7 us  [the longest x2 7.05 us: sum_everywhere(): mine = mine + lax.ppermute(mine, 'quad', [(i, i ^ flip) for i in range(4)])]
    ppermute x6 -> x8, starting transfers between devices: 8.29 us -> 12.7 us  [the longest x3 7.29 us: with_next_and_before(): two = lax.ppermute(second_send, axis, odd + [(j, i) for i, j in odd])]
    unnamed x10 -> x0, local copies, waits for them, and re-layouts: 2.73 us -> none
    ppermute x5 -> x2, waiting for transfers between devices: 5.35 us -> 3.95 us  [swapped(): lax.ppermute(value, axis, [(i, (i + step) % count) for i in range(count)])]
    pallas_call x6, Pallas kernels: 9.99 us -> 11.2 us  [local_call(): pl.pallas_call(kernel, out_shape=shapes, scratch_shapes=scratch, in_specs...]
    slice x1 -> x0, local copies, waits for them, and re-layouts: 1.05 us -> none  [on_device(): above, below = from_both(light[:, :1], light[:, rows - 1:], ROWS)]
    all_to_all x1, waiting for transfers between devices: 7.64 us -> 6.76 us  [sum_everywhere(): lax.all_to_all(spread, plane, split_axis=0, concat_axis=0, tiled=True)]
  transfers between devices with their start and end apart: 12 -> 11, of which waited for: 8 -> 9; matrix products, arithmetic and copies ran while one was open for 0% -> 0% of each run, Pallas kernels for 8% -> 7%
where the time goes in v4:
time: 74 us; the launch traced here: 73.4 us
  waiting for transfers between devices  26.4 us (36%)
  starting transfers between devices  17.3 us (23%)
  blocking collectives  17.1 us (23%)
  Pallas kernels  11.2 us (15%)
    all_to_all x1, blocking collectives, sum_everywhere(): lax.all_to_all(pay.reshape(16, rows // 16, 128), plane, split_axis=0, con...  17.1 us
    pallas_call x6, Pallas kernels, local_call(): pl.pallas_call(kernel, out_shape=shapes, scratch_shapes=scratch, in_specs...  11.2 us
    ppermute x3, starting transfers between devices, with_next_and_before(): two = lax.ppermute(second_send, axis, odd + [(j, i) for i, j in odd])  7.29 us
    ppermute x2, waiting for transfers between devices, sum_everywhere(): mine = mine + lax.ppermute(mine, 'quad', [(i, i ^ flip) for i in range(4)])  7.05 us
    all_to_all x1, waiting for transfers between devices, sum_everywhere(): lax.all_to_all(spread, plane, split_axis=0, concat_axis=0, tiled=True)  6.76 us
    ppermute x3, waiting for transfers between devices, with_next_and_before(): two = lax.ppermute(second_send, axis, odd + [(j, i) for i, j in odd])  6.34 us
    ppermute x2, waiting for transfers between devices, swapped(): lax.ppermute(value, axis, [(i, (i + step) % count) for i in range(count)])  3.95 us
    ppermute x2, starting transfers between devices, sum_everywhere(): mine = mine + lax.ppermute(mine, 'quad', [(i, i ^ flip) for i in range(4)])  3.52 us
  transfers between devices with their start and end apart: 11, of which 9 were waited for; matrix products, arithmetic and copies ran while one was open for 0% of the time, Pallas kernels for 7%

profile of v4, /device:TPU:64, one launch (start us, length us, event | category | flops | bytes accessed | tf_op | source)
XLA Modules:
  0.0 73.4 jit_solution(8969139351054240525)
XLA Ops:
  0.6 2.3 %inner.1 = (bf16[2,192,512]{2,1,0:T(8,128)(2,1)S(1)}, f32[2,2,64,512]{3,2,1,0:T(8,128)S(1)}, bf16[512,512]{1,0:T(8,128)(2,1)S(1)}, bf16[192,192]{1,0:T(8,128)(2,...) custom-call(bf16[2,16,2048]{2,1,0:T(8,128)(2,1)} %bitcast.8, ...), custom_call_target="tpu_custom_call" | custom-call | flops 3000000000 | bytes 9000000 | tf_op jit(solution)/shard_map/inner/pallas_call | solution.py:407
  2.9 1.6 %collective-permute-start.2 = (bf16[2,1,64,512]{3,2,1,0:T(8,128)(2,1)S(1)}, bf16[2,1,64,512]{3,2,1,0:T(8,128)(2,1)S(1)}, u32[]{:S(2)}, u32[]{:S(2)}) collective-permute-start(bf16[2,1,64,512]{3,2,1,0:T(8,128)(2,1)S(1)} %get-tuple-element.32), channel_id=1, source_target_pairs={{0,1},{1,0},{2,3},{3,2},{4,5},{5,4},{6,7},{7,6},{8,9},{9,8},{10,11... | collective-permute-start | bytes 393224 | tf_op jit(solution)/shard_map/ppermute | solution.py:43
  4.5 1.2 %collective-permute-start.3 = (bf16[2,1,64,512]{3,2,1,0:T(8,128)(2,1)S(1)}, bf16[2,1,64,512]{3,2,1,0:T(8,128)(2,1)S(1)}, u32[]{:S(2)}, u32[]{:S(2)}) collective-permute-start(bf16[2,1,64,512]{3,2,1,0:T(8,128)(2,1)S(1)} %get-tuple-element.33), channel_id=1, source_target_pairs={{1,2},{3,4},{5,6},{7,8},{9,10},{11,12},{13,14},{15,0},{2,1},{4,3},... | collective-permute-start | bytes 393224 | tf_op jit(solution)/shard_map/ppermute | solution.py:42
  5.7 3.0 %collective-permute-start.1 = (bf16[2,192,512]{2,1,0:T(8,128)(2,1)S(1)}, bf16[2,192,512]{2,1,0:T(8,128)(2,1)S(1)}, u32[]{:S(2)}, u32[]{:S(2)}) collective-permute-start(bf16[2,192,512]{2,1,0:T(8,128)(2,1)S(1)} %get-tuple-element.24.own_ref), channel_id=1, source_target_pairs={{16,32},{48,0},{32,16},{0,48},{17,33},{49,1},{33,17},{1,49},{18,34... | collective-permute-start | bytes 1179656 | tf_op jit(solution)/shard_map/ppermute | solution.py:42
  8.7 0.1 collective-permute-start
  8.8 0.0 collective-permute-done.2.one_ref
  8.8 4.3 %collective-permute-done.3.two_ref = bf16[2,1,64,512]{3,2,1,0:T(8,128)(2,1)S(1)} collective-permute-done((bf16[2,1,64,512]{3,2,1,0:T(8,128)(2,1)S(1)}, bf16[2,1,64,512]{3,2,1,0:T(8,128)(2,1)S(1)}, u32[]{:S(2)}, u32[]{:S(2)}) %collective-permute-start.3) | collective-permute-done | bytes 131104 | tf_op jit(solution)/shard_map/ppermute | solution.py:42
  13.1 0.5 edge.1
  13.7 3.1 %collective-permute-start.5 = (bf16[2,128,512]{2,1,0:T(8,128)(2,1)S(1)}, bf16[2,128,512]{2,1,0:T(8,128)(2,1)S(1)}, u32[]{:S(2)}, u32[]{:S(2)}) collective-permute-start(bf16[2,128,512]{2,1,0:T(8,128)(2,1)S(1)} %get-tuple-element.35.first_ref), channel_id=1, source_target_pairs={{16,32},{48,0},{32,16},{0,48},{17,33},{49,1},{33,17},{1,49},{18,34... | collective-permute-start | bytes 786440 | tf_op jit(solution)/shard_map/ppermute | solution.py:42
  16.7 0.1 collective-permute-start.4
  16.9 2.1 %collective-permute-done.1.mixed_two_ref = bf16[2,192,512]{2,1,0:T(8,128)(2,1)S(1)} collective-permute-done((bf16[2,192,512]{2,1,0:T(8,128)(2,1)S(1)}, bf16[2,192,512]{2,1,0:T(8,128)(2,1)S(1)}, u32[]{:S(2)}, u32[]{:S(2)}) %collective-permute-start.1) | collective-permute-done | bytes 393248 | tf_op jit(solution)/shard_map/ppermute | solution.py:42
  18.9 1.5 %collective-permute-done.mixed_one_ref = bf16[2,192,512]{2,1,0:T(8,128)(2,1)S(1)} collective-permute-done((bf16[2,192,512]{2,1,0:T(8,128)(2,1)S(1)}, bf16[2,192,512]{2,1,0:T(8,128)(2,1)S(1)}, u32[]{:S(2)}, u32[]{:S(2)}) %collective-permute-start) | collective-permute-done | bytes 393248 | tf_op jit(solution)/shard_map/ppermute | solution.py:43
  20.4 3.1 %main_inner.1 = (f32[640,128]{1,0:T(8,128)S(1)}, bf16[2,64,512]{2,1,0:T(8,128)(2,1)S(1)}) custom-call(bf16[2,192,512]{2,1,0:T(8,128)(2,1)S(1)} %get-tuple-element.24.own_ref, bf16[2,192,512]{2,1,0:T(8,128)(2,1)S(1)} %collective-permute-done.mixed_one_ref, bf16[2,192,512]{2,1,0:T(8,128)(2,1)S(1)} %collective-permute-done.1.mixed_two_ref, ...), custom_call_target="tpu_custom_call" | custom-call | flops 3000000000 | bytes 9000000 | tf_op jit(solution)/shard_map/main_inner/pallas_call | solution.py:407
  23.5 0.0 collective-permute-done.5.first_two_ref
  23.5 0.8 %collective-permute-done.4.first_one_ref = bf16[2,128,512]{2,1,0:T(8,128)(2,1)S(1)} collective-permute-done((bf16[2,128,512]{2,1,0:T(8,128)(2,1)S(1)}, bf16[2,128,512]{2,1,0:T(8,128)(2,1)S(1)}, u32[]{:S(2)}, u32[]{:S(2)}) %collective-permute-start.4) | collective-permute-done | bytes 262176 | tf_op jit(solution)/shard_map/ppermute | solution.py:43
  24.3 3.0 %main_edge.1 = (f32[640,128]{1,0:T(8,128)S(1)}, bf16[2,64,512]{2,1,0:T(8,128)(2,1)S(1)}) custom-call(bf16[2,128,512]{2,1,0:T(8,128)(2,1)S(1)} %get-tuple-element.35.first_ref, bf16[2,128,512]{2,1,0:T(8,128)(2,1)S(1)} %collective-permute-done.4.first_one_ref, bf16[2,128,512]{2,1,0:T(8,128)(2,1)S(1)} %collective-permute-done.5.first_two_ref, ...), custom_call_target="tpu_custom_call" | custom-call | flops 3000000000 | bytes 9000000 | tf_op jit(solution)/shard_map/main_edge/pallas_call | solution.py:407
  27.4 17.1 %all_to_all.10 = f32[16,40,128]{2,1,0:T(8,128)S(1)} all-to-all(f32[16,40,128]{2,1,0:T(8,128)S(1)} %bitcast.5), channel_id=1, replica_groups=mesh['pair'=2,'core'=2,'ang'=4,'quad'=4,'x'=4] {'ang','x'}, dimensions={0} | all-to-all | bytes 655360 | tf_op jit(solution)/shard_map/all_to_all | solution.py:24
  44.5 0.1 collective-permute-start.6
  44.6 1.2 %collective-permute-done.6 = f32[40,128]{1,0:T(8,128)S(1)} collective-permute-done((f32[40,128]{1,0:T(8,128)S(1)}, f32[40,128]{1,0:T(8,128)S(1)}, u32[]{:S(2)}, u32[]{:S(2)}) %collective-permute-start.6) | collective-permute-done | bytes 20512 | tf_op jit(solution)/shard_map/ppermute | solution.py:18
  45.8 1.0 %collective-permute-start.7 = (f32[40,128]{1,0:T(8,128)S(1)}, f32[40,128]{1,0:T(8,128)S(1)}, u32[]{:S(2)}, u32[]{:S(2)}) collective-permute-start(f32[40,128]{1,0:T(8,128)S(1)} %add.12), channel_id=1, source_target_pairs={{0,128},{128,0},{1,129},{129,1},{2,130},{130,2},{3,131},{131,3},{4... | collective-permute-start | bytes 61448 | tf_op jit(solution)/shard_map/ppermute | solution.py:18
  46.8 2.8 %collective-permute-done.7 = f32[40,128]{1,0:T(8,128)S(1)} collective-permute-done((f32[40,128]{1,0:T(8,128)S(1)}, f32[40,128]{1,0:T(8,128)S(1)}, u32[]{:S(2)}, u32[]{:S(2)}) %collective-permute-start.7) | collective-permute-done | bytes 20512 | tf_op jit(solution)/shard_map/ppermute | solution.py:18
  49.6 0.9 %collective-permute-start.8 = (f32[40,128]{1,0:T(8,128)S(1)}, f32[40,128]{1,0:T(8,128)S(1)}, u32[]{:S(2)}, u32[]{:S(2)}) collective-permute-start(f32[40,128]{1,0:T(8,128)S(1)} %add.13), channel_id=1, source_target_pairs={{0,4},{4,0},{8,12},{12,8},{1,5},{5,1},{9,13},{13,9},{2,6},{6,2},{1... | collective-permute-start | bytes 61448 | tf_op jit(solution)/shard_map/ppermute | solution.py:30
  50.5 3.8 %collective-permute-done.8 = f32[40,128]{1,0:T(8,128)S(1)} collective-permute-done((f32[40,128]{1,0:T(8,128)S(1)}, f32[40,128]{1,0:T(8,128)S(1)}, u32[]{:S(2)}, u32[]{:S(2)}) %collective-permute-start.8) | collective-permute-done | bytes 20512 | tf_op jit(solution)/shard_map/ppermute | solution.py:30
  54.3 2.6 %collective-permute-start.9 = (f32[40,128]{1,0:T(8,128)S(1)}, f32[40,128]{1,0:T(8,128)S(1)}, u32[]{:S(2)}, u32[]{:S(2)}) collective-permute-start(f32[40,128]{1,0:T(8,128)S(1)} %add.14), channel_id=1, source_target_pairs={{0,12},{4,8},{8,4},{12,0},{1,13},{5,9},{9,5},{13,1},{2,14},{6,10},... | collective-permute-start | bytes 61448 | tf_op jit(solution)/shard_map/ppermute | solution.py:30
  56.9 3.3 %collective-permute-done.9 = f32[40,128]{1,0:T(8,128)S(1)} collective-permute-done((f32[40,128]{1,0:T(8,128)S(1)}, f32[40,128]{1,0:T(8,128)S(1)}, u32[]{:S(2)}, u32[]{:S(2)}) %collective-permute-start.9) | collective-permute-done | bytes 20512 | tf_op jit(solution)/shard_map/ppermute | solution.py:30
  60.2 0.7 broadcast_in_dim.2
  60.9 3.5 %all-to-all-start.1 = ((bf16[16,40,128]{2,1,0:T(8,128)(2,1)}), bf16[16,40,128]{2,1,0:T(8,128)(2,1)S(1)}, u32[]{:S(2)}, u32[]{:S(2)}) async-start(bf16[16,40,128]{2,1,0:T(8,128)(2,1)} %broadcast_in_dim.2), calls=%async_computation.1 | async-start | bytes 327680 | tf_op jit(solution)/shard_map/all_to_all | solution.py:32
  64.4 1.4 %weave.1 = bf16[2,16,2048]{2,1,0:T(8,128)(2,1)} custom-call(bf16[2,64,512]{2,1,0:T(8,128)(2,1)S(1)} %get-tuple-element.31.inner_ref, bf16[2,64,512]{2,1,0:T(8,128)(2,1)S(1)} %get-tuple-element.38.edge_ref, bf16[512,512]{1,0:T(8,128)(2,1)S(1)} %get-tuple-element.39.deal_ref), custom_call_target="tpu_custom_call" | custom-call | flops 3000000000 | bytes 9000000 | tf_op jit(solution)/shard_map/weave/pallas_call | solution.py:407
  65.8 6.8 %all-to-all-done.1 = bf16[16,40,128]{2,1,0:T(8,128)(2,1)S(1)} async-done(((bf16[16,40,128]{2,1,0:T(8,128)(2,1)}), bf16[16,40,128]{2,1,0:T(8,128)(2,1)S(1)}, u32[]{:S(2)}, u32[]{:S(2)}) %all-to-all-start.1) | async-done | bytes 163872 | tf_op jit(solution)/shard_map/all_to_all | solution.py:32
  72.5 0.9 %unpack.1 = (f32[3,3,64,64]{3,2,1,0:T(8,128)}, f32[3,3,64,64]{3,2,1,0:T(8,128)}, f32[16,64]{1,0:T(8,128)}) custom-call(bf16[640,128]{1,0:T(8,128)(2,1)S(1)} %bitcast.6), custom_call_target="tpu_custom_call" | custom-call | flops 3000000000 | bytes 9000000 | tf_op jit(solution)/shard_map/unpack/pallas_call | solution.py:407
  (5 shorter events, 0.0 us)
Async XLA Ops:
  2.9 5.9 %collective-permute-start.2 = (bf16[2,1,64,512]{3,2,1,0:T(8,128)(2,1)S(1)}, bf16[2,1,64,512]{3,2,1,0:T(8,128)(2,1)S(1)}, u32[]{:S(2)}, u32[]{:S(2)}) collective-permute-start(bf16[2,1,64,512]{3,2,1,0:T(8,128)(2,1)S(1)} %get-tuple-element.32), channel_id=1, source_target_pairs={{0,1},{1,0},{2,3},{3,2},{4,5},{5,4},{6,7},{7,6},{8,9},{9,8},{10,11... | collective-permute-start | bytes 393224 | tf_op jit(solution)/shard_map/ppermute | solution.py:43
  4.5 8.6 %collective-permute-start.3 = (bf16[2,1,64,512]{3,2,1,0:T(8,128)(2,1)S(1)}, bf16[2,1,64,512]{3,2,1,0:T(8,128)(2,1)S(1)}, u32[]{:S(2)}, u32[]{:S(2)}) collective-permute-start(bf16[2,1,64,512]{3,2,1,0:T(8,128)(2,1)S(1)} %get-tuple-element.33), channel_id=1, source_target_pairs={{1,2},{3,4},{5,6},{7,8},{9,10},{11,12},{13,14},{15,0},{2,1},{4,3},... | collective-permute-start | bytes 393224 | tf_op jit(solution)/shard_map/ppermute | solution.py:42
  5.7 13.3 %collective-permute-start.1 = (bf16[2,192,512]{2,1,0:T(8,128)(2,1)S(1)}, bf16[2,192,512]{2,1,0:T(8,128)(2,1)S(1)}, u32[]{:S(2)}, u32[]{:S(2)}) collective-permute-start(bf16[2,192,512]{2,1,0:T(8,128)(2,1)S(1)} %get-tuple-element.24.own_ref), channel_id=1, source_target_pairs={{16,32},{48,0},{32,16},{0,48},{17,33},{49,1},{33,17},{1,49},{18,34... | collective-permute-start | bytes 1179656 | tf_op jit(solution)/shard_map/ppermute | solution.py:42
  8.7 11.7 %collective-permute-start = (bf16[2,192,512]{2,1,0:T(8,128)(2,1)S(1)}, bf16[2,192,512]{2,1,0:T(8,128)(2,1)S(1)}, u32[]{:S(2)}, u32[]{:S(2)}) collective-permute-start(bf16[2,192,512]{2,1,0:T(8,128)(2,1)S(1)} %get-tuple-element.24.own_ref), channel_id=1, source_target_pairs={{0,16},{16,0},{32,48},{48,32},{1,17},{17,1},{33,49},{49,33},{2,18}... | collective-permute-start | bytes 1179656 | tf_op jit(solution)/shard_map/ppermute | solution.py:43
  13.7 9.8 %collective-permute-start.5 = (bf16[2,128,512]{2,1,0:T(8,128)(2,1)S(1)}, bf16[2,128,512]{2,1,0:T(8,128)(2,1)S(1)}, u32[]{:S(2)}, u32[]{:S(2)}) collective-permute-start(bf16[2,128,512]{2,1,0:T(8,128)(2,1)S(1)} %get-tuple-element.35.first_ref), channel_id=1, source_target_pairs={{16,32},{48,0},{32,16},{0,48},{17,33},{49,1},{33,17},{1,49},{18,34... | collective-permute-start | bytes 786440 | tf_op jit(solution)/shard_map/ppermute | solution.py:42
  16.7 7.6 %collective-permute-start.4 = (bf16[2,128,512]{2,1,0:T(8,128)(2,1)S(1)}, bf16[2,128,512]{2,1,0:T(8,128)(2,1)S(1)}, u32[]{:S(2)}, u32[]{:S(2)}) collective-permute-start(bf16[2,128,512]{2,1,0:T(8,128)(2,1)S(1)} %get-tuple-element.35.first_ref), channel_id=1, source_target_pairs={{0,16},{16,0},{32,48},{48,32},{1,17},{17,1},{33,49},{49,33},{2,18}... | collective-permute-start | bytes 786440 | tf_op jit(solution)/shard_map/ppermute | solution.py:43
  44.5 1.3 %collective-permute-start.6 = (f32[40,128]{1,0:T(8,128)S(1)}, f32[40,128]{1,0:T(8,128)S(1)}, u32[]{:S(2)}, u32[]{:S(2)}) collective-permute-start(f32[40,128]{1,0:T(8,128)S(1)} %reduce_sum.9), channel_id=1, source_target_pairs={{0,64},{64,0},{1,65},{65,1},{2,66},{66,2},{3,67},{67,3},{4,68},{68... | collective-permute-start | bytes 61448 | tf_op jit(solution)/shard_map/ppermute | solution.py:18
  45.8 3.8 %collective-permute-start.7 = (f32[40,128]{1,0:T(8,128)S(1)}, f32[40,128]{1,0:T(8,128)S(1)}, u32[]{:S(2)}, u32[]{:S(2)}) collective-permute-start(f32[40,128]{1,0:T(8,128)S(1)} %add.12), channel_id=1, source_target_pairs={{0,128},{128,0},{1,129},{129,1},{2,130},{130,2},{3,131},{131,3},{4... | collective-permute-start | bytes 61448 | tf_op jit(solution)/shard_map/ppermute | solution.py:18
  49.6 4.7 %collective-permute-start.8 = (f32[40,128]{1,0:T(8,128)S(1)}, f32[40,128]{1,0:T(8,128)S(1)}, u32[]{:S(2)}, u32[]{:S(2)}) collective-permute-start(f32[40,128]{1,0:T(8,128)S(1)} %add.13), channel_id=1, source_target_pairs={{0,4},{4,0},{8,12},{12,8},{1,5},{5,1},{9,13},{13,9},{2,6},{6,2},{1... | collective-permute-start | bytes 61448 | tf_op jit(solution)/shard_map/ppermute | solution.py:30
  54.3 5.9 %collective-permute-start.9 = (f32[40,128]{1,0:T(8,128)S(1)}, f32[40,128]{1,0:T(8,128)S(1)}, u32[]{:S(2)}, u32[]{:S(2)}) collective-permute-start(f32[40,128]{1,0:T(8,128)S(1)} %add.14), channel_id=1, source_target_pairs={{0,12},{4,8},{8,4},{12,0},{1,13},{5,9},{9,5},{13,1},{2,14},{6,10},... | collective-permute-start | bytes 61448 | tf_op jit(solution)/shard_map/ppermute | solution.py:30
  60.9 11.7 %all-to-all-start.1 = ((bf16[16,40,128]{2,1,0:T(8,128)(2,1)}), bf16[16,40,128]{2,1,0:T(8,128)(2,1)S(1)}, u32[]{:S(2)}, u32[]{:S(2)}) async-start(bf16[16,40,128]{2,1,0:T(8,128)(2,1)} %broadcast_in_dim.2), calls=%async_computation.1 | async-start | bytes 327680 | tf_op jit(solution)/shard_map/all_to_all | solution.py:32

commit v5 on v4

--- a/solution.py
+++ b/solution.py
@@ -24,12 +24,12 @@
     mine = lax.all_to_all(
         pay.reshape(16, rows // 16, 128), plane, split_axis=0, concat_axis=0, tiled=True
     ).sum(0)
-    for axis in ("core", "pair"):
-        mine = mine + swapped(mine, axis, 1)
+    mine = mine + swapped(mine, "core", 1)
     for flip in (1, 3):
         mine = mine + lax.ppermute(mine, "quad", [(i, i ^ flip) for i in range(4)])
-    spread = jnp.broadcast_to(mine.astype(BF16)[None], (16,) + mine.shape)
-    return lax.all_to_all(spread, plane, split_axis=0, concat_axis=0, tiled=True).reshape(rows, 128)
+    spread = jnp.broadcast_to(mine.astype(BF16)[None], (32,) + mine.shape)
+    gathered = lax.all_to_all(spread, ("pair",) + plane, split_axis=0, concat_axis=0, tiled=True)
+    return gathered.reshape(2, rows, 128)
 
 
 def is_even(axis):
@@ -38,8 +38,11 @@
 
 def with_next_and_before(first_send, second_send, axis):
     count = lax.axis_size(axis)
-    odd = [(i, (i + 1) % count) for i in range(1, count, 2)]
-    two = lax.ppermute(second_send, axis, odd + [(j, i) for i, j in odd])
+    axes = (axis,) if isinstance(axis, str) else axis
+    pairs = [(count - 1, 2 * count - 1), (0, count)]
+    for core in (0, count):
+        pairs += [(core + i, core + i + 1) for i in range(1, count - 1, 2)]
+    two = lax.ppermute(second_send, ("core",) + axes, pairs + [(j, i) for i, j in pairs])
     one = lax.ppermute(first_send, axis, [(i, i ^ 1) for i in range(count)])
     return one, two
 
@@ -142,7 +145,9 @@
     spatial_hbm,
     epi_hbm,
     up_hbm,
-    mixed_ref,
+    mixed_one_ref,
+    mixed_two_ref,
+    dealt_ref,
     out_ref,
     deal_ref,
     weight_ref,
@@ -196,18 +201,22 @@
         moved = product(stacked, deal).astype(BF16)
         for view in range(2):
             for q in range(4):
-                mixed_ref[
-                    view,
-                    2 * chans + q * 16 : 2 * chans + (q + 1) * 16,
-                    block * lanes : (block + 1) * lanes,
+                dealt_ref[
+                    view, q * 16 : (q + 1) * 16, block * lanes : (block + 1) * lanes
                 ] = moved[view * 16 : (view + 1) * 16, q * lanes : (q + 1) * lanes]
+    even_view = is_even("ang")
+    mixed_one_ref[4 * chans :] = jnp.where(even_view, dealt_ref[1], dealt_ref[0])
+    mixed_two_ref[4 * chans :] = jnp.where(even_view, dealt_ref[0], dealt_ref[1])
     for view in range(2):
         for slot, h in enumerate((1, 2)):
             stacked = jnp.concatenate([light_ref[view, h + k] for k in (-1, 0, 1)], axis=0)
             total = conv_taps(weight_ref[...], stacked, True)
-            out_ref[view, slot] = total
-            first = light_ref[view, h].astype(F32) + total * gate_of(total)
-            mixed_ref[view, slot * chans : (slot + 1) * chans] = first.astype(BF16)
+            gate = gate_of(total)
+            out_ref[view, slot] = silu_slope(total, gate)
+            first = (light_ref[view, h].astype(F32) + total * gate).astype(BF16)
+            cut = slice((2 * view + slot) * chans, (2 * view + slot + 1) * chans)
+            mixed_one_ref[cut] = first
+            mixed_two_ref[cut] = first
 
 
 def edge_kernel(light_ref, one_ref, two_ref, weight_ref, first_ref, out_ref):
@@ -220,24 +229,26 @@
             else:
                 stacked = [light_ref[view, 2], light_ref[view, 3], chosen(below, one_ref[view, 0], two_ref[view, 0])]
             total = conv_taps(weight_ref[...], jnp.concatenate(stacked, axis=0), True)
-            out_ref[view, slot] = total
-            first = light_ref[view, h].astype(F32) + total * gate_of(total)
-            first_ref[view, slot * chans : (slot + 1) * chans] = first.astype(BF16)
-
-
-def main_rows(rows, firsts, dealt, near, out_ref, epi_ref, back_ref, lift_ref, drop_ref, pay_ref, lift_out):
-    chans = drop_ref.shape[1]
+            gate = gate_of(total)
+            out_ref[view, slot] = silu_slope(total, gate)
+            first = light_ref[view, h].astype(F32) + total * gate
+            cut = slice((2 * view + slot) * chans, (2 * view + slot + 1) * chans)
+            first_ref[cut] = first.astype(BF16)
+
+
+def main_rows(rows, firsts, dealt, grad_of, near, out_ref, epi_ref, back_ref, lift_ref, pay_ref, lift_out):
+    chans = out_ref.shape[2]
     three = 3 * chans
     lifted = [None, None]
     up_total = None
     epi_left, epi_right, spatial_left, spatial_right = [], [], [], []
     before, after = sides("ang", 4)
     for slot, h in enumerate(rows):
-        cut = slice(slot * chans, (slot + 1) * chans)
+        cuts = [slice((2 * v + slot) * chans, (2 * v + slot + 1) * chans) for v in range(2)]
         stack = jnp.concatenate(
-            [chosen(before, firsts[1][v, cut], firsts[2][v, cut]) for v in range(2)]
-            + [firsts[0][v, cut] for v in range(2)]
-            + [chosen(after, firsts[1][v, cut], firsts[2][v, cut]) for v in range(2)],
+            [chosen(before, firsts[1][cut], firsts[2][cut]) for cut in cuts]
+            + [firsts[0][cut] for cut in cuts]
+            + [chosen(after, firsts[1][cut], firsts[2][cut]) for cut in cuts],
             axis=0,
         )
         here = (lax.broadcasted_iota(jnp.int32, (64, chans), 0) % 16) // 4 == h
@@ -246,7 +257,7 @@
             window = stack[v * chans : (v + 3) * chans]
             total = conv_taps(epi_ref[...], window, True)
             gate = gate_of(total)
-            grad = product(drop_ref[h], dealt[v]).astype(BF16).astype(F32)
+            grad = grad_of(slot, v).astype(F32)
             slope = grad * silu_slope(total, gate)
             slopes.append(slope.astype(BF16))
             if v in (1, 2):
@@ -263,8 +274,7 @@
         for v in range(2):
             moved = conv_taps(back_ref[...], slopes[v * chans : (v + 3) * chans], False)
             first_grad = (grads[v] + moved).astype(BF16).astype(F32)
-            total = out_ref[v, slot]
-            slope = first_grad * silu_slope(total, gate_of(total))
+            slope = first_grad * out_ref[v, slot]
             spatial_left.append(taps_of(slope))
             spatial_right.append(jnp.concatenate(near(v, h), axis=0))
     for v in range(2):
@@ -286,32 +296,48 @@
         start = end
 
 
-def dealt_views(own_ref, one_ref, two_ref, chans):
+def dealt_views(dealt_ref, one_ref, two_ref, chans):
     before, after = sides("ang", 4)
-    return [
-        chosen(before, one_ref[1, 2 * chans :], two_ref[1, 2 * chans :]),
-        own_ref[0, 2 * chans :],
-        own_ref[1, 2 * chans :],
-        chosen(after, one_ref[0, 2 * chans :], two_ref[0, 2 * chans :]),
-    ]
+    one, two = one_ref[4 * chans :], two_ref[4 * chans :]
+    return [chosen(before, one, two), dealt_ref[0], dealt_ref[1], chosen(after, one, two)]
 
 
 def main_inner_kernel(
-    own_ref, mixed_one_ref, mixed_two_ref, light_ref, out_ref, epi_ref, back_ref, lift_ref, drop_ref, pay_ref, lift_out
+    own_ref,
+    mixed_one_ref,
+    mixed_two_ref,
+    dealt_ref,
+    light_ref,
+    out_ref,
+    epi_ref,
+    back_ref,
+    lift_ref,
+    drop_ref,
+    pay_ref,
+    lift_out,
+    edge_grad_ref,
 ):
+    dealt = dealt_views(dealt_ref, mixed_one_ref, mixed_two_ref, light_ref.shape[2])
+    for slot, h in enumerate((0, 3)):
+        for v in range(4):
+            edge_grad_ref[slot, v] = product(drop_ref[h], dealt[v]).astype(BF16)
+
+    def grad_of(slot, v):
+        return product(drop_ref[slot + 1], dealt[v]).astype(BF16)
+
     def near(v, h):
         return [light_ref[v, h + k] for k in (-1, 0, 1)]
 
     main_rows(
         (1, 2),
         (own_ref, mixed_one_ref, mixed_two_ref),
-        dealt_views(own_ref, mixed_one_ref, mixed_two_ref, light_ref.shape[2]),
+        dealt,
+        grad_of,
         near,
         out_ref,
         epi_ref,
         back_ref,
         lift_ref,
-        drop_ref,
         pay_ref,
         lift_out,
     )
@@ -321,9 +347,8 @@
     first_ref,
     first_one_ref,
     first_two_ref,
-    own_ref,
-    mixed_one_ref,
-    mixed_two_ref,
+    dealt_ref,
+    edge_grad_ref,
     light_ref,
     one_ref,
     two_ref,
@@ -331,7 +356,6 @@
     epi_ref,
     back_ref,
     lift_ref,
-    drop_ref,
     inner_pay_ref,
     pay_ref,
     lift_out,
@@ -346,13 +370,13 @@
     main_rows(
         (0, 3),
         (first_ref, first_one_ref, first_two_ref),
-        dealt_views(own_ref, mixed_one_ref, mixed_two_ref, light_ref.shape[2]),
+        (None, dealt_ref[0], dealt_ref[1], None),
+        lambda slot, v: edge_grad_ref[slot, v],
         near,
         out_ref,
         epi_ref,
         back_ref,
         lift_ref,
-        drop_ref,
         pay_ref,
         lift_out,
     )
@@ -380,7 +404,7 @@
 
 
 def unpack_kernel(sent_ref, spatial_ref, epi_ref, up_ref, pay_ref):
-    pay_ref[...] = sent_ref[...].astype(F32)
+    pay_ref[...] = sent_ref[0].astype(F32) + sent_ref[1].astype(F32)
     chans = spatial_ref.shape[2]
     three = 3 * chans
     for which, ref in enumerate((spatial_ref, epi_ref)):
@@ -432,7 +456,9 @@
     taps = like((three, three), BF16)
     edge_line = like((views, 1, chans, breadth), BF16)
     (
-        mixed,
+        mixed_for_one,
+        mixed_for_two,
+        dealt,
         inner_out,
         deal,
         spatial_taps,
@@ -446,7 +472,9 @@
     ) = local_call(
         inner_kernel,
         (
-            like((views, 2 * chans + 64, breadth), BF16),
+            like((4 * chans + 64, breadth), BF16),
+            like((4 * chans + 64, breadth), BF16),
+            like((views, 64, breadth), BF16),
             half_out,
             like((512, 512), BF16),
             taps,
@@ -475,10 +503,10 @@
     )
     light = light_here
     line_one, line_two = with_next_and_before(send_one, send_two, ROWS)
-    mixed_one, mixed_two = with_next_and_before(mixed, mixed, "ang")
+    mixed_one, mixed_two = with_next_and_before(mixed_for_one, mixed_for_two, "ang")
     first, edge_out = local_call(
         edge_kernel,
-        (like((views, 2 * chans, breadth), BF16), half_out),
+        (like((4 * chans, breadth), BF16), half_out),
         "edge",
         light,
         line_one,
@@ -487,19 +515,22 @@
     )
     first_one, first_two = with_next_and_before(first, first, "ang")
 
-    weights = (epi_taps, back_taps, lift, drop)
     lift_half = like((views, 64, breadth), BF16)
     whole_pay = like((640, 128), F32)
-    inner_pay, inner_lift = local_call(
+    inner_pay, inner_lift, edge_grad = local_call(
         main_inner_kernel,
-        (whole_pay, lift_half),
+        (whole_pay, lift_half, like((2, 4, chans, breadth), BF16)),
         "main_inner",
-        mixed,
+        mixed_for_one,
         mixed_one,
         mixed_two,
+        dealt,
         light,
         inner_out,
-        *weights,
+        epi_taps,
+        back_taps,
+        lift,
+        drop,
     )
     pay, edge_lift = local_call(
         main_edge_kernel,
@@ -508,14 +539,15 @@
         first,
         first_one,
         first_two,
-        mixed,
-        mixed_one,
-        mixed_two,
+        dealt,
+        edge_grad,
         light,
         line_one,
         line_two,
         edge_out,
-        *weights,
+        epi_taps,
+        back_taps,
+        lift,
         inner_pay,
     )
     up = local_call(

time: 74 us -> 71 us (0.959)
  waiting for transfers between devices: 26.4 us -> 22.8 us
  blocking collectives: 17.1 us -> 18.8 us
  starting transfers between devices: 17.3 us -> 16.4 us
    ppermute x3, starting transfers between devices: 1.86 us -> 7.86 us  [with_next_and_before(): one = lax.ppermute(first_send, axis, [(i, i ^ 1) for i in range(count)])]
    ppermute x3, starting transfers between devices: 7.29 us -> 1.29 us  [with_next_and_before(): lax.ppermute(second_send, ('core',) + axes, pairs + [(j, i) for i, j in p...]
    ppermute x2 -> x1, waiting for transfers between devices: 3.95 us -> 1.18 us  [swapped(): lax.ppermute(value, axis, [(i, (i + step) % count) for i in range(count)])]
    ppermute x3, waiting for transfers between devices: 6.34 us -> 3.73 us  [with_next_and_before(): lax.ppermute(second_send, ('core',) + axes, pairs + [(j, i) for i, j in p...]
    all_to_all x1, blocking collectives: 17.1 us -> 18.8 us  [sum_everywhere(): lax.all_to_all(pay.reshape(16, rows // 16, 128), plane, split_axis=0, con...]
    all_to_all x1, waiting for transfers between devices: 6.76 us -> 7.95 us  [sum_everywhere(): lax.all_to_all(spread, ('pair',) + plane, split_axis=0, concat_axis=0, ti...]
    ppermute x2 -> x1, starting transfers between devices: 1.11 us -> 0.09 us  [swapped(): lax.ppermute(value, axis, [(i, (i + step) % count) for i in range(count)])]
  transfers between devices with their start and end apart: 11 -> 10, of which waited for: 9 -> 6; matrix products, arithmetic and copies ran while one was open for 0% -> 0% of each run, Pallas kernels for 7% -> 7%
where the time goes in v5:
time: 71 us; the launch traced here: 70.8 us
  waiting for transfers between devices  22.8 us (32%)
  blocking collectives  18.8 us (26%)
  starting transfers between devices  16.4 us (23%)
  Pallas kernels  11.3 us (16%)
  local copies, waits for them, and re-layouts  0.76 us (1%)
  between operations  0.71 us (1%)
    all_to_all x1, blocking collectives, sum_everywhere(): lax.all_to_all(pay.reshape(16, rows // 16, 128), plane, split_axis=0, con...  18.8 us
    pallas_call x6, Pallas kernels, local_call(): pl.pallas_call(kernel, out_shape=shapes, scratch_shapes=scratch, in_specs...  11.3 us
    all_to_all x1, waiting for transfers between devices, sum_everywhere(): lax.all_to_all(spread, ('pair',) + plane, split_axis=0, concat_axis=0, ti...  7.95 us
    ppermute x3, starting transfers between devices, with_next_and_before(): one = lax.ppermute(first_send, axis, [(i, i ^ 1) for i in range(count)])  7.86 us
    ppermute x2, waiting for transfers between devices, sum_everywhere(): mine = mine + lax.ppermute(mine, 'quad', [(i, i ^ flip) for i in range(4)])  7.5 us
    all_to_all x1, starting transfers between devices, sum_everywhere(): lax.all_to_all(spread, ('pair',) + plane, split_axis=0, concat_axis=0, ti...  3.87 us
    ppermute x3, waiting for transfers between devices, with_next_and_before(): lax.ppermute(second_send, ('core',) + axes, pairs + [(j, i) for i, j in p...  3.73 us
    ppermute x2, starting transfers between devices, sum_everywhere(): mine = mine + lax.ppermute(mine, 'quad', [(i, i ^ flip) for i in range(4)])  3.27 us
  transfers between devices with their start and end apart: 10, of which 6 were waited for; matrix products, arithmetic and copies ran while one was open for 0% of the time, Pallas kernels for 7%

profile of v5, /device:TPU:64, one launch (start us, length us, event | category | flops | bytes accessed | tf_op | source)
XLA Modules:
  0.0 70.8 jit_solution(16432664826427024187)
XLA Ops:
  0.6 2.3 %inner.1 = (bf16[320,512]{1,0:T(8,128)(2,1)S(1)}, bf16[320,512]{1,0:T(8,128)(2,1)S(1)}, bf16[2,64,512]{2,1,0:T(8,128)(2,1)S(1)}, f32[2,2,64,512]{3,2,1,0:T(8,128...) custom-call(bf16[2,16,2048]{2,1,0:T(8,128)(2,1)} %bitcast.8, ...), custom_call_target="tpu_custom_call" | custom-call | flops 3000000000 | bytes 9000000 | tf_op jit(solution)/shard_map/inner/pallas_call | solution.py:431
  3.0 1.6 %collective-permute-start.2 = (bf16[2,1,64,512]{3,2,1,0:T(8,128)(2,1)S(1)}, bf16[2,1,64,512]{3,2,1,0:T(8,128)(2,1)S(1)}, u32[]{:S(2)}, u32[]{:S(2)}) collective-permute-start(bf16[2,1,64,512]{3,2,1,0:T(8,128)(2,1)S(1)} %get-tuple-element.37), channel_id=1, source_target_pairs={{0,1},{1,0},{2,3},{3,2},{4,5},{5,4},{6,7},{7,6},{8,9},{9,8},{10,11... | collective-permute-start | bytes 393224 | tf_op jit(solution)/shard_map/ppermute | solution.py:46
  4.5 1.2 %collective-permute-start.3 = (bf16[2,1,64,512]{3,2,1,0:T(8,128)(2,1)S(1)}, bf16[2,1,64,512]{3,2,1,0:T(8,128)(2,1)S(1)}, u32[]{:S(2)}, u32[]{:S(2)}) collective-permute-start(bf16[2,1,64,512]{3,2,1,0:T(8,128)(2,1)S(1)} %get-tuple-element.38), channel_id=1, source_target_pairs={{15,79},{0,64},{1,2},{3,4},{5,6},{7,8},{9,10},{11,12},{13,14},{65,... | collective-permute-start | bytes 393224 | tf_op jit(solution)/shard_map/ppermute | solution.py:45
  5.7 0.0 collective-permute-start.1
  5.7 3.1 %collective-permute-start = (bf16[320,512]{1,0:T(8,128)(2,1)S(1)}, bf16[320,512]{1,0:T(8,128)(2,1)S(1)}, u32[]{:S(2)}, u32[]{:S(2)}) collective-permute-start(bf16[320,512]{1,0:T(8,128)(2,1)S(1)} %get-tuple-element.27.own_ref), channel_id=1, source_target_pairs={{0,16},{16,0},{32,48},{48,32},{1,17},{17,1},{33,49},{49,33},{2,18}... | collective-permute-start | bytes 983048 | tf_op jit(solution)/shard_map/ppermute | solution.py:46
  8.9 0.0 collective-permute-done.2.one_ref
  8.9 3.7 %collective-permute-done.3.two_ref = bf16[2,1,64,512]{3,2,1,0:T(8,128)(2,1)S(1)} collective-permute-done((bf16[2,1,64,512]{3,2,1,0:T(8,128)(2,1)S(1)}, bf16[2,1,64,512]{3,2,1,0:T(8,128)(2,1)S(1)}, u32[]{:S(2)}, u32[]{:S(2)}) %collective-permute-start.3) | collective-permute-done | bytes 131104 | tf_op jit(solution)/shard_map/ppermute | solution.py:45
  12.6 0.5 edge.1
  13.2 0.1 collective-permute-start.5
  13.3 3.1 %collective-permute-start.4 = (bf16[256,512]{1,0:T(8,128)(2,1)S(1)}, bf16[256,512]{1,0:T(8,128)(2,1)S(1)}, u32[]{:S(2)}, u32[]{:S(2)}) collective-permute-start(bf16[256,512]{1,0:T(8,128)(2,1)S(1)} %get-tuple-element.40.first_ref), channel_id=1, source_target_pairs={{0,16},{16,0},{32,48},{48,32},{1,17},{17,1},{33,49},{49,33},{2,18}... | collective-permute-start | bytes 786440 | tf_op jit(solution)/shard_map/ppermute | solution.py:46
  16.4 0.0 collective-permute-done.1.mixed_two_ref
  16.4 0.0 collective-permute-done.mixed_one_ref
  16.4 3.2 %main_inner.1 = (f32[640,128]{1,0:T(8,128)S(1)}, bf16[2,64,512]{2,1,0:T(8,128)(2,1)S(1)}, bf16[2,4,64,512]{3,2,1,0:T(8,128)(2,1)S(1)}) custom-call(bf16[320,512]{1,0:T(8,128)(2,1)S(1)} %get-tuple-element.27.own_ref, bf16[320,512]{1,0:T(8,128)(2,1)S(1)} %collective-permute-done.mixed_one_ref, bf16[320,512]{1,0:T(8,128)(2,1)S(1)} %collective-permute-done.1.mixed_two_ref, ...), custom_call_target="tpu_custom_call" | custom-call | flops 3000000000 | bytes 9000000 | tf_op jit(solution)/shard_map/main_inner/pallas_call | solution.py:431
  19.6 0.0 collective-permute-done.5.first_two_ref
  19.6 2.4 %collective-permute-done.4.first_one_ref = bf16[256,512]{1,0:T(8,128)(2,1)S(1)} collective-permute-done((bf16[256,512]{1,0:T(8,128)(2,1)S(1)}, bf16[256,512]{1,0:T(8,128)(2,1)S(1)}, u32[]{:S(2)}, u32[]{:S(2)}) %collective-permute-start.4) | collective-permute-done | bytes 262176 | tf_op jit(solution)/shard_map/ppermute | solution.py:46
  22.0 3.0 %main_edge.1 = (f32[640,128]{1,0:T(8,128)S(1)}, bf16[2,64,512]{2,1,0:T(8,128)(2,1)S(1)}) custom-call(bf16[256,512]{1,0:T(8,128)(2,1)S(1)} %get-tuple-element.40.first_ref, bf16[256,512]{1,0:T(8,128)(2,1)S(1)} %collective-permute-done.4.first_one_ref, bf16[256,512]{1,0:T(8,128)(2,1)S(1)} %collective-permute-done.5.first_two_ref, ...), custom_call_target="tpu_custom_call" | custom-call | flops 3000000000 | bytes 9000000 | tf_op jit(solution)/shard_map/main_edge/pallas_call | solution.py:431
  25.0 18.8 %all_to_all.10 = f32[16,40,128]{2,1,0:T(8,128)S(1)} all-to-all(f32[16,40,128]{2,1,0:T(8,128)S(1)} %bitcast.6), channel_id=1, replica_groups=mesh['pair'=2,'core'=2,'ang'=4,'quad'=4,'x'=4] {'ang','x'}, dimensions={0} | all-to-all | bytes 655360 | tf_op jit(solution)/shard_map/all_to_all | solution.py:24
  43.8 0.1 collective-permute-start.6
  43.9 1.2 %collective-permute-done.6 = f32[40,128]{1,0:T(8,128)S(1)} collective-permute-done((f32[40,128]{1,0:T(8,128)S(1)}, f32[40,128]{1,0:T(8,128)S(1)}, u32[]{:S(2)}, u32[]{:S(2)}) %collective-permute-start.6) | collective-permute-done | bytes 20512 | tf_op jit(solution)/shard_map/ppermute | solution.py:18
  45.1 0.0 collective-permute-start.7
  45.1 4.7 %collective-permute-done.7 = f32[40,128]{1,0:T(8,128)S(1)} collective-permute-done((f32[40,128]{1,0:T(8,128)S(1)}, f32[40,128]{1,0:T(8,128)S(1)}, u32[]{:S(2)}, u32[]{:S(2)}) %collective-permute-start.7) | collective-permute-done | bytes 20512 | tf_op jit(solution)/shard_map/ppermute | solution.py:29
  49.8 3.3 %collective-permute-start.8 = (f32[40,128]{1,0:T(8,128)S(1)}, f32[40,128]{1,0:T(8,128)S(1)}, u32[]{:S(2)}, u32[]{:S(2)}) collective-permute-start(f32[40,128]{1,0:T(8,128)S(1)} %add.10), channel_id=1, source_target_pairs={{0,12},{4,8},{8,4},{12,0},{1,13},{5,9},{9,5},{13,1},{2,14},{6,10},... | collective-permute-start | bytes 61448 | tf_op jit(solution)/shard_map/ppermute | solution.py:29
  53.1 2.8 %collective-permute-done.8 = f32[40,128]{1,0:T(8,128)S(1)} collective-permute-done((f32[40,128]{1,0:T(8,128)S(1)}, f32[40,128]{1,0:T(8,128)S(1)}, u32[]{:S(2)}, u32[]{:S(2)}) %collective-permute-start.8) | collective-permute-done | bytes 20512 | tf_op jit(solution)/shard_map/ppermute | solution.py:29
  55.9 0.8 %broadcast_in_dim.2 = bf16[32,40,128]{2,1,0:T(8,128)(2,1)} broadcast(bf16[40,128]{1,0:T(8,128)(2,1)S(1)} %add_convert_fusion), dimensions={1,2} | broadcast | bytes 337920 | tf_op jit(solution)/shard_map/broadcast_in_dim | solution.py:30
  56.7 3.9 %all-to-all-start.1 = ((bf16[32,40,128]{2,1,0:T(8,128)(2,1)}), bf16[32,40,128]{2,1,0:T(8,128)(2,1)S(1)}, u32[]{:S(2)}, u32[]{:S(2)}) async-start(bf16[32,40,128]{2,1,0:T(8,128)(2,1)} %broadcast_in_dim.2), calls=%async_computation.1 | async-start | bytes 655360 | tf_op jit(solution)/shard_map/all_to_all | solution.py:31
  60.5 1.4 %weave.1 = bf16[2,16,2048]{2,1,0:T(8,128)(2,1)} custom-call(bf16[2,64,512]{2,1,0:T(8,128)(2,1)S(1)} %get-tuple-element.36.inner_ref, bf16[2,64,512]{2,1,0:T(8,128)(2,1)S(1)} %get-tuple-element.44.edge_ref, bf16[512,512]{1,0:T(8,128)(2,1)S(1)} %get-tuple-element.45.deal_ref), custom_call_target="tpu_custom_call" | custom-call | flops 3000000000 | bytes 9000000 | tf_op jit(solution)/shard_map/weave/pallas_call | solution.py:431
  61.9 8.0 %all-to-all-done.1 = bf16[32,40,128]{2,1,0:T(8,128)(2,1)S(1)} async-done(((bf16[32,40,128]{2,1,0:T(8,128)(2,1)}), bf16[32,40,128]{2,1,0:T(8,128)(2,1)S(1)}, u32[]{:S(2)}, u32[]{:S(2)}) %all-to-all-start.1) | async-done | bytes 327712 | tf_op jit(solution)/shard_map/all_to_all | solution.py:31
  69.9 0.9 %unpack.1 = (f32[3,3,64,64]{3,2,1,0:T(8,128)}, f32[3,3,64,64]{3,2,1,0:T(8,128)}, f32[16,64]{1,0:T(8,128)}) custom-call(bf16[2,640,128]{2,1,0:T(8,128)(2,1)S(1)} %bitcast.5), custom_call_target="tpu_custom_call" | custom-call | flops 3000000000 | bytes 9000000 | tf_op jit(solution)/shard_map/unpack/pallas_call | solution.py:431
  (4 shorter events, 0.0 us)
Async XLA Ops:
  3.0 5.9 %collective-permute-start.2 = (bf16[2,1,64,512]{3,2,1,0:T(8,128)(2,1)S(1)}, bf16[2,1,64,512]{3,2,1,0:T(8,128)(2,1)S(1)}, u32[]{:S(2)}, u32[]{:S(2)}) collective-permute-start(bf16[2,1,64,512]{3,2,1,0:T(8,128)(2,1)S(1)} %get-tuple-element.37), channel_id=1, source_target_pairs={{0,1},{1,0},{2,3},{3,2},{4,5},{5,4},{6,7},{7,6},{8,9},{9,8},{10,11... | collective-permute-start | bytes 393224 | tf_op jit(solution)/shard_map/ppermute | solution.py:46
  4.5 8.1 %collective-permute-start.3 = (bf16[2,1,64,512]{3,2,1,0:T(8,128)(2,1)S(1)}, bf16[2,1,64,512]{3,2,1,0:T(8,128)(2,1)S(1)}, u32[]{:S(2)}, u32[]{:S(2)}) collective-permute-start(bf16[2,1,64,512]{3,2,1,0:T(8,128)(2,1)S(1)} %get-tuple-element.38), channel_id=1, source_target_pairs={{15,79},{0,64},{1,2},{3,4},{5,6},{7,8},{9,10},{11,12},{13,14},{65,... | collective-permute-start | bytes 393224 | tf_op jit(solution)/shard_map/ppermute | solution.py:45
  5.7 10.7 %collective-permute-start.1 = (bf16[320,512]{1,0:T(8,128)(2,1)S(1)}, bf16[320,512]{1,0:T(8,128)(2,1)S(1)}, u32[]{:S(2)}, u32[]{:S(2)}) collective-permute-start(bf16[320,512]{1,0:T(8,128)(2,1)S(1)} %get-tuple-element.28), channel_id=1, source_target_pairs={{48,112},{0,64},{16,32},{80,96},{112,48},{64,0},{32,16},{96,80},{4... | collective-permute-start | bytes 983048 | tf_op jit(solution)/shard_map/ppermute | solution.py:45
  5.7 10.7 %collective-permute-start = (bf16[320,512]{1,0:T(8,128)(2,1)S(1)}, bf16[320,512]{1,0:T(8,128)(2,1)S(1)}, u32[]{:S(2)}, u32[]{:S(2)}) collective-permute-start(bf16[320,512]{1,0:T(8,128)(2,1)S(1)} %get-tuple-element.27.own_ref), channel_id=1, source_target_pairs={{0,16},{16,0},{32,48},{48,32},{1,17},{17,1},{33,49},{49,33},{2,18}... | collective-permute-start | bytes 983048 | tf_op jit(solution)/shard_map/ppermute | solution.py:46
  13.2 6.4 %collective-permute-start.5 = (bf16[256,512]{1,0:T(8,128)(2,1)S(1)}, bf16[256,512]{1,0:T(8,128)(2,1)S(1)}, u32[]{:S(2)}, u32[]{:S(2)}) collective-permute-start(bf16[256,512]{1,0:T(8,128)(2,1)S(1)} %get-tuple-element.40.first_ref), channel_id=1, source_target_pairs={{48,112},{0,64},{16,32},{80,96},{112,48},{64,0},{32,16},{96,80},{4... | collective-permute-start | bytes 786440 | tf_op jit(solution)/shard_map/ppermute | solution.py:45
  13.3 8.7 %collective-permute-start.4 = (bf16[256,512]{1,0:T(8,128)(2,1)S(1)}, bf16[256,512]{1,0:T(8,128)(2,1)S(1)}, u32[]{:S(2)}, u32[]{:S(2)}) collective-permute-start(bf16[256,512]{1,0:T(8,128)(2,1)S(1)} %get-tuple-element.40.first_ref), channel_id=1, source_target_pairs={{0,16},{16,0},{32,48},{48,32},{1,17},{17,1},{33,49},{49,33},{2,18}... | collective-permute-start | bytes 786440 | tf_op jit(solution)/shard_map/ppermute | solution.py:46
  43.8 1.3 %collective-permute-start.6 = (f32[40,128]{1,0:T(8,128)S(1)}, f32[40,128]{1,0:T(8,128)S(1)}, u32[]{:S(2)}, u32[]{:S(2)}) collective-permute-start(f32[40,128]{1,0:T(8,128)S(1)} %reduce_sum.9), channel_id=1, source_target_pairs={{0,64},{64,0},{1,65},{65,1},{2,66},{66,2},{3,67},{67,3},{4,68},{68... | collective-permute-start | bytes 61448 | tf_op jit(solution)/shard_map/ppermute | solution.py:18
  45.1 4.7 %collective-permute-start.7 = (f32[40,128]{1,0:T(8,128)S(1)}, f32[40,128]{1,0:T(8,128)S(1)}, u32[]{:S(2)}, u32[]{:S(2)}) collective-permute-start(f32[40,128]{1,0:T(8,128)S(1)} %add.9), channel_id=1, source_target_pairs={{0,4},{4,0},{8,12},{12,8},{1,5},{5,1},{9,13},{13,9},{2,6},{6,2},{1... | collective-permute-start | bytes 61448 | tf_op jit(solution)/shard_map/ppermute | solution.py:29
  49.8 6.1 %collective-permute-start.8 = (f32[40,128]{1,0:T(8,128)S(1)}, f32[40,128]{1,0:T(8,128)S(1)}, u32[]{:S(2)}, u32[]{:S(2)}) collective-permute-start(f32[40,128]{1,0:T(8,128)S(1)} %add.10), channel_id=1, source_target_pairs={{0,12},{4,8},{8,4},{12,0},{1,13},{5,9},{9,5},{13,1},{2,14},{6,10},... | collective-permute-start | bytes 61448 | tf_op jit(solution)/shard_map/ppermute | solution.py:29
  56.7 13.2 %all-to-all-start.1 = ((bf16[32,40,128]{2,1,0:T(8,128)(2,1)}), bf16[32,40,128]{2,1,0:T(8,128)(2,1)S(1)}, u32[]{:S(2)}, u32[]{:S(2)}) async-start(bf16[32,40,128]{2,1,0:T(8,128)(2,1)} %broadcast_in_dim.2), calls=%async_computation.1 | async-start | bytes 655360 | tf_op jit(solution)/shard_map/all_to_all | solution.py:31

commit v6 on v5

--- a/solution.py
+++ b/solution.py
@@ -69,12 +69,14 @@
 
 
 def from_left(values):
-    return jnp.where(column(values.shape) == 0, 0.0, pltpu.roll(values, 1, axis=1))
+    rolled = pltpu.roll(values, 1, axis=1)
+    return jnp.where(column(values.shape) == 0, jnp.zeros_like(rolled), rolled)
 
 
 def from_right(values):
     width = values.shape[1]
-    return jnp.where(column(values.shape) == width - 1, 0.0, pltpu.roll(values, width - 1, axis=1))
+    rolled = pltpu.roll(values, width - 1, axis=1)
+    return jnp.where(column(values.shape) == width - 1, jnp.zeros_like(rolled), rolled)
 
 
 def product(left, right):
@@ -94,14 +96,16 @@
 
 
 def taps_of(slope):
-    return jnp.concatenate(
-        [from_right(slope).astype(BF16), slope.astype(BF16), from_left(slope).astype(BF16)], axis=0
-    )
+    slope = slope.astype(BF16)
+    return jnp.concatenate([from_right(slope), slope, from_left(slope)], axis=0)
 
 
 def conv_taps(weights, stacked, forward):
-    taps = product(weights, stacked)
-    chans = weights.shape[0] // 3
+    return join_taps(product(weights, stacked), forward)
+
+
+def join_taps(taps, forward):
+    chans = taps.shape[0] // 3
     left, right = (from_left, from_right) if forward else (from_right, from_left)
     return taps[chans : 2 * chans] + left(taps[:chans]) + right(taps[2 * chans :])
 
@@ -121,21 +125,25 @@
         taps_ref[j * chans : (j + 1) * chans] = jnp.concatenate([ref[i, j] for i in range(3)], axis=1)
 
 
-def prepare_weights(spatial_ref, epi_ref, up_ref, taps_ref, epi_taps_ref, back_ref, lift_ref, drop_ref):
+def prepare_weights(spatial_ref, epi_ref, up_ref, taps_ref, epi_taps_ref, back_ref, drop_ref):
     chans = spatial_ref.shape[2]
     forward_taps(spatial_ref, taps_ref)
     forward_taps(epi_ref, epi_taps_ref)
     stacked = jnp.concatenate(
         [jnp.concatenate([epi_ref[2 - s, j] for j in range(3)], axis=1) for s in range(3)], axis=0
     )
-    back_ref[...] = product_nt(unit(3 * chans), stacked).astype(BF16)
+    back = product_nt(unit(3 * chans), stacked).astype(BF16)
     turned = product_nt(unit(chans), up_ref[...]).astype(BF16)
     line = lax.broadcasted_iota(jnp.int32, (64, 16), 0)
     sub = lax.broadcasted_iota(jnp.int32, (64, 16), 1)
     match = sub == 4 * (line % 4) + line // 16
     for h in range(4):
         pick = jnp.where(match & ((line % 16) // 4 == h), 1.0, 0.0).astype(BF16)
-        lift_ref[h] = product(pick, up_ref[...]).astype(BF16)
+        lift = product(pick, up_ref[...]).astype(BF16)
+        back_ref[h, : 3 * chans] = jnp.concatenate([back, jnp.zeros((3 * chans, 64), BF16)], axis=1)
+        back_ref[h, 3 * chans :] = jnp.concatenate(
+            [jnp.zeros((64, 3 * chans), BF16), lift], axis=1
+        )
         drop_ref[h] = product_nt(turned, pick).astype(BF16)
 
 
@@ -153,7 +161,6 @@
     weight_ref,
     epi_taps_ref,
     back_ref,
-    lift_ref,
     drop_ref,
     light_ref,
     one_ref,
@@ -193,7 +200,7 @@
         one_ref[view, 0] = jnp.where(even, light_ref[view, last], light_ref[view, 0])
         two_ref[view, 0] = jnp.where(even, light_ref[view, 0], light_ref[view, last])
     prepare_weights(
-        spatial_ref, epi_ref, up_ref, weight_ref, epi_taps_ref, back_ref, lift_ref, drop_ref
+        spatial_ref, epi_ref, up_ref, weight_ref, epi_taps_ref, back_ref, drop_ref
     )
     for block in range(image_ref.shape[2] // size):
         cut = slice(block * size, (block + 1) * size)
@@ -236,11 +243,10 @@
             first_ref[cut] = first.astype(BF16)
 
 
-def main_rows(rows, firsts, dealt, grad_of, near, out_ref, epi_ref, back_ref, lift_ref, pay_ref, lift_out):
+def main_rows(rows, firsts, dealt, grad_of, near, out_ref, epi_ref, back_ref, pay_ref, lift_out):
     chans = out_ref.shape[2]
     three = 3 * chans
     lifted = [None, None]
-    up_total = None
     epi_left, epi_right, spatial_left, spatial_right = [], [], [], []
     before, after = sides("ang", 4)
     for slot, h in enumerate(rows):
@@ -251,8 +257,8 @@
             + [chosen(after, firsts[1][cut], firsts[2][cut]) for cut in cuts],
             axis=0,
         )
-        here = (lax.broadcasted_iota(jnp.int32, (64, chans), 0) % 16) // 4 == h
-        grads, slopes = [], []
+        here = (lax.broadcasted_iota(jnp.int32, dealt[1].shape, 0) % 16) // 4 == h
+        grads, slopes, seconds = [], [], []
         for v in range(4):
             window = stack[v * chans : (v + 3) * chans]
             total = conv_taps(epi_ref[...], window, True)
@@ -264,16 +270,17 @@
                 grads.append(grad)
                 own = stack[(v + 1) * chans : (v + 2) * chans]
                 second = (own.astype(F32) + total * gate).astype(BF16)
-                part = product(lift_ref[h], second)
-                lifted[v - 1] = part if slot == 0 else lifted[v - 1] + part
-                part = jnp.where(here, product_nt(dealt[v], second), 0.0)
-                up_total = part if up_total is None else up_total + part
-                epi_left.append(taps_of(slope))
-                epi_right.append(window)
+                seconds.append(second)
+                shown = jnp.where(here, dealt[v], jnp.zeros_like(dealt[v]))
+                epi_left.append(jnp.concatenate([taps_of(slope), shown], axis=0))
+                epi_right.append(jnp.concatenate([window, second], axis=0))
         slopes = jnp.concatenate(slopes, axis=0)
         for v in range(2):
-            moved = conv_taps(back_ref[...], slopes[v * chans : (v + 3) * chans], False)
-            first_grad = (grads[v] + moved).astype(BF16).astype(F32)
+            below = jnp.concatenate([slopes[v * chans : (v + 3) * chans], seconds[v]], axis=0)
+            both = product(back_ref[h], below)
+            part = both[three:]
+            lifted[v] = part if slot == 0 else lifted[v] + part
+            first_grad = (grads[v] + join_taps(both[:three], False)).astype(BF16).astype(F32)
             slope = first_grad * out_ref[v, slot]
             spatial_left.append(taps_of(slope))
             spatial_right.append(jnp.concatenate(near(v, h), axis=0))
@@ -285,9 +292,9 @@
     )
     pieces = (
         spatial[:, :128],
-        epi[:, :128],
-        jnp.concatenate([spatial[:, 128:], epi[:, 128:]], axis=1),
-        jnp.concatenate([up_total, jnp.zeros_like(up_total)], axis=1),
+        epi[:three, :128],
+        jnp.concatenate([spatial[:, 128:], epi[:three, 128:three]], axis=1),
+        jnp.concatenate([epi[three:, three:], jnp.zeros((64, 128 - chans), F32)], axis=1),
     )
     start = 0
     for piece in pieces:
@@ -311,7 +318,6 @@
     out_ref,
     epi_ref,
     back_ref,
-    lift_ref,
     drop_ref,
     pay_ref,
     lift_out,
@@ -337,7 +343,6 @@
         out_ref,
         epi_ref,
         back_ref,
-        lift_ref,
         pay_ref,
         lift_out,
     )
@@ -355,7 +360,6 @@
     out_ref,
     epi_ref,
     back_ref,
-    lift_ref,
     inner_pay_ref,
     pay_ref,
     lift_out,
@@ -376,7 +380,6 @@
         out_ref,
         epi_ref,
         back_ref,
-        lift_ref,
         pay_ref,
         lift_out,
     )
@@ -464,7 +467,6 @@
         spatial_taps,
         epi_taps,
         back_taps,
-        lift,
         drop,
         light_here,
         send_one,
@@ -479,8 +481,7 @@
             like((512, 512), BF16),
             taps,
             taps,
-            taps,
-            like((rows, 64, chans), BF16),
+            like((rows, 4 * chans, 4 * chans), BF16),
             like((rows, chans, 64), BF16),
             like(light.shape, BF16),
             edge_line,
@@ -529,7 +530,6 @@
         inner_out,
         epi_taps,
         back_taps,
-        lift,
         drop,
     )
     pay, edge_lift = local_call(
@@ -547,7 +547,6 @@
         edge_out,
         epi_taps,
         back_taps,
-        lift,
         inner_pay,
     )
     up = local_call(

time: 71 us -> 70.2 us (0.989)
  Pallas kernels: 11.3 us -> 9.78 us
    pallas_call x6, Pallas kernels: 11.3 us -> 9.78 us  [local_call(): pl.pallas_call(kernel, out_shape=shapes, scratch_shapes=scratch, in_specs...]
  transfers between devices with their start and end apart: 10 -> 10, of which waited for: 6 -> 6; matrix products, arithmetic and copies ran while one was open for 0% -> 0% of each run, Pallas kernels for 7% -> 6%
where the time goes in v6:
time: 70.2 us; the launch traced here: 70 us
  waiting for transfers between devices  23.5 us (33%)
  blocking collectives  18.8 us (27%)
  starting transfers between devices  16.4 us (23%)
  Pallas kernels  9.78 us (14%)
  local copies, waits for them, and re-layouts  0.76 us (1%)
  between operations  0.71 us (1%)
    all_to_all x1, blocking collectives, sum_everywhere(): lax.all_to_all(pay.reshape(16, rows // 16, 128), plane, split_axis=0, con...  18.8 us
    pallas_call x6, Pallas kernels, local_call(): pl.pallas_call(kernel, out_shape=shapes, scratch_shapes=scratch, in_specs...  9.78 us
    all_to_all x1, waiting for transfers between devices, sum_everywhere(): lax.all_to_all(spread, ('pair',) + plane, split_axis=0, concat_axis=0, ti...  7.95 us
    ppermute x3, starting transfers between devices, with_next_and_before(): one = lax.ppermute(first_send, axis, [(i, i ^ 1) for i in range(count)])  7.86 us
    ppermute x2, waiting for transfers between devices, sum_everywhere(): mine = mine + lax.ppermute(mine, 'quad', [(i, i ^ flip) for i in range(4)])  7.49 us
    all_to_all x1, starting transfers between devices, sum_everywhere(): lax.all_to_all(spread, ('pair',) + plane, split_axis=0, concat_axis=0, ti...  3.87 us
    ppermute x3, waiting for transfers between devices, with_next_and_before(): lax.ppermute(second_send, ('core',) + axes, pairs + [(j, i) for i, j in p...  3.73 us
    ppermute x2, starting transfers between devices, sum_everywhere(): mine = mine + lax.ppermute(mine, 'quad', [(i, i ^ flip) for i in range(4)])  3.28 us
  transfers between devices with their start and end apart: 10, of which 6 were waited for; matrix products, arithmetic and copies ran while one was open for 0% of the time, Pallas kernels for 6%

profile of v6, /device:TPU:64, one launch (start us, length us, event | category | flops | bytes accessed | tf_op | source)
XLA Modules:
  0.0 70.0 jit_solution(5009417940780488797)
XLA Ops:
  0.6 2.3 %inner.1 = (bf16[320,512]{1,0:T(8,128)(2,1)S(1)}, bf16[320,512]{1,0:T(8,128)(2,1)S(1)}, bf16[2,64,512]{2,1,0:T(8,128)(2,1)S(1)}, f32[2,2,64,512]{3,2,1,0:T(8,128...) custom-call(bf16[2,16,2048]{2,1,0:T(8,128)(2,1)} %bitcast.8, ...), custom_call_target="tpu_custom_call" | custom-call | flops 3000000000 | bytes 9000000 | tf_op jit(solution)/shard_map/inner/pallas_call | solution.py:434
  3.0 1.6 %collective-permute-start.2 = (bf16[2,1,64,512]{3,2,1,0:T(8,128)(2,1)S(1)}, bf16[2,1,64,512]{3,2,1,0:T(8,128)(2,1)S(1)}, u32[]{:S(2)}, u32[]{:S(2)}) collective-permute-start(bf16[2,1,64,512]{3,2,1,0:T(8,128)(2,1)S(1)} %get-tuple-element.35), channel_id=1, source_target_pairs={{0,1},{1,0},{2,3},{3,2},{4,5},{5,4},{6,7},{7,6},{8,9},{9,8},{10,11... | collective-permute-start | bytes 393224 | tf_op jit(solution)/shard_map/ppermute | solution.py:46
  4.5 1.2 %collective-permute-start.3 = (bf16[2,1,64,512]{3,2,1,0:T(8,128)(2,1)S(1)}, bf16[2,1,64,512]{3,2,1,0:T(8,128)(2,1)S(1)}, u32[]{:S(2)}, u32[]{:S(2)}) collective-permute-start(bf16[2,1,64,512]{3,2,1,0:T(8,128)(2,1)S(1)} %get-tuple-element.36), channel_id=1, source_target_pairs={{15,79},{0,64},{1,2},{3,4},{5,6},{7,8},{9,10},{11,12},{13,14},{65,... | collective-permute-start | bytes 393224 | tf_op jit(solution)/shard_map/ppermute | solution.py:45
  5.7 0.0 collective-permute-start.1
  5.7 3.1 %collective-permute-start = (bf16[320,512]{1,0:T(8,128)(2,1)S(1)}, bf16[320,512]{1,0:T(8,128)(2,1)S(1)}, u32[]{:S(2)}, u32[]{:S(2)}) collective-permute-start(bf16[320,512]{1,0:T(8,128)(2,1)S(1)} %get-tuple-element.26.own_ref), channel_id=1, source_target_pairs={{0,16},{16,0},{32,48},{48,32},{1,17},{17,1},{33,49},{49,33},{2,18}... | collective-permute-start | bytes 983048 | tf_op jit(solution)/shard_map/ppermute | solution.py:46
  8.9 0.0 collective-permute-done.2.one_ref
  8.9 3.7 %collective-permute-done.3.two_ref = bf16[2,1,64,512]{3,2,1,0:T(8,128)(2,1)S(1)} collective-permute-done((bf16[2,1,64,512]{3,2,1,0:T(8,128)(2,1)S(1)}, bf16[2,1,64,512]{3,2,1,0:T(8,128)(2,1)S(1)}, u32[]{:S(2)}, u32[]{:S(2)}) %collective-permute-start.3) | collective-permute-done | bytes 131104 | tf_op jit(solution)/shard_map/ppermute | solution.py:45
  12.6 0.6 edge.1
  13.2 0.1 collective-permute-start.5
  13.3 3.1 %collective-permute-start.4 = (bf16[256,512]{1,0:T(8,128)(2,1)S(1)}, bf16[256,512]{1,0:T(8,128)(2,1)S(1)}, u32[]{:S(2)}, u32[]{:S(2)}) collective-permute-start(bf16[256,512]{1,0:T(8,128)(2,1)S(1)} %get-tuple-element.38.first_ref), channel_id=1, source_target_pairs={{0,16},{16,0},{32,48},{48,32},{1,17},{17,1},{33,49},{49,33},{2,18}... | collective-permute-start | bytes 786440 | tf_op jit(solution)/shard_map/ppermute | solution.py:46
  16.4 0.0 collective-permute-done.1.mixed_two_ref
  16.4 0.0 collective-permute-done.mixed_one_ref
  16.4 2.5 %main_inner.1 = (f32[640,128]{1,0:T(8,128)S(1)}, bf16[2,64,512]{2,1,0:T(8,128)(2,1)S(1)}, bf16[2,4,64,512]{3,2,1,0:T(8,128)(2,1)S(1)}) custom-call(bf16[320,512]{1,0:T(8,128)(2,1)S(1)} %get-tuple-element.26.own_ref, bf16[320,512]{1,0:T(8,128)(2,1)S(1)} %collective-permute-done.mixed_one_ref, bf16[320,512]{1,0:T(8,128)(2,1)S(1)} %collective-permute-done.1.mixed_two_ref, ...), custom_call_target="tpu_custom_call" | custom-call | flops 3000000000 | bytes 9000000 | tf_op jit(solution)/shard_map/main_inner/pallas_call | solution.py:434
  18.9 0.0 collective-permute-done.5.first_two_ref
  18.9 3.1 %collective-permute-done.4.first_one_ref = bf16[256,512]{1,0:T(8,128)(2,1)S(1)} collective-permute-done((bf16[256,512]{1,0:T(8,128)(2,1)S(1)}, bf16[256,512]{1,0:T(8,128)(2,1)S(1)}, u32[]{:S(2)}, u32[]{:S(2)}) %collective-permute-start.4) | collective-permute-done | bytes 262176 | tf_op jit(solution)/shard_map/ppermute | solution.py:46
  22.0 2.2 %main_edge.1 = (f32[640,128]{1,0:T(8,128)S(1)}, bf16[2,64,512]{2,1,0:T(8,128)(2,1)S(1)}) custom-call(bf16[256,512]{1,0:T(8,128)(2,1)S(1)} %get-tuple-element.38.first_ref, bf16[256,512]{1,0:T(8,128)(2,1)S(1)} %collective-permute-done.4.first_one_ref, bf16[256,512]{1,0:T(8,128)(2,1)S(1)} %collective-permute-done.5.first_two_ref, ...), custom_call_target="tpu_custom_call" | custom-call | flops 3000000000 | bytes 9000000 | tf_op jit(solution)/shard_map/main_edge/pallas_call | solution.py:434
  24.2 18.8 %all_to_all.10 = f32[16,40,128]{2,1,0:T(8,128)S(1)} all-to-all(f32[16,40,128]{2,1,0:T(8,128)S(1)} %bitcast.6), channel_id=1, replica_groups=mesh['pair'=2,'core'=2,'ang'=4,'quad'=4,'x'=4] {'ang','x'}, dimensions={0} | all-to-all | bytes 655360 | tf_op jit(solution)/shard_map/all_to_all | solution.py:24
  43.0 0.1 collective-permute-start.6
  43.1 1.2 %collective-permute-done.6 = f32[40,128]{1,0:T(8,128)S(1)} collective-permute-done((f32[40,128]{1,0:T(8,128)S(1)}, f32[40,128]{1,0:T(8,128)S(1)}, u32[]{:S(2)}, u32[]{:S(2)}) %collective-permute-start.6) | collective-permute-done | bytes 20512 | tf_op jit(solution)/shard_map/ppermute | solution.py:18
  44.3 0.0 collective-permute-start.7
  44.3 4.7 %collective-permute-done.7 = f32[40,128]{1,0:T(8,128)S(1)} collective-permute-done((f32[40,128]{1,0:T(8,128)S(1)}, f32[40,128]{1,0:T(8,128)S(1)}, u32[]{:S(2)}, u32[]{:S(2)}) %collective-permute-start.7) | collective-permute-done | bytes 20512 | tf_op jit(solution)/shard_map/ppermute | solution.py:29
  49.0 3.3 %collective-permute-start.8 = (f32[40,128]{1,0:T(8,128)S(1)}, f32[40,128]{1,0:T(8,128)S(1)}, u32[]{:S(2)}, u32[]{:S(2)}) collective-permute-start(f32[40,128]{1,0:T(8,128)S(1)} %add.10), channel_id=1, source_target_pairs={{0,12},{4,8},{8,4},{12,0},{1,13},{5,9},{9,5},{13,1},{2,14},{6,10},... | collective-permute-start | bytes 61448 | tf_op jit(solution)/shard_map/ppermute | solution.py:29
  52.3 2.8 %collective-permute-done.8 = f32[40,128]{1,0:T(8,128)S(1)} collective-permute-done((f32[40,128]{1,0:T(8,128)S(1)}, f32[40,128]{1,0:T(8,128)S(1)}, u32[]{:S(2)}, u32[]{:S(2)}) %collective-permute-start.8) | collective-permute-done | bytes 20512 | tf_op jit(solution)/shard_map/ppermute | solution.py:29
  55.1 0.8 %broadcast_in_dim.2 = bf16[32,40,128]{2,1,0:T(8,128)(2,1)} broadcast(bf16[40,128]{1,0:T(8,128)(2,1)S(1)} %add_convert_fusion), dimensions={1,2} | broadcast | bytes 337920 | tf_op jit(solution)/shard_map/broadcast_in_dim | solution.py:30
  55.9 3.9 %all-to-all-start.1 = ((bf16[32,40,128]{2,1,0:T(8,128)(2,1)}), bf16[32,40,128]{2,1,0:T(8,128)(2,1)S(1)}, u32[]{:S(2)}, u32[]{:S(2)}) async-start(bf16[32,40,128]{2,1,0:T(8,128)(2,1)} %broadcast_in_dim.2), calls=%async_computation.1 | async-start | bytes 655360 | tf_op jit(solution)/shard_map/all_to_all | solution.py:31
  59.7 1.4 %weave.1 = bf16[2,16,2048]{2,1,0:T(8,128)(2,1)} custom-call(bf16[2,64,512]{2,1,0:T(8,128)(2,1)S(1)} %get-tuple-element.34.inner_ref, bf16[2,64,512]{2,1,0:T(8,128)(2,1)S(1)} %get-tuple-element.42.edge_ref, bf16[512,512]{1,0:T(8,128)(2,1)S(1)} %get-tuple-element.43.deal_ref), custom_call_target="tpu_custom_call" | custom-call | flops 3000000000 | bytes 9000000 | tf_op jit(solution)/shard_map/weave/pallas_call | solution.py:434
  61.1 8.0 %all-to-all-done.1 = bf16[32,40,128]{2,1,0:T(8,128)(2,1)S(1)} async-done(((bf16[32,40,128]{2,1,0:T(8,128)(2,1)}), bf16[32,40,128]{2,1,0:T(8,128)(2,1)S(1)}, u32[]{:S(2)}, u32[]{:S(2)}) %all-to-all-start.1) | async-done | bytes 327712 | tf_op jit(solution)/shard_map/all_to_all | solution.py:31
  69.1 0.9 %unpack.1 = (f32[3,3,64,64]{3,2,1,0:T(8,128)}, f32[3,3,64,64]{3,2,1,0:T(8,128)}, f32[16,64]{1,0:T(8,128)}) custom-call(bf16[2,640,128]{2,1,0:T(8,128)(2,1)S(1)} %bitcast.5), custom_call_target="tpu_custom_call" | custom-call | flops 3000000000 | bytes 9000000 | tf_op jit(solution)/shard_map/unpack/pallas_call | solution.py:434
  (4 shorter events, 0.0 us)
Async XLA Ops:
  3.0 5.9 %collective-permute-start.2 = (bf16[2,1,64,512]{3,2,1,0:T(8,128)(2,1)S(1)}, bf16[2,1,64,512]{3,2,1,0:T(8,128)(2,1)S(1)}, u32[]{:S(2)}, u32[]{:S(2)}) collective-permute-start(bf16[2,1,64,512]{3,2,1,0:T(8,128)(2,1)S(1)} %get-tuple-element.35), channel_id=1, source_target_pairs={{0,1},{1,0},{2,3},{3,2},{4,5},{5,4},{6,7},{7,6},{8,9},{9,8},{10,11... | collective-permute-start | bytes 393224 | tf_op jit(solution)/shard_map/ppermute | solution.py:46
  4.5 8.1 %collective-permute-start.3 = (bf16[2,1,64,512]{3,2,1,0:T(8,128)(2,1)S(1)}, bf16[2,1,64,512]{3,2,1,0:T(8,128)(2,1)S(1)}, u32[]{:S(2)}, u32[]{:S(2)}) collective-permute-start(bf16[2,1,64,512]{3,2,1,0:T(8,128)(2,1)S(1)} %get-tuple-element.36), channel_id=1, source_target_pairs={{15,79},{0,64},{1,2},{3,4},{5,6},{7,8},{9,10},{11,12},{13,14},{65,... | collective-permute-start | bytes 393224 | tf_op jit(solution)/shard_map/ppermute | solution.py:45
  5.7 10.7 %collective-permute-start.1 = (bf16[320,512]{1,0:T(8,128)(2,1)S(1)}, bf16[320,512]{1,0:T(8,128)(2,1)S(1)}, u32[]{:S(2)}, u32[]{:S(2)}) collective-permute-start(bf16[320,512]{1,0:T(8,128)(2,1)S(1)} %get-tuple-element.27), channel_id=1, source_target_pairs={{48,112},{0,64},{16,32},{80,96},{112,48},{64,0},{32,16},{96,80},{4... | collective-permute-start | bytes 983048 | tf_op jit(solution)/shard_map/ppermute | solution.py:45
  5.7 10.7 %collective-permute-start = (bf16[320,512]{1,0:T(8,128)(2,1)S(1)}, bf16[320,512]{1,0:T(8,128)(2,1)S(1)}, u32[]{:S(2)}, u32[]{:S(2)}) collective-permute-start(bf16[320,512]{1,0:T(8,128)(2,1)S(1)} %get-tuple-element.26.own_ref), channel_id=1, source_target_pairs={{0,16},{16,0},{32,48},{48,32},{1,17},{17,1},{33,49},{49,33},{2,18}... | collective-permute-start | bytes 983048 | tf_op jit(solution)/shard_map/ppermute | solution.py:46
  13.2 5.7 %collective-permute-start.5 = (bf16[256,512]{1,0:T(8,128)(2,1)S(1)}, bf16[256,512]{1,0:T(8,128)(2,1)S(1)}, u32[]{:S(2)}, u32[]{:S(2)}) collective-permute-start(bf16[256,512]{1,0:T(8,128)(2,1)S(1)} %get-tuple-element.38.first_ref), channel_id=1, source_target_pairs={{48,112},{0,64},{16,32},{80,96},{112,48},{64,0},{32,16},{96,80},{4... | collective-permute-start | bytes 786440 | tf_op jit(solution)/shard_map/ppermute | solution.py:45
  13.3 8.7 %collective-permute-start.4 = (bf16[256,512]{1,0:T(8,128)(2,1)S(1)}, bf16[256,512]{1,0:T(8,128)(2,1)S(1)}, u32[]{:S(2)}, u32[]{:S(2)}) collective-permute-start(bf16[256,512]{1,0:T(8,128)(2,1)S(1)} %get-tuple-element.38.first_ref), channel_id=1, source_target_pairs={{0,16},{16,0},{32,48},{48,32},{1,17},{17,1},{33,49},{49,33},{2,18}... | collective-permute-start | bytes 786440 | tf_op jit(solution)/shard_map/ppermute | solution.py:46
  43.0 1.3 %collective-permute-start.6 = (f32[40,128]{1,0:T(8,128)S(1)}, f32[40,128]{1,0:T(8,128)S(1)}, u32[]{:S(2)}, u32[]{:S(2)}) collective-permute-start(f32[40,128]{1,0:T(8,128)S(1)} %reduce_sum.9), channel_id=1, source_target_pairs={{0,64},{64,0},{1,65},{65,1},{2,66},{66,2},{3,67},{67,3},{4,68},{68... | collective-permute-start | bytes 61448 | tf_op jit(solution)/shard_map/ppermute | solution.py:18
  44.3 4.7 %collective-permute-start.7 = (f32[40,128]{1,0:T(8,128)S(1)}, f32[40,128]{1,0:T(8,128)S(1)}, u32[]{:S(2)}, u32[]{:S(2)}) collective-permute-start(f32[40,128]{1,0:T(8,128)S(1)} %add.9), channel_id=1, source_target_pairs={{0,4},{4,0},{8,12},{12,8},{1,5},{5,1},{9,13},{13,9},{2,6},{6,2},{1... | collective-permute-start | bytes 61448 | tf_op jit(solution)/shard_map/ppermute | solution.py:29
  49.0 6.1 %collective-permute-start.8 = (f32[40,128]{1,0:T(8,128)S(1)}, f32[40,128]{1,0:T(8,128)S(1)}, u32[]{:S(2)}, u32[]{:S(2)}) collective-permute-start(f32[40,128]{1,0:T(8,128)S(1)} %add.10), channel_id=1, source_target_pairs={{0,12},{4,8},{8,4},{12,0},{1,13},{5,9},{9,5},{13,1},{2,14},{6,10},... | collective-permute-start | bytes 61448 | tf_op jit(solution)/shard_map/ppermute | solution.py:29
  55.9 13.2 %all-to-all-start.1 = ((bf16[32,40,128]{2,1,0:T(8,128)(2,1)}), bf16[32,40,128]{2,1,0:T(8,128)(2,1)S(1)}, u32[]{:S(2)}, u32[]{:S(2)}) async-start(bf16[32,40,128]{2,1,0:T(8,128)(2,1)} %broadcast_in_dim.2), calls=%async_computation.1 | async-start | bytes 655360 | tf_op jit(solution)/shard_map/all_to_all | solution.py:31

commit v7 on v6

--- a/solution.py
+++ b/solution.py
@@ -226,7 +226,7 @@
             mixed_two_ref[cut] = first
 
 
-def edge_kernel(light_ref, one_ref, two_ref, weight_ref, first_ref, out_ref):
+def edge_kernel(light_ref, two_ref, one_ref, weight_ref, first_ref, out_ref):
     chans = light_ref.shape[2]
     above, below = sides(ROWS, 16)
     for view in range(2):
@@ -355,8 +355,8 @@
     dealt_ref,
     edge_grad_ref,
     light_ref,
+    two_ref,
     one_ref,
-    two_ref,
     out_ref,
     epi_ref,
     back_ref,
@@ -510,8 +510,8 @@
         (like((4 * chans, breadth), BF16), half_out),
         "edge",
         light,
+        line_two,
         line_one,
-        line_two,
         spatial_taps,
     )
     first_one, first_two = with_next_and_before(first, first, "ang")
@@ -542,8 +542,8 @@
         dealt,
         edge_grad,
         light,
+        line_two,
         line_one,
-        line_two,
         edge_out,
         epi_taps,
         back_taps,

time: 70.2 us -> 69.5 us (0.990)
    ppermute x3, waiting for transfers between devices: 3.73 us -> 2.22 us  [with_next_and_before(): lax.ppermute(second_send, ('core',) + axes, pairs + [(j, i) for i, j in p...]
    ppermute x3, waiting for transfers between devices: 3.11 us -> 4.1 us  [with_next_and_before(): one = lax.ppermute(first_send, axis, [(i, i ^ 1) for i in range(count)])]
    ppermute x3, starting transfers between devices: 1.28 us -> 2.03 us  [with_next_and_before(): lax.ppermute(second_send, ('core',) + axes, pairs + [(j, i) for i, j in p...]
  transfers between devices with their start and end apart: 10 -> 10, of which waited for: 6 -> 7; matrix products, arithmetic and copies ran while one was open for 0% -> 0% of each run, Pallas kernels for 6% -> 6%
where the time goes in v7:
time: 69.5 us; the launch traced here: 69.3 us
  waiting for transfers between devices  22.8 us (33%)
  blocking collectives  18.5 us (27%)
  starting transfers between devices  16.7 us (24%)
  Pallas kernels  9.78 us (14%)
  local copies, waits for them, and re-layouts  0.76 us (1%)
  between operations  0.71 us (1%)
    all_to_all x1, blocking collectives, sum_everywhere(): lax.all_to_all(pay.reshape(16, rows // 16, 128), plane, split_axis=0, con...  18.5 us
    pallas_call x6, Pallas kernels, local_call(): pl.pallas_call(kernel, out_shape=shapes, scratch_shapes=scratch, in_specs...  9.78 us
    all_to_all x1, waiting for transfers between devices, sum_everywhere(): lax.all_to_all(spread, ('pair',) + plane, split_axis=0, concat_axis=0, ti...  7.95 us
    ppermute x3, starting transfers between devices, with_next_and_before(): one = lax.ppermute(first_send, axis, [(i, i ^ 1) for i in range(count)])  7.42 us
    ppermute x2, waiting for transfers between devices, sum_everywhere(): mine = mine + lax.ppermute(mine, 'quad', [(i, i ^ flip) for i in range(4)])  7.31 us
    ppermute x3, waiting for transfers between devices, with_next_and_before(): one = lax.ppermute(first_send, axis, [(i, i ^ 1) for i in range(count)])  4.1 us
    all_to_all x1, starting transfers between devices, sum_everywhere(): lax.all_to_all(spread, ('pair',) + plane, split_axis=0, concat_axis=0, ti...  3.87 us
    ppermute x2, starting transfers between devices, sum_everywhere(): mine = mine + lax.ppermute(mine, 'quad', [(i, i ^ flip) for i in range(4)])  3.26 us
  transfers between devices with their start and end apart: 10, of which 7 were waited for; matrix products, arithmetic and copies ran while one was open for 0% of the time, Pallas kernels for 6%

profile of v7, /device:TPU:64, one launch (start us, length us, event | category | flops | bytes accessed | tf_op | source)
XLA Modules:
  0.0 69.3 jit_solution(16708858868380251499)
XLA Ops:
  0.6 2.3 %inner.1 = (bf16[320,512]{1,0:T(8,128)(2,1)S(1)}, bf16[320,512]{1,0:T(8,128)(2,1)S(1)}, bf16[2,64,512]{2,1,0:T(8,128)(2,1)S(1)}, f32[2,2,64,512]{3,2,1,0:T(8,128...) custom-call(bf16[2,16,2048]{2,1,0:T(8,128)(2,1)} %bitcast.8, ...), custom_call_target="tpu_custom_call" | custom-call | flops 3000000000 | bytes 9000000 | tf_op jit(solution)/shard_map/inner/pallas_call | solution.py:434
  3.0 1.9 %collective-permute-start.2 = (bf16[2,1,64,512]{3,2,1,0:T(8,128)(2,1)S(1)}, bf16[2,1,64,512]{3,2,1,0:T(8,128)(2,1)S(1)}, u32[]{:S(2)}, u32[]{:S(2)}) collective-permute-start(bf16[2,1,64,512]{3,2,1,0:T(8,128)(2,1)S(1)} %get-tuple-element.35), channel_id=1, source_target_pairs={{15,79},{0,64},{1,2},{3,4},{5,6},{7,8},{9,10},{11,12},{13,14},{65,... | collective-permute-start | bytes 393224 | tf_op jit(solution)/shard_map/ppermute | solution.py:45
  4.9 1.1 %collective-permute-start.3 = (bf16[2,1,64,512]{3,2,1,0:T(8,128)(2,1)S(1)}, bf16[2,1,64,512]{3,2,1,0:T(8,128)(2,1)S(1)}, u32[]{:S(2)}, u32[]{:S(2)}) collective-permute-start(bf16[2,1,64,512]{3,2,1,0:T(8,128)(2,1)S(1)} %get-tuple-element.36), channel_id=1, source_target_pairs={{0,1},{1,0},{2,3},{3,2},{4,5},{5,4},{6,7},{7,6},{8,9},{9,8},{10,11... | collective-permute-start | bytes 393224 | tf_op jit(solution)/shard_map/ppermute | solution.py:46
  6.0 0.0 collective-permute-start.1
  6.0 3.2 %collective-permute-start = (bf16[320,512]{1,0:T(8,128)(2,1)S(1)}, bf16[320,512]{1,0:T(8,128)(2,1)S(1)}, u32[]{:S(2)}, u32[]{:S(2)}) collective-permute-start(bf16[320,512]{1,0:T(8,128)(2,1)S(1)} %get-tuple-element.26.own_ref), channel_id=1, source_target_pairs={{0,16},{16,0},{32,48},{48,32},{1,17},{17,1},{33,49},{49,33},{2,18}... | collective-permute-start | bytes 983048 | tf_op jit(solution)/shard_map/ppermute | solution.py:46
  9.2 2.2 %collective-permute-done.2.two_ref = bf16[2,1,64,512]{3,2,1,0:T(8,128)(2,1)S(1)} collective-permute-done((bf16[2,1,64,512]{3,2,1,0:T(8,128)(2,1)S(1)}, bf16[2,1,64,512]{3,2,1,0:T(8,128)(2,1)S(1)}, u32[]{:S(2)}, u32[]{:S(2)}) %collective-permute-start.2) | collective-permute-done | bytes 131104 | tf_op jit(solution)/shard_map/ppermute | solution.py:45
  11.4 0.0 collective-permute-done.3.one_ref
  11.4 0.6 edge.1
  12.0 0.1 collective-permute-start.5
  12.1 3.1 %collective-permute-start.4 = (bf16[256,512]{1,0:T(8,128)(2,1)S(1)}, bf16[256,512]{1,0:T(8,128)(2,1)S(1)}, u32[]{:S(2)}, u32[]{:S(2)}) collective-permute-start(bf16[256,512]{1,0:T(8,128)(2,1)S(1)} %get-tuple-element.38.first_ref), channel_id=1, source_target_pairs={{0,16},{16,0},{32,48},{48,32},{1,17},{17,1},{33,49},{49,33},{2,18}... | collective-permute-start | bytes 786440 | tf_op jit(solution)/shard_map/ppermute | solution.py:46
  15.2 0.0 collective-permute-done.1.mixed_two_ref
  15.2 1.9 %collective-permute-done.mixed_one_ref = bf16[320,512]{1,0:T(8,128)(2,1)S(1)} collective-permute-done((bf16[320,512]{1,0:T(8,128)(2,1)S(1)}, bf16[320,512]{1,0:T(8,128)(2,1)S(1)}, u32[]{:S(2)}, u32[]{:S(2)}) %collective-permute-start) | collective-permute-done | bytes 327712 | tf_op jit(solution)/shard_map/ppermute | solution.py:46
  17.1 2.5 %main_inner.1 = (f32[640,128]{1,0:T(8,128)S(1)}, bf16[2,64,512]{2,1,0:T(8,128)(2,1)S(1)}, bf16[2,4,64,512]{3,2,1,0:T(8,128)(2,1)S(1)}) custom-call(bf16[320,512]{1,0:T(8,128)(2,1)S(1)} %get-tuple-element.26.own_ref, bf16[320,512]{1,0:T(8,128)(2,1)S(1)} %collective-permute-done.mixed_one_ref, bf16[320,512]{1,0:T(8,128)(2,1)S(1)} %collective-permute-done.1.mixed_two_ref, ...), custom_call_target="tpu_custom_call" | custom-call | flops 3000000000 | bytes 9000000 | tf_op jit(solution)/shard_map/main_inner/pallas_call | solution.py:434
  19.5 0.0 collective-permute-done.5.first_two_ref
  19.6 2.2 %collective-permute-done.4.first_one_ref = bf16[256,512]{1,0:T(8,128)(2,1)S(1)} collective-permute-done((bf16[256,512]{1,0:T(8,128)(2,1)S(1)}, bf16[256,512]{1,0:T(8,128)(2,1)S(1)}, u32[]{:S(2)}, u32[]{:S(2)}) %collective-permute-start.4) | collective-permute-done | bytes 262176 | tf_op jit(solution)/shard_map/ppermute | solution.py:46
  21.8 2.2 %main_edge.1 = (f32[640,128]{1,0:T(8,128)S(1)}, bf16[2,64,512]{2,1,0:T(8,128)(2,1)S(1)}) custom-call(bf16[256,512]{1,0:T(8,128)(2,1)S(1)} %get-tuple-element.38.first_ref, bf16[256,512]{1,0:T(8,128)(2,1)S(1)} %collective-permute-done.4.first_one_ref, bf16[256,512]{1,0:T(8,128)(2,1)S(1)} %collective-permute-done.5.first_two_ref, ...), custom_call_target="tpu_custom_call" | custom-call | flops 3000000000 | bytes 9000000 | tf_op jit(solution)/shard_map/main_edge/pallas_call | solution.py:434
  23.9 18.5 %all_to_all.10 = f32[16,40,128]{2,1,0:T(8,128)S(1)} all-to-all(f32[16,40,128]{2,1,0:T(8,128)S(1)} %bitcast.6), channel_id=1, replica_groups=mesh['pair'=2,'core'=2,'ang'=4,'quad'=4,'x'=4] {'ang','x'}, dimensions={0} | all-to-all | bytes 655360 | tf_op jit(solution)/shard_map/all_to_all | solution.py:24
  42.5 0.1 collective-permute-start.6
  42.6 1.2 %collective-permute-done.6 = f32[40,128]{1,0:T(8,128)S(1)} collective-permute-done((f32[40,128]{1,0:T(8,128)S(1)}, f32[40,128]{1,0:T(8,128)S(1)}, u32[]{:S(2)}, u32[]{:S(2)}) %collective-permute-start.6) | collective-permute-done | bytes 20512 | tf_op jit(solution)/shard_map/ppermute | solution.py:18
  43.8 0.0 collective-permute-start.7
  43.8 4.7 %collective-permute-done.7 = f32[40,128]{1,0:T(8,128)S(1)} collective-permute-done((f32[40,128]{1,0:T(8,128)S(1)}, f32[40,128]{1,0:T(8,128)S(1)}, u32[]{:S(2)}, u32[]{:S(2)}) %collective-permute-start.7) | collective-permute-done | bytes 20512 | tf_op jit(solution)/shard_map/ppermute | solution.py:29
  48.5 3.3 %collective-permute-start.8 = (f32[40,128]{1,0:T(8,128)S(1)}, f32[40,128]{1,0:T(8,128)S(1)}, u32[]{:S(2)}, u32[]{:S(2)}) collective-permute-start(f32[40,128]{1,0:T(8,128)S(1)} %add.10), channel_id=1, source_target_pairs={{0,12},{4,8},{8,4},{12,0},{1,13},{5,9},{9,5},{13,1},{2,14},{6,10},... | collective-permute-start | bytes 61448 | tf_op jit(solution)/shard_map/ppermute | solution.py:29
  51.7 2.6 %collective-permute-done.8 = f32[40,128]{1,0:T(8,128)S(1)} collective-permute-done((f32[40,128]{1,0:T(8,128)S(1)}, f32[40,128]{1,0:T(8,128)S(1)}, u32[]{:S(2)}, u32[]{:S(2)}) %collective-permute-start.8) | collective-permute-done | bytes 20512 | tf_op jit(solution)/shard_map/ppermute | solution.py:29
  54.4 0.8 %broadcast_in_dim.2 = bf16[32,40,128]{2,1,0:T(8,128)(2,1)} broadcast(bf16[40,128]{1,0:T(8,128)(2,1)S(1)} %add_convert_fusion), dimensions={1,2} | broadcast | bytes 337920 | tf_op jit(solution)/shard_map/broadcast_in_dim | solution.py:30
  55.1 3.9 %all-to-all-start.1 = ((bf16[32,40,128]{2,1,0:T(8,128)(2,1)}), bf16[32,40,128]{2,1,0:T(8,128)(2,1)S(1)}, u32[]{:S(2)}, u32[]{:S(2)}) async-start(bf16[32,40,128]{2,1,0:T(8,128)(2,1)} %broadcast_in_dim.2), calls=%async_computation.1 | async-start | bytes 655360 | tf_op jit(solution)/shard_map/all_to_all | solution.py:31
  59.0 1.4 %weave.1 = bf16[2,16,2048]{2,1,0:T(8,128)(2,1)} custom-call(bf16[2,64,512]{2,1,0:T(8,128)(2,1)S(1)} %get-tuple-element.34.inner_ref, bf16[2,64,512]{2,1,0:T(8,128)(2,1)S(1)} %get-tuple-element.42.edge_ref, bf16[512,512]{1,0:T(8,128)(2,1)S(1)} %get-tuple-element.43.deal_ref), custom_call_target="tpu_custom_call" | custom-call | flops 3000000000 | bytes 9000000 | tf_op jit(solution)/shard_map/weave/pallas_call | solution.py:434
  60.4 8.0 %all-to-all-done.1 = bf16[32,40,128]{2,1,0:T(8,128)(2,1)S(1)} async-done(((bf16[32,40,128]{2,1,0:T(8,128)(2,1)}), bf16[32,40,128]{2,1,0:T(8,128)(2,1)S(1)}, u32[]{:S(2)}, u32[]{:S(2)}) %all-to-all-start.1) | async-done | bytes 327712 | tf_op jit(solution)/shard_map/all_to_all | solution.py:31
  68.3 0.9 %unpack.1 = (f32[3,3,64,64]{3,2,1,0:T(8,128)}, f32[3,3,64,64]{3,2,1,0:T(8,128)}, f32[16,64]{1,0:T(8,128)}) custom-call(bf16[2,640,128]{2,1,0:T(8,128)(2,1)S(1)} %bitcast.5), custom_call_target="tpu_custom_call" | custom-call | flops 3000000000 | bytes 9000000 | tf_op jit(solution)/shard_map/unpack/pallas_call | solution.py:434
  (4 shorter events, 0.0 us)
Async XLA Ops:
  3.0 8.4 %collective-permute-start.2 = (bf16[2,1,64,512]{3,2,1,0:T(8,128)(2,1)S(1)}, bf16[2,1,64,512]{3,2,1,0:T(8,128)(2,1)S(1)}, u32[]{:S(2)}, u32[]{:S(2)}) collective-permute-start(bf16[2,1,64,512]{3,2,1,0:T(8,128)(2,1)S(1)} %get-tuple-element.35), channel_id=1, source_target_pairs={{15,79},{0,64},{1,2},{3,4},{5,6},{7,8},{9,10},{11,12},{13,14},{65,... | collective-permute-start | bytes 393224 | tf_op jit(solution)/shard_map/ppermute | solution.py:45
  4.9 6.5 %collective-permute-start.3 = (bf16[2,1,64,512]{3,2,1,0:T(8,128)(2,1)S(1)}, bf16[2,1,64,512]{3,2,1,0:T(8,128)(2,1)S(1)}, u32[]{:S(2)}, u32[]{:S(2)}) collective-permute-start(bf16[2,1,64,512]{3,2,1,0:T(8,128)(2,1)S(1)} %get-tuple-element.36), channel_id=1, source_target_pairs={{0,1},{1,0},{2,3},{3,2},{4,5},{5,4},{6,7},{7,6},{8,9},{9,8},{10,11... | collective-permute-start | bytes 393224 | tf_op jit(solution)/shard_map/ppermute | solution.py:46
  6.0 9.2 %collective-permute-start.1 = (bf16[320,512]{1,0:T(8,128)(2,1)S(1)}, bf16[320,512]{1,0:T(8,128)(2,1)S(1)}, u32[]{:S(2)}, u32[]{:S(2)}) collective-permute-start(bf16[320,512]{1,0:T(8,128)(2,1)S(1)} %get-tuple-element.27), channel_id=1, source_target_pairs={{48,112},{0,64},{16,32},{80,96},{112,48},{64,0},{32,16},{96,80},{4... | collective-permute-start | bytes 983048 | tf_op jit(solution)/shard_map/ppermute | solution.py:45
  6.0 11.0 %collective-permute-start = (bf16[320,512]{1,0:T(8,128)(2,1)S(1)}, bf16[320,512]{1,0:T(8,128)(2,1)S(1)}, u32[]{:S(2)}, u32[]{:S(2)}) collective-permute-start(bf16[320,512]{1,0:T(8,128)(2,1)S(1)} %get-tuple-element.26.own_ref), channel_id=1, source_target_pairs={{0,16},{16,0},{32,48},{48,32},{1,17},{17,1},{33,49},{49,33},{2,18}... | collective-permute-start | bytes 983048 | tf_op jit(solution)/shard_map/ppermute | solution.py:46
  12.0 7.6 %collective-permute-start.5 = (bf16[256,512]{1,0:T(8,128)(2,1)S(1)}, bf16[256,512]{1,0:T(8,128)(2,1)S(1)}, u32[]{:S(2)}, u32[]{:S(2)}) collective-permute-start(bf16[256,512]{1,0:T(8,128)(2,1)S(1)} %get-tuple-element.38.first_ref), channel_id=1, source_target_pairs={{48,112},{0,64},{16,32},{80,96},{112,48},{64,0},{32,16},{96,80},{4... | collective-permute-start | bytes 786440 | tf_op jit(solution)/shard_map/ppermute | solution.py:45
  12.1 9.7 %collective-permute-start.4 = (bf16[256,512]{1,0:T(8,128)(2,1)S(1)}, bf16[256,512]{1,0:T(8,128)(2,1)S(1)}, u32[]{:S(2)}, u32[]{:S(2)}) collective-permute-start(bf16[256,512]{1,0:T(8,128)(2,1)S(1)} %get-tuple-element.38.first_ref), channel_id=1, source_target_pairs={{0,16},{16,0},{32,48},{48,32},{1,17},{17,1},{33,49},{49,33},{2,18}... | collective-permute-start | bytes 786440 | tf_op jit(solution)/shard_map/ppermute | solution.py:46
  42.5 1.3 %collective-permute-start.6 = (f32[40,128]{1,0:T(8,128)S(1)}, f32[40,128]{1,0:T(8,128)S(1)}, u32[]{:S(2)}, u32[]{:S(2)}) collective-permute-start(f32[40,128]{1,0:T(8,128)S(1)} %reduce_sum.9), channel_id=1, source_target_pairs={{0,64},{64,0},{1,65},{65,1},{2,66},{66,2},{3,67},{67,3},{4,68},{68... | collective-permute-start | bytes 61448 | tf_op jit(solution)/shard_map/ppermute | solution.py:18
  43.8 4.7 %collective-permute-start.7 = (f32[40,128]{1,0:T(8,128)S(1)}, f32[40,128]{1,0:T(8,128)S(1)}, u32[]{:S(2)}, u32[]{:S(2)}) collective-permute-start(f32[40,128]{1,0:T(8,128)S(1)} %add.9), channel_id=1, source_target_pairs={{0,4},{4,0},{8,12},{12,8},{1,5},{5,1},{9,13},{13,9},{2,6},{6,2},{1... | collective-permute-start | bytes 61448 | tf_op jit(solution)/shard_map/ppermute | solution.py:29
  48.5 5.9 %collective-permute-start.8 = (f32[40,128]{1,0:T(8,128)S(1)}, f32[40,128]{1,0:T(8,128)S(1)}, u32[]{:S(2)}, u32[]{:S(2)}) collective-permute-start(f32[40,128]{1,0:T(8,128)S(1)} %add.10), channel_id=1, source_target_pairs={{0,12},{4,8},{8,4},{12,0},{1,13},{5,9},{9,5},{13,1},{2,14},{6,10},... | collective-permute-start | bytes 61448 | tf_op jit(solution)/shard_map/ppermute | solution.py:29
  55.1 13.2 %all-to-all-start.1 = ((bf16[32,40,128]{2,1,0:T(8,128)(2,1)}), bf16[32,40,128]{2,1,0:T(8,128)(2,1)S(1)}, u32[]{:S(2)}, u32[]{:S(2)}) async-start(bf16[32,40,128]{2,1,0:T(8,128)(2,1)} %broadcast_in_dim.2), calls=%async_computation.1 | async-start | bytes 655360 | tf_op jit(solution)/shard_map/all_to_all | solution.py:31

commit v8 on v7

--- a/solution.py
+++ b/solution.py
@@ -311,8 +311,8 @@
 
 def main_inner_kernel(
     own_ref,
+    mixed_two_ref,
     mixed_one_ref,
-    mixed_two_ref,
     dealt_ref,
     light_ref,
     out_ref,
@@ -350,8 +350,8 @@
 
 def main_edge_kernel(
     first_ref,
+    first_two_ref,
     first_one_ref,
-    first_two_ref,
     dealt_ref,
     edge_grad_ref,
     light_ref,
@@ -523,8 +523,8 @@
         (whole_pay, lift_half, like((2, 4, chans, breadth), BF16)),
         "main_inner",
         mixed_for_one,
+        mixed_two,
         mixed_one,
-        mixed_two,
         dealt,
         light,
         inner_out,
@@ -537,8 +537,8 @@
         (whole_pay, lift_half),
         "main_edge",
         first,
+        first_two,
         first_one,
-        first_two,
         dealt,
         edge_grad,
         light,

time: 69.5 us -> 69.5 us (level)
  starting transfers between devices: 16.7 us -> 15.1 us
  waiting for transfers between devices: 22.8 us -> 24.3 us
    ppermute x3, waiting for transfers between devices: 4.1 us -> 5.67 us  [with_next_and_before(): one = lax.ppermute(first_send, axis, [(i, i ^ 1) for i in range(count)])]
    ppermute x3, starting transfers between devices: 7.42 us -> 5.95 us  [with_next_and_before(): one = lax.ppermute(first_send, axis, [(i, i ^ 1) for i in range(count)])]
where the time goes in v8:
time: 69.5 us; the launch traced here: 69.3 us
  waiting for transfers between devices  24.3 us (35%)
  blocking collectives  18.5 us (27%)
  starting transfers between devices  15.1 us (22%)
  Pallas kernels  9.79 us (14%)
  local copies, waits for them, and re-layouts  0.76 us (1%)
    all_to_all x1, blocking collectives, sum_everywhere(): lax.all_to_all(pay.reshape(16, rows // 16, 128), plane, split_axis=0, con...  18.5 us
    pallas_call x6, Pallas kernels, local_call(): pl.pallas_call(kernel, out_shape=shapes, scratch_shapes=scratch, in_specs...  9.79 us
    all_to_all x1, waiting for transfers between devices, sum_everywhere(): lax.all_to_all(spread, ('pair',) + plane, split_axis=0, concat_axis=0, ti...  7.95 us
    ppermute x2, waiting for transfers between devices, sum_everywhere(): mine = mine + lax.ppermute(mine, 'quad', [(i, i ^ flip) for i in range(4)])  7.28 us
    ppermute x3, starting transfers between devices, with_next_and_before(): one = lax.ppermute(first_send, axis, [(i, i ^ 1) for i in range(count)])  5.95 us
    ppermute x3, waiting for transfers between devices, with_next_and_before(): one = lax.ppermute(first_send, axis, [(i, i ^ 1) for i in range(count)])  5.67 us
    all_to_all x1, starting transfers between devices, sum_everywhere(): lax.all_to_all(spread, ('pair',) + plane, split_axis=0, concat_axis=0, ti...  3.87 us
    ppermute x2, starting transfers between devices, sum_everywhere(): mine = mine + lax.ppermute(mine, 'quad', [(i, i ^ flip) for i in range(4)])  3.29 us
  transfers between devices with their start and end apart: 10, of which 7 were waited for; matrix products, arithmetic and copies ran while one was open for 0% of the time, Pallas kernels for 6%

profile of v8, /device:TPU:64, one launch (start us, length us, event | category | flops | bytes accessed | tf_op | source)
XLA Modules:
  0.0 69.3 jit_solution(4130532895129741887)
XLA Ops:
  0.6 2.3 %inner.1 = (bf16[320,512]{1,0:T(8,128)(2,1)S(1)}, bf16[320,512]{1,0:T(8,128)(2,1)S(1)}, bf16[2,64,512]{2,1,0:T(8,128)(2,1)S(1)}, f32[2,2,64,512]{3,2,1,0:T(8,128...) custom-call(bf16[2,16,2048]{2,1,0:T(8,128)(2,1)} %bitcast.8, ...), custom_call_target="tpu_custom_call" | custom-call | flops 3000000000 | bytes 9000000 | tf_op jit(solution)/shard_map/inner/pallas_call | solution.py:434
  3.0 1.9 %collective-permute-start.2 = (bf16[2,1,64,512]{3,2,1,0:T(8,128)(2,1)S(1)}, bf16[2,1,64,512]{3,2,1,0:T(8,128)(2,1)S(1)}, u32[]{:S(2)}, u32[]{:S(2)}) collective-permute-start(bf16[2,1,64,512]{3,2,1,0:T(8,128)(2,1)S(1)} %get-tuple-element.35), channel_id=1, source_target_pairs={{15,79},{0,64},{1,2},{3,4},{5,6},{7,8},{9,10},{11,12},{13,14},{65,... | collective-permute-start | bytes 393224 | tf_op jit(solution)/shard_map/ppermute | solution.py:45
  4.9 1.1 %collective-permute-start.3 = (bf16[2,1,64,512]{3,2,1,0:T(8,128)(2,1)S(1)}, bf16[2,1,64,512]{3,2,1,0:T(8,128)(2,1)S(1)}, u32[]{:S(2)}, u32[]{:S(2)}) collective-permute-start(bf16[2,1,64,512]{3,2,1,0:T(8,128)(2,1)S(1)} %get-tuple-element.36), channel_id=1, source_target_pairs={{0,1},{1,0},{2,3},{3,2},{4,5},{5,4},{6,7},{7,6},{8,9},{9,8},{10,11... | collective-permute-start | bytes 393224 | tf_op jit(solution)/shard_map/ppermute | solution.py:46
  6.0 0.0 collective-permute-start
  6.0 3.2 %collective-permute-start.1 = (bf16[320,512]{1,0:T(8,128)(2,1)S(1)}, bf16[320,512]{1,0:T(8,128)(2,1)S(1)}, u32[]{:S(2)}, u32[]{:S(2)}) collective-permute-start(bf16[320,512]{1,0:T(8,128)(2,1)S(1)} %get-tuple-element.26.own_ref), channel_id=1, source_target_pairs={{0,16},{16,0},{32,48},{48,32},{1,17},{17,1},{33,49},{49,33},{2,18}... | collective-permute-start | bytes 983048 | tf_op jit(solution)/shard_map/ppermute | solution.py:46
  9.2 2.2 %collective-permute-done.2.two_ref = bf16[2,1,64,512]{3,2,1,0:T(8,128)(2,1)S(1)} collective-permute-done((bf16[2,1,64,512]{3,2,1,0:T(8,128)(2,1)S(1)}, bf16[2,1,64,512]{3,2,1,0:T(8,128)(2,1)S(1)}, u32[]{:S(2)}, u32[]{:S(2)}) %collective-permute-start.2) | collective-permute-done | bytes 131104 | tf_op jit(solution)/shard_map/ppermute | solution.py:45
  11.4 0.0 collective-permute-done.3.one_ref
  11.4 0.6 edge.1
  12.0 1.7 %collective-permute-start.5 = (bf16[256,512]{1,0:T(8,128)(2,1)S(1)}, bf16[256,512]{1,0:T(8,128)(2,1)S(1)}, u32[]{:S(2)}, u32[]{:S(2)}) collective-permute-start(bf16[256,512]{1,0:T(8,128)(2,1)S(1)} %get-tuple-element.38.first_ref), channel_id=1, source_target_pairs={{0,16},{16,0},{32,48},{48,32},{1,17},{17,1},{33,49},{49,33},{2,18}... | collective-permute-start | bytes 786440 | tf_op jit(solution)/shard_map/ppermute | solution.py:46
  13.6 0.0 collective-permute-start.4
  13.6 0.0 collective-permute-done.mixed_two_ref
  13.6 4.2 %collective-permute-done.1.mixed_one_ref = bf16[320,512]{1,0:T(8,128)(2,1)S(1)} collective-permute-done((bf16[320,512]{1,0:T(8,128)(2,1)S(1)}, bf16[320,512]{1,0:T(8,128)(2,1)S(1)}, u32[]{:S(2)}, u32[]{:S(2)}) %collective-permute-start.1) | collective-permute-done | bytes 327712 | tf_op jit(solution)/shard_map/ppermute | solution.py:46
  17.8 2.5 %main_inner.1 = (f32[640,128]{1,0:T(8,128)S(1)}, bf16[2,64,512]{2,1,0:T(8,128)(2,1)S(1)}, bf16[2,4,64,512]{3,2,1,0:T(8,128)(2,1)S(1)}) custom-call(bf16[320,512]{1,0:T(8,128)(2,1)S(1)} %get-tuple-element.26.own_ref, bf16[320,512]{1,0:T(8,128)(2,1)S(1)} %collective-permute-done.mixed_two_ref, bf16[320,512]{1,0:T(8,128)(2,1)S(1)} %collective-permute-done.1.mixed_one_ref, ...), custom_call_target="tpu_custom_call" | custom-call | flops 3000000000 | bytes 9000000 | tf_op jit(solution)/shard_map/main_inner/pallas_call | solution.py:434
  20.3 1.5 %collective-permute-done.5.first_one_ref = bf16[256,512]{1,0:T(8,128)(2,1)S(1)} collective-permute-done((bf16[256,512]{1,0:T(8,128)(2,1)S(1)}, bf16[256,512]{1,0:T(8,128)(2,1)S(1)}, u32[]{:S(2)}, u32[]{:S(2)}) %collective-permute-start.5) | collective-permute-done | bytes 262176 | tf_op jit(solution)/shard_map/ppermute | solution.py:46
  21.8 0.0 collective-permute-done.4.first_two_ref
  21.8 2.2 %main_edge.1 = (f32[640,128]{1,0:T(8,128)S(1)}, bf16[2,64,512]{2,1,0:T(8,128)(2,1)S(1)}) custom-call(bf16[256,512]{1,0:T(8,128)(2,1)S(1)} %get-tuple-element.38.first_ref, bf16[256,512]{1,0:T(8,128)(2,1)S(1)} %collective-permute-done.4.first_two_ref, bf16[256,512]{1,0:T(8,128)(2,1)S(1)} %collective-permute-done.5.first_one_ref, ...), custom_call_target="tpu_custom_call" | custom-call | flops 3000000000 | bytes 9000000 | tf_op jit(solution)/shard_map/main_edge/pallas_call | solution.py:434
  24.0 18.5 %all_to_all.10 = f32[16,40,128]{2,1,0:T(8,128)S(1)} all-to-all(f32[16,40,128]{2,1,0:T(8,128)S(1)} %bitcast.6), channel_id=1, replica_groups=mesh['pair'=2,'core'=2,'ang'=4,'quad'=4,'x'=4] {'ang','x'}, dimensions={0} | all-to-all | bytes 655360 | tf_op jit(solution)/shard_map/all_to_all | solution.py:24
  42.5 0.1 collective-permute-start.6
  42.6 1.2 %collective-permute-done.6 = f32[40,128]{1,0:T(8,128)S(1)} collective-permute-done((f32[40,128]{1,0:T(8,128)S(1)}, f32[40,128]{1,0:T(8,128)S(1)}, u32[]{:S(2)}, u32[]{:S(2)}) %collective-permute-start.6) | collective-permute-done | bytes 20512 | tf_op jit(solution)/shard_map/ppermute | solution.py:18
  43.8 0.0 collective-permute-start.7
  43.8 4.7 %collective-permute-done.7 = f32[40,128]{1,0:T(8,128)S(1)} collective-permute-done((f32[40,128]{1,0:T(8,128)S(1)}, f32[40,128]{1,0:T(8,128)S(1)}, u32[]{:S(2)}, u32[]{:S(2)}) %collective-permute-start.7) | collective-permute-done | bytes 20512 | tf_op jit(solution)/shard_map/ppermute | solution.py:29
  48.5 3.3 %collective-permute-start.8 = (f32[40,128]{1,0:T(8,128)S(1)}, f32[40,128]{1,0:T(8,128)S(1)}, u32[]{:S(2)}, u32[]{:S(2)}) collective-permute-start(f32[40,128]{1,0:T(8,128)S(1)} %add.10), channel_id=1, source_target_pairs={{0,12},{4,8},{8,4},{12,0},{1,13},{5,9},{9,5},{13,1},{2,14},{6,10},... | collective-permute-start | bytes 61448 | tf_op jit(solution)/shard_map/ppermute | solution.py:29
  51.8 2.6 %collective-permute-done.8 = f32[40,128]{1,0:T(8,128)S(1)} collective-permute-done((f32[40,128]{1,0:T(8,128)S(1)}, f32[40,128]{1,0:T(8,128)S(1)}, u32[]{:S(2)}, u32[]{:S(2)}) %collective-permute-start.8) | collective-permute-done | bytes 20512 | tf_op jit(solution)/shard_map/ppermute | solution.py:29
  54.4 0.8 %broadcast_in_dim.2 = bf16[32,40,128]{2,1,0:T(8,128)(2,1)} broadcast(bf16[40,128]{1,0:T(8,128)(2,1)S(1)} %add_convert_fusion), dimensions={1,2} | broadcast | bytes 337920 | tf_op jit(solution)/shard_map/broadcast_in_dim | solution.py:30
  55.2 3.9 %all-to-all-start.1 = ((bf16[32,40,128]{2,1,0:T(8,128)(2,1)}), bf16[32,40,128]{2,1,0:T(8,128)(2,1)S(1)}, u32[]{:S(2)}, u32[]{:S(2)}) async-start(bf16[32,40,128]{2,1,0:T(8,128)(2,1)} %broadcast_in_dim.2), calls=%async_computation.1 | async-start | bytes 655360 | tf_op jit(solution)/shard_map/all_to_all | solution.py:31
  59.0 1.4 %weave.1 = bf16[2,16,2048]{2,1,0:T(8,128)(2,1)} custom-call(bf16[2,64,512]{2,1,0:T(8,128)(2,1)S(1)} %get-tuple-element.34.inner_ref, bf16[2,64,512]{2,1,0:T(8,128)(2,1)S(1)} %get-tuple-element.42.edge_ref, bf16[512,512]{1,0:T(8,128)(2,1)S(1)} %get-tuple-element.43.deal_ref), custom_call_target="tpu_custom_call" | custom-call | flops 3000000000 | bytes 9000000 | tf_op jit(solution)/shard_map/weave/pallas_call | solution.py:434
  60.4 8.0 %all-to-all-done.1 = bf16[32,40,128]{2,1,0:T(8,128)(2,1)S(1)} async-done(((bf16[32,40,128]{2,1,0:T(8,128)(2,1)}), bf16[32,40,128]{2,1,0:T(8,128)(2,1)S(1)}, u32[]{:S(2)}, u32[]{:S(2)}) %all-to-all-start.1) | async-done | bytes 327712 | tf_op jit(solution)/shard_map/all_to_all | solution.py:31
  68.4 0.9 %unpack.1 = (f32[3,3,64,64]{3,2,1,0:T(8,128)}, f32[3,3,64,64]{3,2,1,0:T(8,128)}, f32[16,64]{1,0:T(8,128)}) custom-call(bf16[2,640,128]{2,1,0:T(8,128)(2,1)S(1)} %bitcast.5), custom_call_target="tpu_custom_call" | custom-call | flops 3000000000 | bytes 9000000 | tf_op jit(solution)/shard_map/unpack/pallas_call | solution.py:434
  (4 shorter events, 0.0 us)
Async XLA Ops:
  3.0 8.4 %collective-permute-start.2 = (bf16[2,1,64,512]{3,2,1,0:T(8,128)(2,1)S(1)}, bf16[2,1,64,512]{3,2,1,0:T(8,128)(2,1)S(1)}, u32[]{:S(2)}, u32[]{:S(2)}) collective-permute-start(bf16[2,1,64,512]{3,2,1,0:T(8,128)(2,1)S(1)} %get-tuple-element.35), channel_id=1, source_target_pairs={{15,79},{0,64},{1,2},{3,4},{5,6},{7,8},{9,10},{11,12},{13,14},{65,... | collective-permute-start | bytes 393224 | tf_op jit(solution)/shard_map/ppermute | solution.py:45
  4.9 6.5 %collective-permute-start.3 = (bf16[2,1,64,512]{3,2,1,0:T(8,128)(2,1)S(1)}, bf16[2,1,64,512]{3,2,1,0:T(8,128)(2,1)S(1)}, u32[]{:S(2)}, u32[]{:S(2)}) collective-permute-start(bf16[2,1,64,512]{3,2,1,0:T(8,128)(2,1)S(1)} %get-tuple-element.36), channel_id=1, source_target_pairs={{0,1},{1,0},{2,3},{3,2},{4,5},{5,4},{6,7},{7,6},{8,9},{9,8},{10,11... | collective-permute-start | bytes 393224 | tf_op jit(solution)/shard_map/ppermute | solution.py:46
  6.0 7.6 %collective-permute-start = (bf16[320,512]{1,0:T(8,128)(2,1)S(1)}, bf16[320,512]{1,0:T(8,128)(2,1)S(1)}, u32[]{:S(2)}, u32[]{:S(2)}) collective-permute-start(bf16[320,512]{1,0:T(8,128)(2,1)S(1)} %get-tuple-element.27), channel_id=1, source_target_pairs={{48,112},{0,64},{16,32},{80,96},{112,48},{64,0},{32,16},{96,80},{4... | collective-permute-start | bytes 983048 | tf_op jit(solution)/shard_map/ppermute | solution.py:45
  6.0 11.8 %collective-permute-start.1 = (bf16[320,512]{1,0:T(8,128)(2,1)S(1)}, bf16[320,512]{1,0:T(8,128)(2,1)S(1)}, u32[]{:S(2)}, u32[]{:S(2)}) collective-permute-start(bf16[320,512]{1,0:T(8,128)(2,1)S(1)} %get-tuple-element.26.own_ref), channel_id=1, source_target_pairs={{0,16},{16,0},{32,48},{48,32},{1,17},{17,1},{33,49},{49,33},{2,18}... | collective-permute-start | bytes 983048 | tf_op jit(solution)/shard_map/ppermute | solution.py:46
  12.0 9.8 %collective-permute-start.5 = (bf16[256,512]{1,0:T(8,128)(2,1)S(1)}, bf16[256,512]{1,0:T(8,128)(2,1)S(1)}, u32[]{:S(2)}, u32[]{:S(2)}) collective-permute-start(bf16[256,512]{1,0:T(8,128)(2,1)S(1)} %get-tuple-element.38.first_ref), channel_id=1, source_target_pairs={{0,16},{16,0},{32,48},{48,32},{1,17},{17,1},{33,49},{49,33},{2,18}... | collective-permute-start | bytes 786440 | tf_op jit(solution)/shard_map/ppermute | solution.py:46
  13.6 8.1 %collective-permute-start.4 = (bf16[256,512]{1,0:T(8,128)(2,1)S(1)}, bf16[256,512]{1,0:T(8,128)(2,1)S(1)}, u32[]{:S(2)}, u32[]{:S(2)}) collective-permute-start(bf16[256,512]{1,0:T(8,128)(2,1)S(1)} %get-tuple-element.38.first_ref), channel_id=1, source_target_pairs={{48,112},{0,64},{16,32},{80,96},{112,48},{64,0},{32,16},{96,80},{4... | collective-permute-start | bytes 786440 | tf_op jit(solution)/shard_map/ppermute | solution.py:45
  42.5 1.3 %collective-permute-start.6 = (f32[40,128]{1,0:T(8,128)S(1)}, f32[40,128]{1,0:T(8,128)S(1)}, u32[]{:S(2)}, u32[]{:S(2)}) collective-permute-start(f32[40,128]{1,0:T(8,128)S(1)} %reduce_sum.9), channel_id=1, source_target_pairs={{0,64},{64,0},{1,65},{65,1},{2,66},{66,2},{3,67},{67,3},{4,68},{68... | collective-permute-start | bytes 61448 | tf_op jit(solution)/shard_map/ppermute | solution.py:18
  43.8 4.7 %collective-permute-start.7 = (f32[40,128]{1,0:T(8,128)S(1)}, f32[40,128]{1,0:T(8,128)S(1)}, u32[]{:S(2)}, u32[]{:S(2)}) collective-permute-start(f32[40,128]{1,0:T(8,128)S(1)} %add.9), channel_id=1, source_target_pairs={{0,4},{4,0},{8,12},{12,8},{1,5},{5,1},{9,13},{13,9},{2,6},{6,2},{1... | collective-permute-start | bytes 61448 | tf_op jit(solution)/shard_map/ppermute | solution.py:29
  48.5 5.9 %collective-permute-start.8 = (f32[40,128]{1,0:T(8,128)S(1)}, f32[40,128]{1,0:T(8,128)S(1)}, u32[]{:S(2)}, u32[]{:S(2)}) collective-permute-start(f32[40,128]{1,0:T(8,128)S(1)} %add.10), channel_id=1, source_target_pairs={{0,12},{4,8},{8,4},{12,0},{1,13},{5,9},{9,5},{13,1},{2,14},{6,10},... | collective-permute-start | bytes 61448 | tf_op jit(solution)/shard_map/ppermute | solution.py:29
  55.2 13.2 %all-to-all-start.1 = ((bf16[32,40,128]{2,1,0:T(8,128)(2,1)}), bf16[32,40,128]{2,1,0:T(8,128)(2,1)S(1)}, u32[]{:S(2)}, u32[]{:S(2)}) async-start(bf16[32,40,128]{2,1,0:T(8,128)(2,1)} %broadcast_in_dim.2), calls=%async_computation.1 | async-start | bytes 655360 | tf_op jit(solution)/shard_map/all_to_all | solution.py:31
